TPU v7x, 32 devices: a whole 2x2x4 slice. The times are simulated.
32 devices in a mesh: dp: 4 (over y, x), expert: 4 (over z), mp: 2 (over core).
Axes of the slice: x: 2, y: 2, z: 4, core: 2. Of those that a mesh axis runs over, the one named last changes fastest.
Arguments:
- tokens: bfloat16 [8192, 768], P(('dp', 'expert', 'mp')), may hold values from -6 to 6
- cotangent: bfloat16 [8192, 768], P(('dp', 'expert', 'mp')), may hold values from -6 to 6
- routes: int32 [8192, 1], P(('dp', 'expert')), may hold values from 0 to 3; in each aligned block of 512 rows (0 to 511, 512 to 1023, ...) at most 256 rows name the same one
- buckets: int32 [512, 512], replicated, may hold values from 0 to 31
- norm_first: float32 [768], replicated, may hold values from 0.5 to 1.5
- query_first: bfloat16 [768, 768], P('expert', 'mp'), may hold values from -0.21875 to 0.21875
- key_first: bfloat16 [768, 768], P('expert', 'mp'), may hold values from -0.21875 to 0.21875
- value_first: bfloat16 [768, 768], P('expert', 'mp'), may hold values from -0.21875 to 0.21875
- output_first: bfloat16 [768, 768], P('mp', 'expert'), may hold values from -1.75 to 1.75
- table_first: float32 [32, 12], replicated, may hold values from -4 to 4
- dense_gain: float32 [768], replicated, may hold values from 0.5 to 1.5
- dense_in: bfloat16 [768, 3072], P('expert', 'mp'), may hold values from -0.21875 to 0.21875
- dense_out: bfloat16 [3072, 768], P('mp', 'expert'), may hold values from -0.109375 to 0.109375
- norm_second: float32 [768], replicated, may hold values from 0.5 to 1.5
- query_second: bfloat16 [768, 768], P('expert', 'mp'), may hold values from -0.21875 to 0.21875
- key_second: bfloat16 [768, 768], P('expert', 'mp'), may hold values from -0.21875 to 0.21875
- value_second: bfloat16 [768, 768], P('expert', 'mp'), may hold values from -0.21875 to 0.21875
- output_second: bfloat16 [768, 768], P('mp', 'expert'), may hold values from -1.75 to 1.75
- table_second: float32 [32, 12], replicated, may hold values from -4 to 4
- expert_gain: float32 [768], replicated, may hold values from 0.5 to 1.5
- router: bfloat16 [768, 4], replicated, may hold values from -0.109375 to 0.109375
- expert_in: bfloat16 [4, 768, 3072], P('expert', None, 'mp'), may hold values from -0.21875 to 0.21875
- expert_out: bfloat16 [4, 3072, 768], P('expert', 'mp'), may hold values from -0.625 to 0.625
Outputs:
- block_output: float32 [8192, 768], P(('dp', 'expert', 'mp'))
- grad_tokens: float32 [8192, 768], P(('dp', 'expert', 'mp'))
- grad_norm_first: float32 [768], replicated
- grad_query_first: float32 [768, 768], P('expert', 'mp')
- grad_key_first: float32 [768, 768], P('expert', 'mp')
- grad_value_first: float32 [768, 768], P('expert', 'mp')
- grad_output_first: float32 [768, 768], P('mp', 'expert')
- grad_table_first: float32 [32, 12], replicated
- grad_dense_gain: float32 [768], replicated
- grad_dense_in: float32 [768, 3072], P('expert', 'mp')
- grad_dense_out: float32 [3072, 768], P('mp', 'expert')
- grad_norm_second: float32 [768], replicated
- grad_query_second: float32 [768, 768], P('expert', 'mp')
- grad_key_second: float32 [768, 768], P('expert', 'mp')
- grad_value_second: float32 [768, 768], P('expert', 'mp')
- grad_output_second: float32 [768, 768], P('mp', 'expert')
- grad_table_second: float32 [32, 12], replicated
- grad_expert_gain: float32 [768], replicated
- grad_router: float32 [768, 4], replicated
- grad_expert_in: float32 [4, 768, 3072], P('expert', None, 'mp')
- grad_expert_out: float32 [4, 3072, 768], P('expert', 'mp')
Inputs may be any that keep to these rules, and one draw needn't show every extreme that they name: `routes`: in each aligned block of 512 rows (one sequence) no expert is named by more than 256 rows, and in every draw some block has an expert named by exactly 256 rows.
All inputs are finite; a program needn't handle non-finite values.
Results may differ from a plain program's by a relative error of at most 0.03.
Values may be sent and summed in bfloat16 or wider, within the bound.
No kernel may reach another device: no remote copies, remote signals or barrier semaphores. Data moves between devices by JAX's collectives and lax.ppermute only.
A program may use at most 192 MiB of HBM per device.

v0:
```python
import functools

import jax
import jax.numpy as jnp
from jax import lax
from jax.experimental import pallas as pl
from jax.experimental.pallas import tpu as pltpu
from jax.sharding import PartitionSpec as P

EPSILON = 1e-06
BF16 = jnp.bfloat16
F32 = jnp.float32


def smooth_act(values):
    inner = 0.7978845608 * (values + 0.044715 * values * values * values)
    return 0.5 * values * (1.0 + jnp.tanh(inner))


def smooth_slope(values):
    inner = 0.7978845608 * (values + 0.044715 * values * values * values)
    tangent = jnp.tanh(inner)
    return 0.5 * (1.0 + tangent) + 0.5 * values * (1.0 - tangent * tangent) * 0.7978845608 * (
        1.0 + 0.134145 * values * values
    )


def row_scale(rows):
    return lax.rsqrt(jnp.mean(rows * rows, axis=-1, keepdims=True) + EPSILON)


def normalize(rows, gain):
    return rows * row_scale(rows) * gain


def dot_nn(a, b):
    return jnp.dot(a, b, preferred_element_type=F32)


def dot_tn(a, b):
    return lax.dot_general(a, b, (((0,), (0,)), ((), ())), preferred_element_type=F32)


def dot_nt(a, b):
    return lax.dot_general(a, b, (((1,), (1,)), ((), ())), preferred_element_type=F32)


def flip(x, axis, bit):
    count = lax.axis_size(axis)
    return lax.ppermute(x, axis, [(i, i ^ (1 << bit)) for i in range(count)])


def shift(x, axis, step):
    count = lax.axis_size(axis)
    return lax.ppermute(x, axis, [(i, (i + step) % count) for i in range(count)])


def kernel_call(body, outs, scalars, arrays, limit=48):
    vmem = pl.BlockSpec(memory_space=pltpu.VMEM)
    return pl.pallas_call(
        body,
        out_shape=[jax.ShapeDtypeStruct(shape, dtype) for shape, dtype in outs],
        in_specs=[pl.BlockSpec(memory_space=pltpu.SMEM)] + [vmem] * len(arrays),
        out_specs=[vmem] * len(outs),
        compiler_params=pltpu.CompilerParams(vmem_limit_bytes=limit << 20),
    )(scalars, *arrays)


def place_scalars():
    return jnp.stack([lax.axis_index("expert"), lax.axis_index("dp") & 3]).astype(jnp.int32)


def plane_spread(held):
    from_x = flip(held, "dp", 0)
    from_y = flip(held, "dp", 1)
    return held, from_x, from_y, flip(from_x[:, 0], "dp", 1), flip(from_y[:, 1], "dp", 0)


def gather_pair(left, right):
    count = lax.axis_size("expert")
    rows = left.shape[0] // 4
    place = (lax.axis_index("dp") & 3) * rows
    piece = jnp.stack([lax.dynamic_slice_in_dim(t, place, rows, 0) for t in (left, right)])
    return plane_spread(jnp.stack([shift(piece, "expert", step) for step in range(1, count)]))


def assemble(left, right, pieces):
    count = lax.axis_size("expert")
    rows, cols = left.shape
    quarter = rows // 4

    def body(where, left_ref, right_ref, own, from_x, from_y, diag_left, diag_right, *outs):
        z, place = where[0], where[1]
        for side, (shard, diag) in enumerate(((left_ref, diag_left), (right_ref, diag_right))):
            outs[side][pl.ds(pl.multiple_of(z * rows, 16), rows), :] = shard[...]
            for step in range(1, count):
                base = lax.rem(z + count - step, count) * rows
                for key, ref in ((0, own), (1, from_x), (2, from_y), (3, diag)):
                    row = pl.multiple_of(base + (place ^ key) * quarter, 16)
                    outs[side][pl.ds(row, quarter), :] = (
                        ref[step - 1] if key == 3 else ref[step - 1, side]
                    )

    full = ((count * rows, cols), left.dtype)
    return kernel_call(body, [full, full], place_scalars(), (left, right) + tuple(pieces))


def add_low(a, b):
    return (a.astype(F32) + b.astype(F32)).astype(BF16)


def reduce_pair(send_a, send_b, keep_a, keep_b):
    blocks, _, rows, cols = send_a.shape
    where = place_scalars()
    got_a, got_b = flip(send_a, "dp", 0), flip(send_b, "dp", 1)

    def second(where, keep_a, keep_b, got_a, got_b, send_a, send_b, next_a, next_b):
        x, y = where[1] & 1, where[1] >> 1
        for k in range(blocks):
            send_a[k] = add_low(keep_a[k, 1 - y], got_a[k, 1 - y])
            next_a[k] = add_low(keep_a[k, y], got_a[k, y])
            send_b[k] = add_low(keep_b[k, 1 - x], got_b[k, 1 - x])
            next_b[k] = add_low(keep_b[k, x], got_b[k, x])

    part = ((blocks, rows, cols), BF16)
    send_a, send_b, keep_a, keep_b = kernel_call(
        second, [part] * 4, where, (keep_a, keep_b, got_a, got_b)
    )
    got_a, got_b = flip(send_a, "dp", 1), flip(send_b, "dp", 0)
    far_bits = range(2, lax.axis_size("dp").bit_length() - 1)
    for bit in far_bits:
        keep_a, keep_b = add_low(keep_a, got_a), add_low(keep_b, got_b)
        got_a, got_b = flip(keep_a, "dp", bit), flip(keep_b, "dp", bit)

    def third(where, keep_a, keep_b, got_a, got_b, own, *sends):
        for step in range(blocks):
            block = lax.rem(where[0] + step, blocks)
            out = own if step == 0 else sends[step - 1]
            out[0] = add_low(keep_a[block], got_a[block])
            out[1] = add_low(keep_b[block], got_b[block])

    own, *sends = kernel_call(
        third, [((2, rows, cols), BF16)] * blocks, where, (keep_a, keep_b, got_a, got_b)
    )
    total = own.astype(F32)
    for step, send in enumerate(sends):
        total = total + shift(send, "expert", step + 1).astype(F32)
    held = total.astype(BF16)[None]
    spread = plane_spread(held)

    def last(where, own, from_x, from_y, diag_a, diag_b, out_a, out_b):
        place = where[1]
        for side, (out, diag) in enumerate(((out_a, diag_a), (out_b, diag_b))):
            for key, ref in ((0, own), (1, from_x), (2, from_y), (3, diag)):
                row = pl.multiple_of((place ^ key) * rows, 8)
                value = ref[0] if key == 3 else ref[0, side]
                out[pl.ds(row, rows), :] = value.astype(F32)

    return kernel_call(last, [((4 * rows, cols), F32)] * 2, where, spread)


def all_sum(x):
    for axis in ("mp", "dp", "expert"):
        for bit in range(lax.axis_size(axis).bit_length() - 1):
            x = x + flip(x, axis, bit)
    return x


def whole(shape):
    return pl.BlockSpec(shape, lambda *_: (0,) * len(shape))


PARAMS = pltpu.CompilerParams(vmem_limit_bytes=56 << 20)


def build_bias(buckets, tables):
    heads = tables.shape[0]
    seq_len = buckets.shape[0]
    padded = jnp.pad(tables, ((0, 0), (0, 128 - tables.shape[1])))

    def body(bucket_ref, table_ref, out_ref):
        head = pl.program_id(0)
        row = jnp.broadcast_to(table_ref[pl.ds(head, 1), :], (seq_len, 128))
        for part in range(seq_len // 128):
            index = bucket_ref[:, part * 128 : (part + 1) * 128]
            out_ref[0, :, part * 128 : (part + 1) * 128] = jnp.take_along_axis(row, index, axis=1)

    return pl.pallas_call(
        body,
        out_shape=jax.ShapeDtypeStruct((heads, seq_len, seq_len), F32),
        grid=(heads,),
        in_specs=[whole((seq_len, seq_len)), whole((heads, 128))],
        out_specs=pl.BlockSpec((1, seq_len, seq_len), lambda h: (h, 0, 0)),
        compiler_params=PARAMS,
    )(buckets, padded)


def lane_masks(head_width):
    lane = lax.broadcasted_iota(jnp.int32, (1, 2 * head_width), 1)
    return [lane < head_width, lane >= head_width]


def masked(value, mask):
    return jnp.where(mask, value, jnp.zeros_like(value))


def stream_sum(base, partials):
    total = base[...].astype(F32)
    if partials:
        total = total + (partials[0][...].astype(F32) + partials[1][...].astype(F32))
    return total


def attention_forward(base, partials, gain, weights, bias):
    seq_len, model = base.shape
    heads = bias.shape[0]
    width = weights[0].shape[1] // 2
    head_width = width // heads
    chunk = 128
    scale = head_width**-0.5
    count = len(partials)

    def body(*refs):
        base_ref, part_refs = refs[0], refs[1 : 1 + count]
        gain_ref, wa_ref, wb_ref, bias_ref = refs[1 + count : 5 + count]
        stream_ref, normed_ref, joint_ref, prob_ref, mixed_ref, partial_ref = refs[5 + count :]
        step = pl.program_id(0)

        @pl.when(step == 0)
        def _():
            rows = stream_sum(base_ref, part_refs)
            stream_ref[...] = rows
            normed = normalize(rows, gain_ref[...]).astype(BF16)
            normed_ref[...] = normed
            left = dot_nn(normed, wa_ref[...]).astype(BF16)
            joint_ref[:, :width] = left[:, :width] * jnp.asarray(scale, BF16)
            joint_ref[:, width : 2 * width] = left[:, width:]
            joint_ref[:, 2 * width :] = dot_nn(normed, wb_ref[:, :width]).astype(BF16)

        masks = lane_masks(head_width)
        rows = pl.ds(pl.multiple_of(step * chunk, chunk), chunk)
        for pair in range(heads // 2):
            cols = slice(pair * 2 * head_width, (pair + 1) * 2 * head_width)
            query = joint_ref[rows, cols]
            key = joint_ref[:, slice(width + cols.start, width + cols.stop)]
            value = joint_ref[:, slice(2 * width + cols.start, 2 * width + cols.stop)]
            mixed = None
            for side in range(2):
                head = 2 * pair + side
                scores = dot_nt(query, masked(key, masks[side])) + bias_ref[head]
                exp_part = jnp.exp(scores - jnp.max(scores, axis=-1, keepdims=True))
                prob = (exp_part / jnp.sum(exp_part, axis=-1, keepdims=True)).astype(BF16)
                prob_ref[head] = prob
                out = dot_nn(prob, masked(value, masks[side]))
                mixed = out if mixed is None else mixed + out
            mixed_ref[:, cols] = mixed.astype(BF16)
        partial_ref[...] = dot_nt(mixed_ref[...], wb_ref[:, width:]).astype(BF16)

    full = (seq_len, model)
    shapes = [
        (full, F32, whole(full)),
        (full, BF16, whole(full)),
        ((seq_len, 3 * width), BF16, whole((seq_len, 3 * width))),
        ((heads, seq_len, seq_len), BF16, pl.BlockSpec((heads, chunk, seq_len), lambda i: (0, i, 0))),
        ((seq_len, width), BF16, pl.BlockSpec((chunk, width), lambda i: (i, 0))),
        (full, BF16, pl.BlockSpec((chunk, model), lambda i: (i, 0))),
    ]
    return pl.pallas_call(
        body,
        out_shape=[jax.ShapeDtypeStruct(shape, dtype) for shape, dtype, _ in shapes],
        grid=(seq_len // chunk,),
        in_specs=[whole(full)] * (1 + count)
        + [whole((1, model)), whole(weights[0].shape), whole(weights[1].shape)]
        + [pl.BlockSpec((heads, chunk, seq_len), lambda i: (0, i, 0))],
        out_specs=[spec for _, _, spec in shapes],
        compiler_params=PARAMS,
    )(base, *partials, gain[None], *weights, bias)


def attention_backward(grad, weights, joint, prob):
    seq_len, model = grad.shape
    heads = prob.shape[0]
    width = weights[0].shape[1] // 2
    head_width = width // heads
    chunk = 128
    steps = seq_len // chunk
    scale = head_width**-0.5

    def body(grad_ref, wa_ref, wb_ref, joint_ref, prob_ref, dj_ref, ds_ref, partial_ref, dk_acc, dv_acc):
        step = pl.program_id(0)

        @pl.when(step == 0)
        def _():
            dk_acc[...] = jnp.zeros_like(dk_acc)
            dv_acc[...] = jnp.zeros_like(dv_acc)

        masks = lane_masks(head_width)
        rows = pl.ds(pl.multiple_of(step * chunk, chunk), chunk)
        grad_mixed = dot_nn(grad_ref[...], wb_ref[:, width:]).astype(BF16)
        for pair in range(heads // 2):
            cols = slice(pair * 2 * head_width, (pair + 1) * 2 * head_width)
            query = joint_ref[rows, cols]
            key = joint_ref[:, slice(width + cols.start, width + cols.stop)]
            value = joint_ref[:, slice(2 * width + cols.start, 2 * width + cols.stop)]
            go = grad_mixed[:, cols]
            dq = None
            dk = None
            dv = None
            for side in range(2):
                head = 2 * pair + side
                low = prob_ref[head]
                wide = low.astype(F32)
                grad_prob = dot_nt(go, masked(value, masks[side]))
                inner = jnp.sum(wide * grad_prob, axis=-1, keepdims=True)
                ds = (wide * (grad_prob - inner)).astype(BF16)
                ds_ref[head] = ds
                one_q = dot_nn(ds, masked(key, masks[side]))
                one_k = dot_tn(ds, masked(query, masks[side]))
                one_v = dot_tn(low, masked(go, masks[side]))
                dq = one_q if dq is None else dq + one_q
                dk = one_k if dk is None else dk + one_k
                dv = one_v if dv is None else dv + one_v
            dj_ref[rows, cols] = (dq * scale).astype(BF16)
            dk_acc[:, cols] += dk
            dv_acc[:, cols] += dv

        @pl.when(step == steps - 1)
        def _():
            dj_ref[:, width : 2 * width] = dk_acc[...].astype(BF16)
            dj_ref[:, 2 * width :] = dv_acc[...].astype(BF16)
            partial_ref[...] = (
                dot_nt(dj_ref[:, : 2 * width], wa_ref[...])
                + dot_nt(dj_ref[:, 2 * width :], wb_ref[:, :width])
            ).astype(BF16)

    full = (seq_len, model)
    rows_of = pl.BlockSpec((heads, chunk, seq_len), lambda i: (0, i, 0))
    return pl.pallas_call(
        body,
        out_shape=[
            jax.ShapeDtypeStruct((seq_len, 3 * width), BF16),
            jax.ShapeDtypeStruct(prob.shape, BF16),
            jax.ShapeDtypeStruct(full, BF16),
        ],
        grid=(steps,),
        in_specs=[
            pl.BlockSpec((chunk, model), lambda i: (i, 0)),
            whole(weights[0].shape),
            whole(weights[1].shape),
            whole(joint.shape),
            rows_of,
        ],
        out_specs=[whole((seq_len, 3 * width)), rows_of, whole(full)],
        scratch_shapes=[pltpu.VMEM((seq_len, width), F32)] * 2,
        compiler_params=PARAMS,
    )(grad, *weights, joint, prob)


def split_first(where, a, b, send_a, send_b, keep_a, keep_b, blocks):
    rows = send_a.shape[2]
    x, y = where[1] & 1, where[1] >> 1
    for k in range(blocks):
        for j in range(2):
            for i in range(2):
                at = (k * 4 + j * 2 + i) * rows
                piece_a, piece_b = a[at : at + rows], b[at : at + rows]

                @pl.when(x == i)
                def _():
                    keep_a[k, j] = piece_a

                @pl.when(x != i)
                def _():
                    send_a[k, j] = piece_a

                @pl.when(y == j)
                def _():
                    keep_b[k, i] = piece_b

                @pl.when(y != j)
                def _():
                    send_b[k, i] = piece_b


def weight_grads(blocks, lefts, rights):
    model = lefts[0][0].shape[1]
    cols = sum(y.shape[1] for _, y in lefts)
    rows = model // blocks // 4
    half = ((blocks, 2, rows, cols), BF16)
    flat = [t for pair in lefts + rights for t in pair]

    def body(where, *refs):
        inputs, outs = refs[: len(flat)], refs[len(flat) :]

        def side(number, pairs):
            return jnp.concatenate(
                [
                    dot_tn(inputs[number + 2 * i][...], inputs[number + 2 * i + 1][...]).astype(BF16)
                    for i in range(len(pairs))
                ],
                axis=1,
            )

        split_first(where, side(0, lefts), side(2 * len(lefts), rights), *outs, blocks)

    return kernel_call(body, [half] * 4, place_scalars(), flat)


def table_grad(ds, buckets, bucket_count):
    heads, seq_len, _ = ds.shape
    group = 8

    def body(ds_ref, bucket_ref, out_ref, acc):
        acc[...] = jnp.zeros_like(acc)

        def one(number, carry):
            rows = pl.ds(pl.multiple_of(number * group, group), group)
            index = bucket_ref[rows, :]
            hot = jnp.concatenate(
                [jnp.where(index == level, 1.0, 0.0) for level in range(bucket_count)], axis=0
            ).astype(BF16)
            left = jnp.concatenate(
                [ds_ref[head, rows, :].astype(F32) for head in range(heads)], axis=0
            ).astype(BF16)
            acc[...] += dot_nt(left, hot)
            return carry

        lax.fori_loop(0, seq_len // group, one, 0, unroll=2)
        shape = acc.shape
        same = (
            lax.broadcasted_iota(jnp.int32, shape, 0) % group
            == lax.broadcasted_iota(jnp.int32, shape, 1) % group
        )
        kept = jnp.where(same, acc[...], 0.0)
        spread = (
            lax.broadcasted_iota(jnp.int32, (shape[1], bucket_count), 0) // group
            == lax.broadcasted_iota(jnp.int32, (shape[1], bucket_count), 1)
        ).astype(F32)
        gather = (
            lax.broadcasted_iota(jnp.int32, (heads, shape[0]), 1) // group
            == lax.broadcasted_iota(jnp.int32, (heads, shape[0]), 0)
        ).astype(F32)
        exact = dict(preferred_element_type=F32, precision=lax.Precision.HIGHEST)
        out_ref[...] = jnp.dot(gather, jnp.dot(kept, spread, **exact), **exact)

    vmem = pl.BlockSpec(memory_space=pltpu.VMEM)
    return pl.pallas_call(
        body,
        out_shape=jax.ShapeDtypeStruct((heads, bucket_count), F32),
        in_specs=[vmem, vmem],
        out_specs=vmem,
        scratch_shapes=[pltpu.VMEM((heads * group, bucket_count * group), F32)],
        compiler_params=PARAMS,
    )(ds, buckets)


def dense_forward(base, partials, gain, w_in, w_out):
    seq_len, model = base.shape
    hidden_width = w_in.shape[1]
    chunk = 512
    steps = hidden_width // chunk

    def body(base_ref, own_ref, got_ref, gain_ref, in_ref, out_ref, stream_ref, normed_ref, hidden_ref, slope_ref, partial_ref, acc):
        step = pl.program_id(0)

        @pl.when(step == 0)
        def _():
            rows = stream_sum(base_ref, (own_ref, got_ref))
            stream_ref[...] = rows
            normed_ref[...] = normalize(rows, gain_ref[...]).astype(BF16)
            acc[...] = jnp.zeros_like(acc)

        pre = dot_nn(normed_ref[...], in_ref[...])
        hidden = smooth_act(pre).astype(BF16)
        hidden_ref[...] = hidden
        slope_ref[...] = smooth_slope(pre).astype(BF16)
        acc[...] += dot_nt(hidden, out_ref[...])

        @pl.when(step == steps - 1)
        def _():
            partial_ref[...] = acc[...].astype(BF16)

    full = (seq_len, model)
    col = pl.BlockSpec((model, chunk), lambda i: (0, i))
    act = pl.BlockSpec((seq_len, chunk), lambda i: (0, i))
    return pl.pallas_call(
        body,
        out_shape=[
            jax.ShapeDtypeStruct(full, F32),
            jax.ShapeDtypeStruct(full, BF16),
            jax.ShapeDtypeStruct((seq_len, hidden_width), BF16),
            jax.ShapeDtypeStruct((seq_len, hidden_width), BF16),
            jax.ShapeDtypeStruct(full, BF16),
        ],
        grid=(steps,),
        in_specs=[whole(full)] * 3 + [whole((1, model)), col, col],
        out_specs=[whole(full), whole(full), act, act, whole(full)],
        scratch_shapes=[pltpu.VMEM(full, F32)],
        compiler_params=PARAMS,
    )(base, *partials, gain[None], w_in, w_out)


def norm_step(grad_ref, rows_ref, gain_ref, own_ref, got_ref):
    upstream = own_ref[...].astype(F32) + got_ref[...].astype(F32)
    rows = rows_ref[...].astype(F32)
    scale = row_scale(rows)
    scaled = upstream * gain_ref[...]
    inner = jnp.mean(scaled * rows, axis=-1, keepdims=True)
    grad_rows = scale * scaled - rows * (scale * scale * scale * inner)
    grad_gain = jnp.sum(upstream * rows * scale, axis=0, keepdims=True)
    return grad_ref[...].astype(F32) + grad_rows, grad_gain


def norm_kernel(grad, rows, gain, partials):
    full = rows.shape

    def body(_, grad_ref, rows_ref, gain_ref, own_ref, got_ref, out_ref, low_ref, gain_out):
        total, gain_out[...] = norm_step(grad_ref, rows_ref, gain_ref, own_ref, got_ref)
        out_ref[...] = total
        low_ref[...] = total.astype(BF16)

    return kernel_call(
        body,
        [(full, F32), (full, BF16), ((1, full[1]), F32)],
        place_scalars(),
        (grad, rows, gain[None]) + tuple(partials),
    )


def dense_backward(grad, rows, gain, partials, w_in, w_out, slope):
    seq_len, model = rows.shape
    hidden_width = w_in.shape[1]
    chunk = 512
    steps = hidden_width // chunk

    def body(grad_ref, rows_ref, gain_ref, own_ref, got_ref, in_ref, out_ref, slope_ref, total_ref, low_ref, dpre_ref, partial_ref, gain_out, acc):
        step = pl.program_id(0)

        @pl.when(step == 0)
        def _():
            total, gain_out[...] = norm_step(grad_ref, rows_ref, gain_ref, own_ref, got_ref)
            total_ref[...] = total
            low_ref[...] = total.astype(BF16)
            acc[...] = jnp.zeros_like(acc)

        dpre = (dot_nn(low_ref[...], out_ref[...]) * slope_ref[...].astype(F32)).astype(BF16)
        dpre_ref[...] = dpre
        acc[...] += dot_nt(dpre, in_ref[...])

        @pl.when(step == steps - 1)
        def _():
            partial_ref[...] = acc[...].astype(BF16)

    full = (seq_len, model)
    col = pl.BlockSpec((model, chunk), lambda i: (0, i))
    act = pl.BlockSpec((seq_len, chunk), lambda i: (0, i))
    return pl.pallas_call(
        body,
        out_shape=[
            jax.ShapeDtypeStruct(full, F32),
            jax.ShapeDtypeStruct(full, BF16),
            jax.ShapeDtypeStruct((seq_len, hidden_width), BF16),
            jax.ShapeDtypeStruct(full, BF16),
            jax.ShapeDtypeStruct((1, model), F32),
        ],
        grid=(steps,),
        in_specs=[whole(full)] * 2 + [whole((1, model))] + [whole(full)] * 2 + [col, col, act],
        out_specs=[whole(full), whole(full), act, whole(full), whole((1, model))],
        scratch_shapes=[pltpu.VMEM(full, F32)],
        compiler_params=PARAMS,
    )(grad, rows, gain[None], *partials, w_in, w_out, slope)


def send_slots(base, partials, gain, spots, blocks):
    seq_len, model = base.shape
    slots = spots[1] // blocks
    full = (seq_len, model)

    def body(_, base_ref, own_ref, got_ref, gain_ref, spot_ref, stream_ref, normed_ref, *outs):
        rows = stream_sum(base_ref, (own_ref, got_ref))
        stream_ref[...] = rows
        normed = normalize(rows, gain_ref[...]).astype(BF16)
        normed_ref[...] = normed
        for block in range(blocks):
            slot = lax.broadcasted_iota(jnp.int32, (slots, seq_len), 0) + block * slots
            hot = jnp.where(slot == spot_ref[...], 1.0, 0.0).astype(BF16)
            outs[block][...] = dot_nn(hot, normed).astype(BF16)

    return kernel_call(
        body,
        [(full, F32), (full, BF16)] + [((slots, model), BF16)] * blocks,
        place_scalars(),
        (base, *partials, gain[None], spots[0]),
    )


def stacked(blocks):
    rows, cols = blocks[0].shape

    def body(_, *refs):
        for number, ref in enumerate(refs[:-1]):
            refs[-1][number * rows : (number + 1) * rows, :] = ref[...]

    return kernel_call(body, [((len(blocks) * rows, cols), blocks[0].dtype)], place_scalars(), blocks)[0]


def route_softmax(rows, router):
    logits = dot_nt(rows, router)
    exp_part = jnp.exp(logits - jnp.max(logits, axis=-1, keepdims=True))
    return exp_part / jnp.sum(exp_part, axis=-1, keepdims=True)


def expert_step(rows, grads, router, w_in, w_out):
    half, model = rows[0].shape
    hidden_width = w_in.shape[1]
    chunk = 256
    steps = hidden_width // chunk
    total = 2 * half

    def body(where, own_ref, other_ref, own_grad, other_grad, router_ref, in_ref, out_ref, hidden_ref, dpre_ref, grad_ref, res_own, res_other, back_own, back_other, res_acc, back_acc, rows_ref):
        step = pl.program_id(0)

        @pl.when(step == 0)
        def _():
            rows_ref[:half, :] = own_ref[...]
            rows_ref[half:, :] = other_ref[...]
            here = lax.broadcasted_iota(jnp.int32, (1, router_ref.shape[0]), 1) == where[0]
            for side, grad in enumerate((own_grad, other_grad)):
                part = slice(side * half, (side + 1) * half)
                prob = route_softmax(rows_ref[part, :], router_ref[...])
                gate = jnp.sum(jnp.where(here, prob, 0.0), axis=-1, keepdims=True)
                grad_ref[part, :] = (gate * grad[...].astype(F32)).astype(BF16)
            res_acc[...] = jnp.zeros_like(res_acc)
            back_acc[...] = jnp.zeros_like(back_acc)

        pre = dot_nn(rows_ref[...], in_ref[...])
        hidden = smooth_act(pre).astype(BF16)
        hidden_ref[...] = hidden
        dpre = (dot_nt(grad_ref[...], out_ref[...]) * smooth_slope(pre)).astype(BF16)
        dpre_ref[...] = dpre
        res_acc[...] += dot_nn(hidden, out_ref[...])
        back_acc[...] += dot_nt(dpre, in_ref[...])

        @pl.when(step == steps - 1)
        def _():
            res_own[...] = res_acc[:half, :]
            res_other[...] = res_acc[half:, :].astype(BF16)
            back_own[...] = back_acc[:half, :]
            back_other[...] = back_acc[half:, :].astype(BF16)

    part = (half, model)
    act = pl.BlockSpec((total, chunk), lambda i: (0, i))
    return pl.pallas_call(
        body,
        out_shape=[
            jax.ShapeDtypeStruct((total, hidden_width), BF16),
            jax.ShapeDtypeStruct((total, hidden_width), BF16),
            jax.ShapeDtypeStruct((total, model), BF16),
            jax.ShapeDtypeStruct(part, F32),
            jax.ShapeDtypeStruct(part, BF16),
            jax.ShapeDtypeStruct(part, F32),
            jax.ShapeDtypeStruct(part, BF16),
        ],
        grid=(steps,),
        in_specs=[pl.BlockSpec(memory_space=pltpu.SMEM)]
        + [whole(part)] * 4
        + [
            whole(router.shape),
            pl.BlockSpec((model, chunk), lambda i: (0, i)),
            pl.BlockSpec((chunk, model), lambda i: (i, 0)),
        ],
        out_specs=[act, act, whole((total, model))] + [whole(part)] * 4,
        scratch_shapes=[pltpu.VMEM((total, model), F32)] * 2 + [pltpu.VMEM((total, model), BF16)],
        compiler_params=PARAMS,
    )(place_scalars(), *rows, *grads, router, w_in, w_out)


def expert_finish(result, back, rows, grads, router, blocks):
    half, model = rows.shape
    slots = half // blocks

    def body(where, res_own, res_got, back_own, back_got, rows_ref, grad_ref, router_ref, *outs):
        here = lax.broadcasted_iota(jnp.int32, (1, router_ref.shape[0]), 1) == where[0]
        prob = route_softmax(rows_ref[...], router_ref[...])
        gate = jnp.sum(jnp.where(here, prob, 0.0), axis=-1, keepdims=True)
        result = res_own[...] + res_got[...].astype(F32)
        grad_gate = jnp.sum(grad_ref[...].astype(F32) * result, axis=-1, keepdims=True)
        dz = (prob * (jnp.where(here, grad_gate, 0.0) - grad_gate * gate)).astype(BF16)
        total = back_own[...] + back_got[...].astype(F32) + dot_nn(dz, router_ref[...])
        for block in range(blocks):
            part = slice(block * slots, (block + 1) * slots)
            outs[block][...] = total[part, :].astype(BF16)
            outs[blocks + block][...] = result[part, :].astype(BF16)
        outs[-1][...] = dot_tn(dz, rows_ref[...])

    return kernel_call(
        body,
        [((slots, model), BF16)] * (2 * blocks) + [(router.shape, F32)],
        place_scalars(),
        (*result, *back, rows, grads, router),
    )


def expert_grads(rows, hidden, dpre, grads):
    half, model = rows[0].shape
    hidden_width = hidden.shape[1]
    chunk = 256

    def body(own_ref, other_ref, hidden_ref, dpre_ref, grad_ref, in_ref, out_ref, rows_ref):
        @pl.when(pl.program_id(0) == 0)
        def _():
            rows_ref[:half, :] = own_ref[...]
            rows_ref[half:, :] = other_ref[...]

        in_ref[...] = dot_tn(rows_ref[...], dpre_ref[...]).astype(BF16)
        out_ref[...] = dot_tn(hidden_ref[...], grad_ref[...]).astype(BF16)

    act = pl.BlockSpec((2 * half, chunk), lambda i: (0, i))
    return pl.pallas_call(
        body,
        out_shape=[
            jax.ShapeDtypeStruct((model, hidden_width), BF16),
            jax.ShapeDtypeStruct((hidden_width, model), BF16),
        ],
        grid=(hidden_width // chunk,),
        in_specs=[whole((half, model))] * 2 + [act, act, whole((2 * half, model))],
        out_specs=[
            pl.BlockSpec((model, chunk), lambda i: (0, i)),
            pl.BlockSpec((chunk, model), lambda i: (i, 0)),
        ],
        scratch_shapes=[pltpu.VMEM((2 * half, model), BF16)],
        compiler_params=PARAMS,
    )(*rows, hidden, dpre, grads)


def receive_slots(grad, rows, gain, spots, halves):
    full = rows.shape
    half = halves[0].shape[0]

    def body(_, grad_ref, rows_ref, gain_ref, spot_ref, own_ref, got_ref, out_ref, low_ref, gain_out):
        slot = lax.broadcasted_iota(jnp.int32, (full[0], half), 1)
        first = jnp.where(slot == spot_ref[...], 1.0, 0.0).astype(BF16)
        second = jnp.where(slot + half == spot_ref[...], 1.0, 0.0).astype(BF16)
        upstream = dot_nn(first, own_ref[...]) + dot_nn(second, got_ref[...])
        value = rows_ref[...]
        scale = row_scale(value)
        scaled = upstream * gain_ref[...]
        inner = jnp.mean(scaled * value, axis=-1, keepdims=True)
        total = grad_ref[...].astype(F32) + (
            scale * scaled - value * (scale * scale * scale * inner)
        )
        gain_out[...] = jnp.sum(upstream * value * scale, axis=0, keepdims=True)
        out_ref[...] = total
        low_ref[...] = total.astype(BF16)

    return kernel_call(
        body,
        [(full, F32), (full, BF16), ((1, full[1]), F32)],
        place_scalars(),
        (grad, rows, gain[None], spots) + tuple(halves),
    )


def on_device(
    tokens,
    cotangent,
    routes,
    buckets,
    norm_first,
    query_first,
    key_first,
    value_first,
    output_first,
    table_first,
    dense_gain,
    dense_in,
    dense_out,
    norm_second,
    query_second,
    key_second,
    value_second,
    output_second,
    table_second,
    expert_gain,
    router,
    expert_in,
    expert_out,
):
    mp_index = lax.axis_index("mp")
    z_index = lax.axis_index("expert")
    z_count = lax.axis_size("expert")
    tok_local, model_width = tokens.shape
    seq_len = buckets.shape[0]
    expert_count = router.shape[1]
    capacity = seq_len // 2
    slots = capacity // lax.axis_size("mp")
    bucket_count = table_first.shape[0]
    head_local = table_first.shape[1] // lax.axis_size("mp")

    width = query_first.shape[1]
    shards = (
        (
            jnp.concatenate([query_first, key_first], axis=1),
            jnp.concatenate([value_first, output_first.T], axis=1),
        ),
        (dense_in, dense_out.T),
        (
            jnp.concatenate([query_second, key_second], axis=1),
            jnp.concatenate([value_second, output_second.T], axis=1),
        ),
    )
    gathered = [gather_pair(*pair) for pair in shards]

    stream_zero = lax.all_gather(tokens, "mp", axis=0, tiled=True)
    grad_four = lax.all_gather(cotangent, "mp", axis=0, tiled=True)

    def local_bias(table):
        return build_bias(
            buckets, lax.dynamic_slice_in_dim(table, mp_index * head_local, head_local, 1).T
        )

    chosen = routes[:, 0]
    experts = jnp.arange(expert_count, dtype=jnp.int32)
    picked = chosen[:, None] == experts[None, :]
    order = jnp.arange(seq_len, dtype=jnp.int32)
    earlier = (order[None, :] < order[:, None]).astype(BF16)
    rank = jnp.sum(
        jnp.where(picked, dot_nn(earlier, picked.astype(BF16)), 0.0), axis=1
    ).astype(jnp.int32)
    distance = (chosen - z_index + z_count) % z_count
    spot = distance * slots + rank % slots
    half = z_count * slots
    in_own_half = rank // slots == mp_index
    send_spots = jnp.where(in_own_half, spot, -1)[None, :]
    back_spots = jnp.where(in_own_half, spot, spot + half)[:, None]

    def dispatch(blocks):
        own = stacked(
            [blocks[0]] + [shift(blocks[step], "expert", step) for step in range(1, z_count)]
        )
        return own, flip(own, "mp", 0)

    def give_back(blocks):
        own = stacked(
            [blocks[0]]
            + [shift(blocks[step], "expert", z_count - step) for step in range(1, z_count)]
        )
        return own, flip(own, "mp", 0)

    def swapped(partial):
        return partial, flip(partial, "mp", 0)

    weights_one = assemble(*shards[0], gathered[0])
    _, normed_one, joint_one, prob_one, mixed_one, partial = attention_forward(
        stream_zero, (), norm_first, weights_one, local_bias(table_first)
    )
    w_in_full, w_out_full = assemble(*shards[1], gathered[1])
    stream_one, normed_ff, hidden, slope, partial = dense_forward(
        stream_zero, swapped(partial), dense_gain, w_in_full, w_out_full
    )

    grad_four, partial = lax.optimization_barrier((grad_four, partial))
    to_slots = (jnp.arange(half, dtype=jnp.int32)[:, None] == send_spots).astype(BF16)
    grad_sent = dot_nn(to_slots, grad_four).astype(BF16)
    grad_slots = dispatch([grad_sent[i * slots : (i + 1) * slots] for i in range(z_count)])

    weights_two = assemble(*shards[2], gathered[2])
    stream_two, normed_two, joint_two, prob_two, mixed_two, partial = attention_forward(
        stream_one, swapped(partial), norm_second, weights_two, local_bias(table_second)
    )

    stream_three, moe_rows, *sent = send_slots(
        stream_two, swapped(partial), expert_gain, (send_spots, half), z_count
    )
    moe_slots = dispatch(sent)
    router_rows = router.T
    expert_hidden, expert_dpre, expert_rows, res_own, res_other, back_own, back_other = expert_step(
        moe_slots, grad_slots, router_rows, expert_in[0], expert_out[0]
    )
    *returns, grad_router = expert_finish(
        (res_own, flip(res_other, "mp", 0)),
        (back_own, flip(back_other, "mp", 0)),
        moe_slots[0],
        grad_slots[0],
        router_rows,
        z_count,
    )
    back_slots = give_back(returns[:z_count])
    grad_expert_in, grad_expert_out = expert_grads(
        moe_slots, expert_hidden, expert_dpre, expert_rows
    )
    expert_in_sum, expert_out_sum = lax.psum((grad_expert_in, grad_expert_out), "dp")

    grad_three, grad_low, grad_expert_gain = receive_slots(
        grad_four, stream_three, expert_gain, back_spots, back_slots
    )

    dj_two, ds_two, partial = attention_backward(grad_low, weights_two, joint_two, prob_two)

    def attention_grads(normed, dj, low, mixed):
        return reduce_pair(
            *weight_grads(
                z_count,
                [(normed, dj[:, : 2 * width])],
                [(normed, dj[:, 2 * width :]), (low, mixed)],
            )
        )

    two = attention_grads(normed_two, dj_two, grad_low, mixed_two)
    grad_two, grad_low, dpre, partial, grad_norm_second = dense_backward(
        grad_three, stream_two, norm_second, swapped(partial), w_in_full, w_out_full, slope
    )
    ff_in, ff_out = reduce_pair(
        *weight_grads(z_count, [(normed_ff, dpre)], [(grad_low, hidden)])
    )
    grad_one, grad_low, grad_dense_gain = norm_kernel(
        grad_two, stream_one, dense_gain, swapped(partial)
    )
    dj_one, ds_one, partial = attention_backward(grad_low, weights_one, joint_one, prob_one)
    one = attention_grads(normed_one, dj_one, grad_low, mixed_one)
    grad_zero, _, grad_norm_first = norm_kernel(
        grad_one, stream_zero, norm_first, swapped(partial)
    )
    first_row = mp_index * tok_local
    grad_zero = lax.dynamic_slice_in_dim(grad_zero, first_row, tok_local, 0)

    result_own, result_got = give_back(returns[z_count:])
    spots_here = lax.dynamic_slice_in_dim(back_spots, first_row, tok_local, 0)
    lanes = jnp.arange(half, dtype=jnp.int32)[None, :]
    result_rows = dot_nn((lanes == spots_here).astype(BF16), result_own) + dot_nn(
        (lanes + half == spots_here).astype(BF16), result_got
    )
    own_rows = lax.dynamic_slice_in_dim(moe_rows, first_row, tok_local, 0)
    own_picked = lax.dynamic_slice_in_dim(picked, first_row, tok_local, 0)
    own_gate = jnp.sum(
        jnp.where(own_picked, route_softmax(own_rows, router_rows), 0.0), axis=-1, keepdims=True
    )
    final_rows = (
        lax.dynamic_slice_in_dim(stream_three, first_row, tok_local, 0) + own_gate * result_rows
    )

    table_one_grad = table_grad(ds_one, buckets, bucket_count)
    table_two_grad = table_grad(ds_two, buckets, bucket_count)

    def full_table(local):
        zero = jnp.zeros((table_first.shape[1], bucket_count), F32)
        return lax.dynamic_update_slice_in_dim(zero, local, mp_index * head_local, 0)

    share = 1.0 / lax.axis_size("mp")
    parts = [
        grad_norm_first[0] * share,
        grad_dense_gain[0] * share,
        grad_norm_second[0] * share,
        grad_expert_gain[0] * share,
        grad_router.reshape(-1),
        full_table(table_one_grad).reshape(-1),
        full_table(table_two_grad).reshape(-1),
    ]
    sizes = [p.shape[0] for p in parts]
    packed = all_sum(jnp.concatenate(parts).reshape(-1, 128)).reshape(-1)
    small, start = [], 0
    for size in sizes:
        small.append(packed[start : start + size])
        start += size
    router_sum = small[4].reshape(expert_count, model_width).T
    table_one_sum = small[5].reshape(table_first.shape[1], bucket_count).T
    table_two_sum = small[6].reshape(table_first.shape[1], bucket_count).T

    return (
        final_rows,
        grad_zero,
        small[0],
        one[0][:, :width],
        one[0][:, width:],
        one[1][:, :width],
        one[1][:, width:].T,
        table_one_sum,
        small[1],
        ff_in,
        ff_out.T,
        small[2],
        two[0][:, :width],
        two[0][:, width:],
        two[1][:, :width],
        two[1][:, width:].T,
        table_two_sum,
        small[3],
        router_sum,
        expert_in_sum.astype(F32)[None],
        expert_out_sum.astype(F32)[None],
    )


def solution(mesh):
    rows = P(("dp", "expert", "mp"), None)
    cols_in, cols_out = P("expert", "mp"), P("mp", "expert")
    attention_in = (P(), cols_in, cols_in, cols_in, cols_out, P())
    dense = (P(), cols_in, cols_out)
    return jax.shard_map(
        on_device,
        mesh=mesh,
        in_specs=(rows, rows, P(("dp", "expert"), None), P())
        + attention_in
        + dense
        + attention_in
        + (P(), P(), P("expert", None, "mp"), P("expert", "mp", None)),
        out_specs=(rows, rows)
        + attention_in
        + dense
        + attention_in
        + (P(), P(), P("expert", None, "mp"), P("expert", "mp", None)),
        check_vma=False,
    )
```

profile of v0, /device:TPU:0, one launch (start us, length us, event | category | flops | bytes accessed | tf_op | source)
XLA Modules:
  0.0 558.0 jit_solution(4270499882315716307)
XLA Ops:
  10.2 5.1 collective-permute-start.2
  22.8 5.7 %collective-permute-done.1 = bf16[2,48,768]{2,1,0:T(8,128)(2,1)S(1)} collective-permute-done((bf16[2,48,768]{2,1,0:T(8,128)(2,1)S(1)}, bf16[2,48,768]{2,1,0:T(8,128)(2,1)S(1)}, u32[]{:S(2)}, u32[]{:S(2)}) %collective-permute-start.1) | collective-permute-done | bytes 147488 | tf_op jit(solution)/shard_map/ppermute | solution.py:55
  28.5 12.3 %collective-permute-start.18 = (bf16[2,48,768]{2,1,0:T(8,128)(2,1)}, bf16[2,48,768]{2,1,0:T(8,128)(2,1)}, u32[]{:S(2)}, u32[]{:S(2)}) collective-permute-start(bf16[2,48,768]{2,1,0:T(8,128)(2,1)} %pad_maximum_fusion.7), channel_id=1, source_target_pairs={{0,6},{2,0},{4,2},{6,4},{1,7},{3,1},{5,3},{7,5},{8,14},{10,8},{12,... | collective-permute-start | bytes 442376 | tf_op jit(solution)/shard_map/ppermute | solution.py:55
  44.3 9.5 %collective-permute-done.9 = bf16[2,48,1536]{2,1,0:T(8,128)(2,1)S(1)} collective-permute-done((bf16[2,48,1536]{2,1,0:T(8,128)(2,1)S(1)}, bf16[2,48,1536]{2,1,0:T(8,128)(2,1)S(1)}, u32[]{:S(2)}, u32[]{:S(2)}) %collective-permute-start.9) | collective-permute-done | bytes 294944 | tf_op jit(solution)/shard_map/ppermute | solution.py:55
  64.9 7.4 %shard_map.383.refs_4_ = f32[6,512,512]{2,1,0:T(8,128)} custom-call(s32[512,512]{1,0:T(8,128)} %bucket_ref.7, f32[6,128]{1,0:T(8,128)} %pad.7.table_ref), custom_call_target="tpu_custom_call" | custom-call | tf_op jit(solution)/shard_map/pallas_call | solution.py:188
  75.1 6.8 %collective-permute-done.6.diag_right = bf16[3,48,768]{2,1,0:T(8,128)(2,1)S(1)} collective-permute-done((bf16[3,48,768]{2,1,0:T(8,128)(2,1)}, bf16[3,48,768]{2,1,0:T(8,128)(2,1)S(1)}, u32[]{:S(2)}, u32[]{:S(2)}) %collective-permute-start.6) | collective-permute-done | bytes 221216 | tf_op jit(solution)/shard_map/ppermute | solution.py:50
  81.9 5.9 %collective-permute-start.17 = (bf16[2,48,768]{2,1,0:T(8,128)(2,1)}, bf16[2,48,768]{2,1,0:T(8,128)(2,1)S(1)}, u32[]{:S(2)}, u32[]{:S(2)}) collective-permute-start(bf16[2,48,768]{2,1,0:T(8,128)(2,1)} %pad_maximum_fusion.7), channel_id=1, source_target_pairs={{0,4},{2,6},{4,0},{6,2},{1,5},{3,7},{5,1},{7,3},{8,12},{10,14},{12... | collective-permute-start | bytes 442376 | tf_op jit(solution)/shard_map/ppermute | solution.py:55
  90.5 12.3 %shard_map.384 = (f32[512,768]{1,0:T(8,128)}, bf16[512,768]{1,0:T(8,128)(2,1)}, bf16[512,1152]{1,0:T(8,128)(2,1)}, bf16[6,512,512]{2,1,0:T(8,128)(2,1)}, bf16[51...) custom-call(bf16[512,768]{1,0:T(8,128)(2,1)} %all_gather.6.refs_0_.base_ref.rows_ref, ...), custom_call_target="tpu_custom_call" | custom-call | tf_op jit(solution)/shard_map/pallas_call | solution.py:268
  116.9 7.4 %shard_map.388.refs_6_ = f32[6,512,512]{2,1,0:T(8,128)} custom-call(s32[512,512]{1,0:T(8,128)} %bucket_ref.7, f32[6,128]{1,0:T(8,128)} %pad.8.table_ref), custom_call_target="tpu_custom_call" | custom-call | tf_op jit(solution)/shard_map/pallas_call | solution.py:188
  129.8 9.7 %shard_map.386 = (f32[512,768]{1,0:T(8,128)}, bf16[512,768]{1,0:T(8,128)(2,1)}, bf16[512,1536]{1,0:T(8,128)(2,1)}, bf16[512,1536]{1,0:T(8,128)(2,1)}, bf16[512,768]{1,0:T(8,128)(2,1)}) custom-call(bf16[512,768]{1,0:T(8,128)(2,1)} %all_gather.6.refs_0_.base_ref.rows_ref, bf16[512,768]{1,0:T(8,128)(2,1)} %get-tuple-element.132.own_ref, ...), custom_call_target="tpu_custom_call" | custom-call | tf_op jit(solution)/shard_map/pallas_call | solution.py:486
  142.1 5.5 collective-permute-done.22.diag_right
  152.5 13.2 %shard_map.389 = (f32[512,768]{1,0:T(8,128)}, bf16[512,768]{1,0:T(8,128)(2,1)}, bf16[512,1152]{1,0:T(8,128)(2,1)}, bf16[6,512,512]{2,1,0:T(8,128)(2,1)}, bf16[51...) custom-call(f32[512,768]{1,0:T(8,128)} %get-tuple-element.135.refs_0_.rows_ref, bf16[512,768]{1,0:T(8,128)(2,1)} %get-tuple-element.137.refs_1_, ...), custom_call_target="tpu_custom_call" | custom-call | tf_op jit(solution)/shard_map/pallas_call | solution.py:268
  180.1 15.8 %collective-permute-done.29.refs_2_ = bf16[128,768]{1,0:T(8,128)(2,1)S(1)} collective-permute-done((bf16[128,768]{1,0:T(8,128)(2,1)S(1)}, bf16[128,768]{1,0:T(8,128)(2,1)S(1)}, u32[]{:S(2)}, u32[]{:S(2)}) %collective-permute-start.29) | collective-permute-done | bytes 196640 | tf_op jit(solution)/shard_map/ppermute | solution.py:55
  204.1 21.7 %shard_map.393 = (bf16[1024,1536]{1,0:T(8,128)(2,1)}, bf16[1024,1536]{1,0:T(8,128)(2,1)}, bf16[1024,768]{1,0:T(8,128)(2,1)}, f32[512,768]{1,0:T(8,128)}, bf16[51...) custom-call(s32[2]{0:T(128)} %copy-done.32, bf16[512,768]{1,0:T(8,128)(2,1)} %copy-done, ...), custom_call_target="tpu_custom_call" | custom-call | tf_op jit(solution)/shard_map/pallas_call | solution.py:653
  234.9 8.0 %collective-permute-start.38 = (bf16[128,768]{1,0:T(8,128)(2,1)S(1)}, bf16[128,768]{1,0:T(8,128)(2,1)S(1)}, u32[]{:S(2)}, u32[]{:S(2)}) collective-permute-start(bf16[128,768]{1,0:T(8,128)(2,1)S(1)} %get-tuple-element.158), channel_id=1, source_target_pairs={{0,6},{2,0},{4,2},{6,4},{1,7},{3,1},{5,3},{7,5},{8,14},{10,8},{12,... | collective-permute-start | bytes 589832 | tf_op jit(solution)/shard_map/ppermute | solution.py:55
  243.5 4.7 collective-permute-done.38.refs_1_
  248.3 10.8 %collective-permute-done.39.refs_2_ = bf16[128,768]{1,0:T(8,128)(2,1)S(1)} collective-permute-done((bf16[128,768]{1,0:T(8,128)(2,1)S(1)}, bf16[128,768]{1,0:T(8,128)(2,1)S(1)}, u32[]{:S(2)}, u32[]{:S(2)}) %collective-permute-start.39) | collective-permute-done | bytes 196640 | tf_op jit(solution)/shard_map/ppermute | solution.py:55
  267.0 13.5 %shard_map.398 = (bf16[512,1152]{1,0:T(8,128)(2,1)}, bf16[6,512,512]{2,1,0:T(8,128)(2,1)}, bf16[512,768]{1,0:T(8,128)(2,1)}) custom-call(bf16[512,768]{1,0:T(8,128)(2,1)} %copy-done.13, bf16[768,768]{1,0:T(8,128)(2,1)} %copy-done.5, bf16[768,768]{1,0:T(8,128)(2,1)} %copy-done.6, bf16[512,1152]{1,0:T(8,128)(2,1)} %get-tuple-element.163.joint_ref, ...), custom_call_target="tpu_custom_call" | custom-call | tf_op jit(solution)/shard_map/pallas_call | solution.py:338
  287.9 14.4 %collective-permute-done.35.refs_2_ = bf16[128,768]{1,0:T(8,128)(2,1)S(1)} collective-permute-done((bf16[128,768]{1,0:T(8,128)(2,1)S(1)}, bf16[128,768]{1,0:T(8,128)(2,1)S(1)}, u32[]{:S(2)}, u32[]{:S(2)}) %collective-permute-start.35) | collective-permute-done | bytes 196640 | tf_op jit(solution)/shard_map/ppermute | solution.py:55
  309.8 10.1 %shard_map.399 = (f32[512,768]{1,0:T(8,128)}, bf16[512,768]{1,0:T(8,128)(2,1)}, bf16[512,1536]{1,0:T(8,128)(2,1)}, bf16[512,768]{1,0:T(8,128)(2,1)}, f32[1,768]{1,0:T(1,128)}) custom-call(f32[512,768]{1,0:T(8,128)} %copy-done.18, f32[512,768]{1,0:T(8,128)} %get-tuple-element.140.base_ref.rows_ref, f32[1,768]{1,0:T(1,128)} %broadcast_in_dim.59.refs_3_.gain_ref, ...), custom_call_target="tpu_custom_call" | custom-call | tf_op jit(solution)/shard_map/pallas_call | solution.py:557
  328.9 10.6 %shard_map.417 = (bf16[768,1536]{1,0:T(8,128)(2,1)}, bf16[1536,768]{1,0:T(8,128)(2,1)}) custom-call(bf16[512,768]{1,0:T(8,128)(2,1)} %copy-done, bf16[512,768]{1,0:T(8,128)(2,1)} %copy-done.42, bf16[1024,1536]{1,0:T(8,128)(2,1)} %get-tuple-element.234.hidden_ref, bf16[1024,1536]{1,0:T(8,128)(2,1)} %get-tuple-element.235.dpre_ref, ...), custom_call_target="tpu_custom_call" | custom-call | tf_op jit(solution)/shard_map/pallas_call | solution.py:719
  346.2 13.4 %shard_map.401 = (bf16[512,1152]{1,0:T(8,128)(2,1)}, bf16[6,512,512]{2,1,0:T(8,128)(2,1)}, bf16[512,768]{1,0:T(8,128)(2,1)}) custom-call(bf16[512,768]{1,0:T(8,128)(2,1)} %copy-done.11, bf16[768,768]{1,0:T(8,128)(2,1)} %copy-done.7, bf16[768,768]{1,0:T(8,128)(2,1)} %copy-done.8, bf16[512,1152]{1,0:T(8,128)(2,1)} %get-tuple-element.171.joint_ref, ...), custom_call_target="tpu_custom_call" | custom-call | tf_op jit(solution)/shard_map/pallas_call | solution.py:338
  367.5 12.2 %shard_map.404 = f32[6,32]{1,0:T(8,128)} custom-call(bf16[6,512,512]{2,1,0:T(8,128)(2,1)} %get-tuple-element.181.ds_ref, s32[512,512]{1,0:T(8,128)} %bucket_ref.7), custom_call_target="tpu_custom_call" | custom-call | tf_op jit(solution)/shard_map/pallas_call | solution.py:447
  381.1 7.0 %shard_map.409 = (bf16[4,2,48,1536]{3,2,1,0:T(8,128)(2,1)}, bf16[4,2,48,1536]{3,2,1,0:T(8,128)(2,1)}, bf16[4,2,48,1536]{3,2,1,0:T(8,128)(2,1)S(1)}, bf16[4,2,48,1536]{3,2,1,0:T(8,128)(2,1)}) custom-call(s32[2]{0:T(128)S(1)} %copy-done.33, bf16[512,768]{1,0:T(8,128)(2,1)S(1)} %copy-done.25, bf16[512,1536]{1,0:T(8,128)(2,1)} %get-tuple-element.200.refs_1_, ...), custom_call_target="tpu_custom_call" | custom-call | tf_op jit(solution)/shard_map/pallas_call | solution.py:60
  392.0 12.2 %shard_map.403 = f32[6,32]{1,0:T(8,128)} custom-call(bf16[6,512,512]{2,1,0:T(8,128)(2,1)} %get-tuple-element.180.ds_ref, s32[512,512]{1,0:T(8,128)} %bucket_ref.7), custom_call_target="tpu_custom_call" | custom-call | tf_op jit(solution)/shard_map/pallas_call | solution.py:447
  417.9 16.3 %collective-permute-done.80.from_y = bf16[1,2,48,768]{3,2,1,0:T(8,128)(2,1)} collective-permute-done((bf16[1,2,48,768]{3,2,1,0:T(8,128)(2,1)}, bf16[1,2,48,768]{3,2,1,0:T(8,128)(2,1)}, u32[]{:S(2)}, u32[]{:S(2)}) %collective-permute-start.80) | collective-permute-done | bytes 147488 | tf_op jit(solution)/shard_map/ppermute | solution.py:50
  437.0 13.3 %collective-permute-done.79.from_x = bf16[1,2,48,768]{3,2,1,0:T(8,128)(2,1)S(1)} collective-permute-done((bf16[1,2,48,768]{3,2,1,0:T(8,128)(2,1)}, bf16[1,2,48,768]{3,2,1,0:T(8,128)(2,1)S(1)}, u32[]{:S(2)}, u32[]{:S(2)}) %collective-permute-start.79) | collective-permute-done | bytes 147488 | tf_op jit(solution)/shard_map/ppermute | solution.py:50
  462.8 9.3 %collective-permute-done.47 = f32[54,128]{1,0:T(8,128)S(1)} collective-permute-done((f32[54,128]{1,0:T(8,128)S(1)}, f32[54,128]{1,0:T(8,128)S(1)}, u32[]{:S(2)}, u32[]{:S(2)}) %collective-permute-start.47) | collective-permute-done | bytes 27680 | tf_op jit(solution)/shard_map/ppermute | solution.py:50
  497.4 6.8 %collective-permute-done.64.got_b = bf16[4,48,1536]{2,1,0:T(8,128)(2,1)S(1)} collective-permute-done((bf16[4,48,1536]{2,1,0:T(8,128)(2,1)S(1)}, bf16[4,48,1536]{2,1,0:T(8,128)(2,1)S(1)}, u32[]{:S(2)}, u32[]{:S(2)}) %collective-permute-start.64) | collective-permute-done | bytes 589856 | tf_op jit(solution)/shard_map/ppermute | solution.py:50
  516.9 9.6 %collective-permute-done.66 = bf16[2,48,1536]{2,1,0:T(8,128)(2,1)S(1)} collective-permute-done((bf16[2,48,1536]{2,1,0:T(8,128)(2,1)S(1)}, bf16[2,48,1536]{2,1,0:T(8,128)(2,1)S(1)}, u32[]{:S(2)}, u32[]{:S(2)}) %collective-permute-start.66) | collective-permute-done | bytes 294944 | tf_op jit(solution)/shard_map/ppermute | solution.py:55
  534.3 5.5 collective-permute-done.68.from_x
  541.5 4.6 broadcast_in_dim.67
  (445 shorter events, 221.6 us)
Async XLA Ops:
  7.2 534.2 %all-reduce.5.cloned.1.call-start = ((), (), s32[]{:S(2)}) async-start(), calls=%async_computation | async-start | bytes 9437184 | tf_op jit(solution)/shard_map/psum | solution.py:892
  15.3 25.5 %collective-permute-start = (bf16[2,48,768]{2,1,0:T(8,128)(2,1)S(1)}, bf16[2,48,768]{2,1,0:T(8,128)(2,1)S(1)}, u32[]{:S(2)}, u32[]{:S(2)}) collective-permute-start(bf16[2,48,768]{2,1,0:T(8,128)(2,1)S(1)} %pad_maximum_fusion.6), channel_id=1, source_target_pairs={{0,2},{2,4},{4,6},{6,0},{1,3},{3,5},{5,7},{7,1},{8,10},{10,12},{12... | collective-permute-start | bytes 442376 | tf_op jit(solution)/shard_map/ppermute | solution.py:55
  17.3 25.4 %collective-permute-start.10 = (bf16[2,48,1536]{2,1,0:T(8,128)(2,1)S(1)}, bf16[2,48,1536]{2,1,0:T(8,128)(2,1)S(1)}, u32[]{:S(2)}, u32[]{:S(2)}) collective-permute-start(bf16[2,48,1536]{2,1,0:T(8,128)(2,1)S(1)} %pad_maximum_fusion.5), channel_id=1, source_target_pairs={{0,6},{2,0},{4,2},{6,4},{1,7},{3,1},{5,3},{7,5},{8,14},{10,8},{12,... | collective-permute-start | bytes 884744 | tf_op jit(solution)/shard_map/ppermute | solution.py:55
  20.2 33.6 %collective-permute-start.9 = (bf16[2,48,1536]{2,1,0:T(8,128)(2,1)S(1)}, bf16[2,48,1536]{2,1,0:T(8,128)(2,1)S(1)}, u32[]{:S(2)}, u32[]{:S(2)}) collective-permute-start(bf16[2,48,1536]{2,1,0:T(8,128)(2,1)S(1)} %pad_maximum_fusion.5), channel_id=1, source_target_pairs={{0,4},{2,6},{4,0},{6,2},{1,5},{3,7},{5,1},{7,3},{8,12},{10,14},{12... | collective-permute-start | bytes 884744 | tf_op jit(solution)/shard_map/ppermute | solution.py:55
  22.1 31.8 %collective-permute-start.8 = (bf16[2,48,1536]{2,1,0:T(8,128)(2,1)S(1)}, bf16[2,48,1536]{2,1,0:T(8,128)(2,1)}, u32[]{:S(2)}, u32[]{:S(2)}) collective-permute-start(bf16[2,48,1536]{2,1,0:T(8,128)(2,1)S(1)} %pad_maximum_fusion.5), channel_id=1, source_target_pairs={{0,2},{2,4},{4,6},{6,0},{1,3},{3,5},{5,7},{7,1},{8,10},{10,12},{12... | collective-permute-start | bytes 884744 | tf_op jit(solution)/shard_map/ppermute | solution.py:55
  28.5 79.6 %collective-permute-start.18 = (bf16[2,48,768]{2,1,0:T(8,128)(2,1)}, bf16[2,48,768]{2,1,0:T(8,128)(2,1)}, u32[]{:S(2)}, u32[]{:S(2)}) collective-permute-start(bf16[2,48,768]{2,1,0:T(8,128)(2,1)} %pad_maximum_fusion.7), channel_id=1, source_target_pairs={{0,6},{2,0},{4,2},{6,4},{1,7},{3,1},{5,3},{7,5},{8,14},{10,8},{12,... | collective-permute-start | bytes 442376 | tf_op jit(solution)/shard_map/ppermute | solution.py:55
  54.9 47.9 %collective-permute-start.12 = (bf16[3,2,48,1536]{3,2,0,1:T(8,128)(2,1)S(1)}, bf16[3,2,48,1536]{3,2,0,1:T(8,128)(2,1)}, u32[]{:S(2)}, u32[]{:S(2)}) collective-permute-start(bf16[3,2,48,1536]{3,2,0,1:T(8,128)(2,1)S(1)} %pad_maximum_fusion), channel_id=1, source_target_pairs={{0,16},{8,24},{16,0},{24,8},{1,17},{9,25},{17,1},{25,9},{2,18},{10... | collective-permute-start | bytes 2654216 | tf_op jit(solution)/shard_map/ppermute | solution.py:50
  57.2 47.6 %collective-permute-start.11 = (bf16[3,2,48,1536]{3,2,0,1:T(8,128)(2,1)S(1)}, bf16[3,2,48,1536]{3,2,0,1:T(8,128)(2,1)}, u32[]{:S(2)}, u32[]{:S(2)}) collective-permute-start(bf16[3,2,48,1536]{3,2,0,1:T(8,128)(2,1)S(1)} %pad_maximum_fusion), channel_id=1, source_target_pairs={{0,8},{8,0},{16,24},{24,16},{1,9},{9,1},{17,25},{25,17},{2,10},{10... | collective-permute-start | bytes 2654216 | tf_op jit(solution)/shard_map/ppermute | solution.py:50
  61.4 26.3 %collective-permute-start.5 = (bf16[3,48,768]{2,1,0:T(8,128)(2,1)}, bf16[3,48,768]{2,1,0:T(8,128)(2,1)S(1)}, u32[]{:S(2)}, u32[]{:S(2)}) collective-permute-start(bf16[3,48,768]{2,1,0:T(8,128)(2,1)} %slice_bitcast_fusion.7), channel_id=1, source_target_pairs={{0,16},{8,24},{16,0},{24,8},{1,17},{9,25},{17,1},{25,9},{2,18},{10... | collective-permute-start | bytes 663560 | tf_op jit(solution)/shard_map/ppermute | solution.py:50
  81.9 26.8 %collective-permute-start.17 = (bf16[2,48,768]{2,1,0:T(8,128)(2,1)}, bf16[2,48,768]{2,1,0:T(8,128)(2,1)S(1)}, u32[]{:S(2)}, u32[]{:S(2)}) collective-permute-start(bf16[2,48,768]{2,1,0:T(8,128)(2,1)} %pad_maximum_fusion.7), channel_id=1, source_target_pairs={{0,4},{2,6},{4,0},{6,2},{1,5},{3,7},{5,1},{7,3},{8,12},{10,14},{12... | collective-permute-start | bytes 442376 | tf_op jit(solution)/shard_map/ppermute | solution.py:55
  102.8 27.0 %collective-permute-start.7 = (bf16[512,768]{1,0:T(8,128)(2,1)}, bf16[512,768]{1,0:T(8,128)(2,1)}, u32[]{:S(2)}, u32[]{:S(2)}) collective-permute-start(bf16[512,768]{1,0:T(8,128)(2,1)} %get-tuple-element.132.own_ref), channel_id=1, source_target_pairs={{0,1},{1,0},{2,3},{3,2},{4,5},{5,4},{6,7},{7,6},{8,9},{9,8},{10,11... | collective-permute-start | bytes 2359304 | tf_op jit(solution)/shard_map/ppermute | solution.py:50
  104.8 22.0 %collective-permute-start.14 = (bf16[3,48,1536]{2,1,0:T(8,128)(2,1)}, bf16[3,48,1536]{2,1,0:T(8,128)(2,1)S(1)}, u32[]{:S(2)}, u32[]{:S(2)}) collective-permute-start(bf16[3,48,1536]{2,1,0:T(8,128)(2,1)} %slice_bitcast_fusion), channel_id=1, source_target_pairs={{0,8},{8,0},{16,24},{24,16},{1,9},{9,1},{17,25},{25,17},{2,10},{10... | collective-permute-start | bytes 1327112 | tf_op jit(solution)/shard_map/ppermute | solution.py:50
  109.6 30.1 %collective-permute-start.20 = (bf16[3,2,48,768]{3,2,0,1:T(8,128)(2,1)S(1)}, bf16[3,2,48,768]{3,2,0,1:T(8,128)(2,1)S(1)}, u32[]{:S(2)}, u32[]{:S(2)}) collective-permute-start(bf16[3,2,48,768]{3,2,0,1:T(8,128)(2,1)S(1)} %pad_maximum_fusion.2), channel_id=1, source_target_pairs={{0,16},{8,24},{16,0},{24,8},{1,17},{9,25},{17,1},{25,9},{2,18},{10... | collective-permute-start | bytes 1327112 | tf_op jit(solution)/shard_map/ppermute | solution.py:50
  111.7 29.7 %collective-permute-start.19 = (bf16[3,2,48,768]{3,2,0,1:T(8,128)(2,1)S(1)}, bf16[3,2,48,768]{3,2,0,1:T(8,128)(2,1)S(1)}, u32[]{:S(2)}, u32[]{:S(2)}) collective-permute-start(bf16[3,2,48,768]{3,2,0,1:T(8,128)(2,1)S(1)} %pad_maximum_fusion.2), channel_id=1, source_target_pairs={{0,8},{8,0},{16,24},{24,16},{1,9},{9,1},{17,25},{25,17},{2,10},{10... | collective-permute-start | bytes 1327112 | tf_op jit(solution)/shard_map/ppermute | solution.py:50
  170.4 25.6 %collective-permute-start.29 = (bf16[128,768]{1,0:T(8,128)(2,1)S(1)}, bf16[128,768]{1,0:T(8,128)(2,1)S(1)}, u32[]{:S(2)}, u32[]{:S(2)}) collective-permute-start(bf16[128,768]{1,0:T(8,128)(2,1)S(1)} %get-tuple-element.245), channel_id=1, source_target_pairs={{0,4},{2,6},{4,0},{6,2},{1,5},{3,7},{5,1},{7,3},{8,12},{10,14},{12... | collective-permute-start | bytes 589832 | tf_op jit(solution)/shard_map/ppermute | solution.py:55
  170.5 25.5 %collective-permute-start.28 = (bf16[128,768]{1,0:T(8,128)(2,1)S(1)}, bf16[128,768]{1,0:T(8,128)(2,1)S(1)}, u32[]{:S(2)}, u32[]{:S(2)}) collective-permute-start(bf16[128,768]{1,0:T(8,128)(2,1)S(1)} %get-tuple-element.246), channel_id=1, source_target_pairs={{0,2},{2,4},{4,6},{6,0},{1,3},{3,5},{5,7},{7,1},{8,10},{10,12},{12... | collective-permute-start | bytes 589832 | tf_op jit(solution)/shard_map/ppermute | solution.py:55
  174.3 22.3 %collective-permute-start.24 = (bf16[128,768]{1,0:T(8,128)(2,1)S(1)}, bf16[128,768]{1,0:T(8,128)(2,1)S(1)}, u32[]{:S(2)}, u32[]{:S(2)}) collective-permute-start(bf16[128,768]{1,0:T(8,128)(2,1)S(1)} %get-tuple-element.145), channel_id=1, source_target_pairs={{0,2},{2,4},{4,6},{6,0},{1,3},{3,5},{5,7},{7,1},{8,10},{10,12},{12... | collective-permute-start | bytes 589832 | tf_op jit(solution)/shard_map/ppermute | solution.py:55
  177.2 22.9 %collective-permute-start.25 = (bf16[128,768]{1,0:T(8,128)(2,1)S(1)}, bf16[128,768]{1,0:T(8,128)(2,1)S(1)}, u32[]{:S(2)}, u32[]{:S(2)}) collective-permute-start(bf16[128,768]{1,0:T(8,128)(2,1)S(1)} %get-tuple-element.146), channel_id=1, source_target_pairs={{0,4},{2,6},{4,0},{6,2},{1,5},{3,7},{5,1},{7,3},{8,12},{10,14},{12... | collective-permute-start | bytes 589832 | tf_op jit(solution)/shard_map/ppermute | solution.py:55
  178.2 22.0 %collective-permute-start.26 = (bf16[128,768]{1,0:T(8,128)(2,1)S(1)}, bf16[128,768]{1,0:T(8,128)(2,1)S(1)}, u32[]{:S(2)}, u32[]{:S(2)}) collective-permute-start(bf16[128,768]{1,0:T(8,128)(2,1)S(1)} %get-tuple-element.147), channel_id=1, source_target_pairs={{0,6},{2,0},{4,2},{6,4},{1,7},{3,1},{5,3},{7,5},{8,14},{10,8},{12,... | collective-permute-start | bytes 589832 | tf_op jit(solution)/shard_map/ppermute | solution.py:55
  280.5 28.4 %collective-permute-start.42 = (bf16[512,768]{1,0:T(8,128)(2,1)}, bf16[512,768]{1,0:T(8,128)(2,1)S(1)}, u32[]{:S(2)}, u32[]{:S(2)}) collective-permute-start(bf16[512,768]{1,0:T(8,128)(2,1)} %get-tuple-element.165.own_ref), channel_id=1, source_target_pairs={{0,1},{1,0},{2,3},{3,2},{4,5},{5,4},{6,7},{7,6},{8,9},{9,8},{10,11... | collective-permute-start | bytes 2359304 | tf_op jit(solution)/shard_map/ppermute | solution.py:50
  302.9 56.9 %collective-permute-start.37 = (bf16[512,768]{1,0:T(8,128)(2,1)S(1)}, bf16[512,768]{1,0:T(8,128)(2,1)}, u32[]{:S(2)}, u32[]{:S(2)}) collective-permute-start(bf16[512,768]{1,0:T(8,128)(2,1)S(1)} %shard_map.395), channel_id=1, source_target_pairs={{0,1},{1,0},{2,3},{3,2},{4,5},{5,4},{6,7},{7,6},{8,9},{9,8},{10,11... | collective-permute-start | bytes 2359304 | tf_op jit(solution)/shard_map/ppermute | solution.py:50
  326.3 35.9 %collective-permute-start.74 = (bf16[4,48,768]{2,1,0:T(8,128)(2,1)}, bf16[4,48,768]{2,1,0:T(8,128)(2,1)S(1)}, u32[]{:S(2)}, u32[]{:S(2)}) collective-permute-start(bf16[4,48,768]{2,1,0:T(8,128)(2,1)} %get-tuple-element.226), channel_id=1, source_target_pairs={{0,16},{8,24},{16,0},{24,8},{1,17},{9,25},{17,1},{25,9},{2,18},{10... | collective-permute-start | bytes 884744 | tf_op jit(solution)/shard_map/ppermute | solution.py:50
  326.8 35.4 %collective-permute-start.75 = (bf16[4,48,768]{2,1,0:T(8,128)(2,1)}, bf16[4,48,768]{2,1,0:T(8,128)(2,1)}, u32[]{:S(2)}, u32[]{:S(2)}) collective-permute-start(bf16[4,48,768]{2,1,0:T(8,128)(2,1)} %get-tuple-element.227), channel_id=1, source_target_pairs={{0,8},{8,0},{16,24},{24,16},{1,9},{9,1},{17,25},{25,17},{2,10},{10... | collective-permute-start | bytes 884744 | tf_op jit(solution)/shard_map/ppermute | solution.py:50
  359.6 53.2 %collective-permute-start.44 = (bf16[512,768]{1,0:T(8,128)(2,1)}, bf16[512,768]{1,0:T(8,128)(2,1)}, u32[]{:S(2)}, u32[]{:S(2)}) collective-permute-start(bf16[512,768]{1,0:T(8,128)(2,1)} %get-tuple-element.173.own_ref), channel_id=1, source_target_pairs={{0,1},{1,0},{2,3},{3,2},{4,5},{5,4},{6,7},{7,6},{8,9},{9,8},{10,11... | collective-permute-start | bytes 2359304 | tf_op jit(solution)/shard_map/ppermute | solution.py:50
  363.4 25.8 %collective-permute-start.76 = (bf16[2,48,768]{2,1,0:T(8,128)(2,1)S(1)}, bf16[2,48,768]{2,1,0:T(8,128)(2,1)S(1)}, u32[]{:S(2)}, u32[]{:S(2)}) collective-permute-start(bf16[2,48,768]{2,1,0:T(8,128)(2,1)S(1)} %get-tuple-element.229), channel_id=1, source_target_pairs={{0,2},{2,4},{4,6},{6,0},{1,3},{3,5},{5,7},{7,1},{8,10},{10,12},{12... | collective-permute-start | bytes 442376 | tf_op jit(solution)/shard_map/ppermute | solution.py:55
  363.4 27.0 %collective-permute-start.77 = (bf16[2,48,768]{2,1,0:T(8,128)(2,1)S(1)}, bf16[2,48,768]{2,1,0:T(8,128)(2,1)S(1)}, u32[]{:S(2)}, u32[]{:S(2)}) collective-permute-start(bf16[2,48,768]{2,1,0:T(8,128)(2,1)S(1)} %get-tuple-element.230), channel_id=1, source_target_pairs={{0,4},{2,6},{4,0},{6,2},{1,5},{3,7},{5,1},{7,3},{8,12},{10,14},{12... | collective-permute-start | bytes 442376 | tf_op jit(solution)/shard_map/ppermute | solution.py:55
  363.5 26.9 %collective-permute-start.78 = (bf16[2,48,768]{2,1,0:T(8,128)(2,1)S(1)}, bf16[2,48,768]{2,1,0:T(8,128)(2,1)S(1)}, u32[]{:S(2)}, u32[]{:S(2)}) collective-permute-start(bf16[2,48,768]{2,1,0:T(8,128)(2,1)S(1)} %get-tuple-element.231), channel_id=1, source_target_pairs={{0,6},{2,0},{4,2},{6,4},{1,7},{3,1},{5,3},{7,5},{8,14},{10,8},{12,... | collective-permute-start | bytes 442376 | tf_op jit(solution)/shard_map/ppermute | solution.py:55
  388.2 92.4 %collective-permute-start.61 = (bf16[4,2,48,1536]{3,2,1,0:T(8,128)(2,1)}, bf16[4,2,48,1536]{3,2,1,0:T(8,128)(2,1)}, u32[]{:S(2)}, u32[]{:S(2)}) collective-permute-start(bf16[4,2,48,1536]{3,2,1,0:T(8,128)(2,1)} %get-tuple-element.205), channel_id=1, source_target_pairs={{0,8},{8,0},{16,24},{24,16},{1,9},{9,1},{17,25},{25,17},{2,10},{10... | collective-permute-start | bytes 3538952 | tf_op jit(solution)/shard_map/ppermute | solution.py:50
  389.1 92.7 %collective-permute-start.62 = (bf16[4,2,48,1536]{3,2,1,0:T(8,128)(2,1)}, bf16[4,2,48,1536]{3,2,1,0:T(8,128)(2,1)}, u32[]{:S(2)}, u32[]{:S(2)}) collective-permute-start(bf16[4,2,48,1536]{3,2,1,0:T(8,128)(2,1)} %get-tuple-element.206), channel_id=1, source_target_pairs={{0,16},{8,24},{16,0},{24,8},{1,17},{9,25},{17,1},{25,9},{2,18},{10... | collective-permute-start | bytes 3538952 | tf_op jit(solution)/shard_map/ppermute | solution.py:50
  391.2 43.0 %collective-permute-start.80 = (bf16[1,2,48,768]{3,2,1,0:T(8,128)(2,1)}, bf16[1,2,48,768]{3,2,1,0:T(8,128)(2,1)}, u32[]{:S(2)}, u32[]{:S(2)}) collective-permute-start(bf16[1,2,48,768]{3,2,1,0:T(8,128)(2,1)} %fusion.18.own), channel_id=1, source_target_pairs={{0,16},{8,24},{16,0},{24,8},{1,17},{9,25},{17,1},{25,9},{2,18},{10... | collective-permute-start | bytes 442376 | tf_op jit(solution)/shard_map/ppermute | solution.py:50
  411.1 39.4 %collective-permute-start.50 = (bf16[4,2,48,768]{3,2,1,0:T(8,128)(2,1)S(1)}, bf16[4,2,48,768]{3,2,1,0:T(8,128)(2,1)S(1)}, u32[]{:S(2)}, u32[]{:S(2)}) collective-permute-start(bf16[4,2,48,768]{3,2,1,0:T(8,128)(2,1)S(1)} %get-tuple-element.187), channel_id=1, source_target_pairs={{0,8},{8,0},{16,24},{24,16},{1,9},{9,1},{17,25},{25,17},{2,10},{10... | collective-permute-start | bytes 1769480 | tf_op jit(solution)/shard_map/ppermute | solution.py:50
  412.8 39.5 %collective-permute-start.51 = (bf16[4,2,48,768]{3,2,1,0:T(8,128)(2,1)S(1)}, bf16[4,2,48,768]{3,2,1,0:T(8,128)(2,1)S(1)}, u32[]{:S(2)}, u32[]{:S(2)}) collective-permute-start(bf16[4,2,48,768]{3,2,1,0:T(8,128)(2,1)S(1)} %get-tuple-element.188), channel_id=1, source_target_pairs={{0,16},{8,24},{16,0},{24,8},{1,17},{9,25},{17,1},{25,9},{2,18},{10... | collective-permute-start | bytes 1769480 | tf_op jit(solution)/shard_map/ppermute | solution.py:50
  (133 other events, 1518.9 us)
Sparse Core Ops, SparseCore 0:
  339.7 139.8 all-reduce.4
where the time goes:
time: 568 us; the launch traced here: 558 us
  Pallas kernels  189 us (33%)
  waiting for transfers between devices  166 us (29%)
  starting transfers between devices  112 us (20%)
  local copies, waits for them, and re-layouts  49.4 us (9%)
  between operations  15.8 us (3%)
  other arithmetic  14.4 us (3%)
  matrix products  5.89 us (1%)
    ppermute x53, waiting for transfers between devices, flip(): return lax.ppermute(x, axis, [(i, i ^ 1 << bit) for i in range(count)])  89.1 us
    ppermute x30, waiting for transfers between devices, shift(): lax.ppermute(x, axis, [(i, (i + step) % count) for i in range(count)])  77 us
    ppermute x30, starting transfers between devices, shift(): lax.ppermute(x, axis, [(i, (i + step) % count) for i in range(count)])  66.5 us
    pallas_call x24, Pallas kernels, kernel_call(): pl.pallas_call(body, out_shape=[jax.ShapeDtypeStruct(shape, dtype) for sh...  45.7 us
    ppermute x53, starting transfers between devices, flip(): return lax.ppermute(x, axis, [(i, i ^ 1 << bit) for i in range(count)])  45.1 us
    pallas_call x2, Pallas kernels, attention_backward(): pl.pallas_call(body, out_shape=[jax.ShapeDtypeStruct((seq_len, 3 * width)...  27 us
    pallas_call x2, Pallas kernels, attention_forward(): pl.pallas_call(body, out_shape=[jax.ShapeDtypeStruct(shape, dtype) for sh...  25.5 us
    pallas_call x2, Pallas kernels, table_grad(): pl.pallas_call(body, out_shape=jax.ShapeDtypeStruct((heads, bucket_count)...  24.3 us
  transfers between devices with their start and end apart: 84, of which 32 were waited for; matrix products, arithmetic and copies ran while one was open for 8% of the time, Pallas kernels for 24%

commit v1 on v0

--- a/solution.py
+++ b/solution.py
@@ -12,17 +12,14 @@
 F32 = jnp.float32
 
 
-def smooth_act(values):
-    inner = 0.7978845608 * (values + 0.044715 * values * values * values)
-    return 0.5 * values * (1.0 + jnp.tanh(inner))
-
-
-def smooth_slope(values):
-    inner = 0.7978845608 * (values + 0.044715 * values * values * values)
-    tangent = jnp.tanh(inner)
-    return 0.5 * (1.0 + tangent) + 0.5 * values * (1.0 - tangent * tangent) * 0.7978845608 * (
-        1.0 + 0.134145 * values * values
-    )
+def smooth_both(values):
+    square = values * values
+    tangent = jnp.tanh(0.7978845608 * values * (1.0 + 0.044715 * square))
+    rest = 0.5 * (1.0 + tangent)
+    slope = rest + (0.5 * 0.7978845608) * values * (1.0 - tangent * tangent) * (
+        1.0 + 0.134145 * square
+    )
+    return values * rest, slope
 
 
 def row_scale(rows):
@@ -50,12 +47,24 @@
     return lax.ppermute(x, axis, [(i, i ^ (1 << bit)) for i in range(count)])
 
 
+def meet(*values):
+    leaves, tree = jax.tree.flatten(values)
+    return jax.tree.unflatten(tree, lax.optimization_barrier(leaves))
+
+
+def tie(value, *others):
+    return meet(value, *others)[0]
+
+
 def shift(x, axis, step):
     count = lax.axis_size(axis)
     return lax.ppermute(x, axis, [(i, (i + step) % count) for i in range(count)])
 
 
-def kernel_call(body, outs, scalars, arrays, limit=48):
+COST = pl.CostEstimate(flops=1, transcendentals=0, bytes_accessed=1)
+
+
+def kernel_call(body, outs, scalars, arrays, limit=16):
     vmem = pl.BlockSpec(memory_space=pltpu.VMEM)
     return pl.pallas_call(
         body,
@@ -63,6 +72,7 @@
         in_specs=[pl.BlockSpec(memory_space=pltpu.SMEM)] + [vmem] * len(arrays),
         out_specs=[vmem] * len(outs),
         compiler_params=pltpu.CompilerParams(vmem_limit_bytes=limit << 20),
+        cost_estimate=COST,
     )(scalars, *arrays)
 
 
@@ -70,18 +80,26 @@
     return jnp.stack([lax.axis_index("expert"), lax.axis_index("dp") & 3]).astype(jnp.int32)
 
 
-def plane_spread(held):
-    from_x = flip(held, "dp", 0)
-    from_y = flip(held, "dp", 1)
-    return held, from_x, from_y, flip(from_x[:, 0], "dp", 1), flip(from_y[:, 1], "dp", 0)
-
-
-def gather_pair(left, right):
-    count = lax.axis_size("expert")
+def plane_first(held):
+    return flip(held, "dp", 0), flip(held, "dp", 1)
+
+
+def plane_second(from_x, from_y):
+    return flip(from_x[:, 0], "dp", 1), flip(from_y[:, 1], "dp", 0)
+
+
+def quarter_of(left, right):
     rows = left.shape[0] // 4
     place = (lax.axis_index("dp") & 3) * rows
-    piece = jnp.stack([lax.dynamic_slice_in_dim(t, place, rows, 0) for t in (left, right)])
-    return plane_spread(jnp.stack([shift(piece, "expert", step) for step in range(1, count)]))
+    return jnp.stack([lax.dynamic_slice_in_dim(t, place, rows, 0) for t in (left, right)])
+
+
+def z_parts(piece):
+    return [shift(piece, "expert", step) for step in range(1, lax.axis_size("expert"))]
+
+
+def z_spread(piece):
+    return jnp.stack(z_parts(piece))
 
 
 def assemble(left, right, pieces):
@@ -109,12 +127,18 @@
     return (a.astype(F32) + b.astype(F32)).astype(BF16)
 
 
-def reduce_pair(send_a, send_b, keep_a, keep_b):
-    blocks, _, rows, cols = send_a.shape
-    where = place_scalars()
-    got_a, got_b = flip(send_a, "dp", 0), flip(send_b, "dp", 1)
-
-    def second(where, keep_a, keep_b, got_a, got_b, send_a, send_b, next_a, next_b):
+def first_trip(send_a, send_b):
+    return flip(send_a, "dp", 0), flip(send_b, "dp", 1)
+
+
+def second_trip(send_a, send_b):
+    return flip(send_a, "dp", 1), flip(send_b, "dp", 0)
+
+
+def reduce_second(keep_a, keep_b, got_a, got_b):
+    blocks = keep_a.shape[0]
+
+    def body(where, keep_a, keep_b, got_a, got_b, send_a, send_b, next_a, next_b):
         x, y = where[1] & 1, where[1] >> 1
         for k in range(blocks):
             send_a[k] = add_low(keep_a[k, 1 - y], got_a[k, 1 - y])
@@ -122,33 +146,83 @@
             send_b[k] = add_low(keep_b[k, 1 - x], got_b[k, 1 - x])
             next_b[k] = add_low(keep_b[k, x], got_b[k, x])
 
-    part = ((blocks, rows, cols), BF16)
-    send_a, send_b, keep_a, keep_b = kernel_call(
-        second, [part] * 4, where, (keep_a, keep_b, got_a, got_b)
-    )
-    got_a, got_b = flip(send_a, "dp", 1), flip(send_b, "dp", 0)
-    far_bits = range(2, lax.axis_size("dp").bit_length() - 1)
-    for bit in far_bits:
+    parts = [((blocks,) + keep.shape[2:], BF16) for keep in (keep_a, keep_b)]
+    return kernel_call(body, parts * 2, place_scalars(), (keep_a, keep_b, got_a, got_b))
+
+
+def far_sum(keep_a, keep_b, got_a, got_b):
+    for bit in range(2, lax.axis_size("dp").bit_length() - 1):
         keep_a, keep_b = add_low(keep_a, got_a), add_low(keep_b, got_b)
         got_a, got_b = flip(keep_a, "dp", bit), flip(keep_b, "dp", bit)
-
-    def third(where, keep_a, keep_b, got_a, got_b, own, *sends):
-        for step in range(blocks):
+    return keep_a, keep_b, got_a, got_b
+
+
+def expert_held(*parts):
+    def body(where, keep_a, keep_b, got_a, got_b, held_a, held_b):
+        held_a[...] = add_low(keep_a[...], got_a[...])
+        held_b[...] = add_low(keep_b[...], got_b[...])
+
+    shapes = [(part.shape, BF16) for part in parts[:2]]
+    return kernel_call(body, shapes, place_scalars(), far_sum(*parts))
+
+
+def plane_first_e(held, got):
+    return (
+        (flip(held[0], "dp", 0), flip(held[1], "dp", 1)),
+        (flip(got[0], "dp", 0), flip(got[1], "dp", 1)),
+    )
+
+
+def expert_last(held, got, diagonal):
+    def body(where, *refs):
+        place = where[1]
+        for side in range(2):
+            own, near, far_near, far_diag = (refs[side + 2 * number] for number in range(4))
+            rows, cols = own.shape[1:]
+            first = 2 if side == 0 else 1
+            for key, ref in ((0, own), (first, near), (3 - first, far_near), (3, far_diag)):
+                if side == 0:
+                    at = pl.multiple_of((place ^ key) * cols, 128)
+                    refs[8][:, pl.ds(at, cols)] = ref[0].astype(F32)
+                else:
+                    at = pl.multiple_of((place ^ key) * rows, 16)
+                    refs[9][pl.ds(at, rows), :] = ref[0].astype(F32)
+
+    (_, model, quarter), _ = (part.shape for part in held)
+    shapes = [((model, 4 * quarter), F32), ((4 * quarter, model), F32)]
+    return kernel_call(body, shapes, place_scalars(), (*held, *got, *diagonal[0], *diagonal[1]))
+
+
+def reduce_third(*parts):
+    blocks, rows, cols = parts[0].shape
+
+    def body(where, keep_a, keep_b, got_a, got_b, *outs):
+        for step, out in enumerate(outs):
             block = lax.rem(where[0] + step, blocks)
-            out = own if step == 0 else sends[step - 1]
-            out[0] = add_low(keep_a[block], got_a[block])
-            out[1] = add_low(keep_b[block], got_b[block])
+            out[0, 0] = add_low(keep_a[block], got_a[block])
+            out[0, 1] = add_low(keep_b[block], got_b[block])
 
     own, *sends = kernel_call(
-        third, [((2, rows, cols), BF16)] * blocks, where, (keep_a, keep_b, got_a, got_b)
-    )
+        body, [((1, 2, rows, cols), BF16)] * blocks, place_scalars(), far_sum(*parts)
+    )
+    return own, sends
+
+
+def z_trip(sends):
+    return [shift(send, "expert", step + 1) for step, send in enumerate(sends)]
+
+
+def reduce_fourth(own, got):
     total = own.astype(F32)
-    for step, send in enumerate(sends):
-        total = total + shift(send, "expert", step + 1).astype(F32)
-    held = total.astype(BF16)[None]
-    spread = plane_spread(held)
-
-    def last(where, own, from_x, from_y, diag_a, diag_b, out_a, out_b):
+    for part in got:
+        total = total + part.astype(F32)
+    return total.astype(BF16)
+
+
+def reduce_last(held, near, diagonal):
+    _, _, rows, cols = held.shape
+
+    def body(where, own, from_x, from_y, diag_a, diag_b, out_a, out_b):
         place = where[1]
         for side, (out, diag) in enumerate(((out_a, diag_a), (out_b, diag_b))):
             for key, ref in ((0, own), (1, from_x), (2, from_y), (3, diag)):
@@ -156,29 +230,52 @@
                 value = ref[0] if key == 3 else ref[0, side]
                 out[pl.ds(row, rows), :] = value.astype(F32)
 
-    return kernel_call(last, [((4 * rows, cols), F32)] * 2, where, spread)
-
-
-def all_sum(x):
-    for axis in ("mp", "dp", "expert"):
-        for bit in range(lax.axis_size(axis).bit_length() - 1):
-            x = x + flip(x, axis, bit)
-    return x
+    return kernel_call(
+        body, [((4 * rows, cols), F32)] * 2, place_scalars(), (held, *near, *diagonal)
+    )
+
+
+def pack_small(gains, router, tables):
+    model = gains[0].shape[1]
+    heads, levels = tables[0].shape
+    top = len(gains) + router.shape[0]
+    share = 1.0 / lax.axis_size("mp")
+
+    def body(core, *refs):
+        out = refs[-1]
+        out[...] = jnp.zeros_like(out)
+        for number in range(len(gains)):
+            out[number : number + 1, :] = refs[number][...] * share
+        out[len(gains) : top, :] = refs[len(gains)][...]
+        for layer in range(2):
+            for side in range(2):
+
+                @pl.when(core[0] == side)
+                def _():
+                    at = (layer * 2 + side) * 128
+                    out[top : top + heads, at : at + levels] = refs[len(gains) + 1 + layer][...]
+
+    return kernel_call(
+        body,
+        [((16, model), F32)],
+        jnp.stack([lax.axis_index("mp")]).astype(jnp.int32),
+        (*gains, router, *tables),
+    )[0]
 
 
 def whole(shape):
-    return pl.BlockSpec(shape, lambda *_: (0,) * len(shape))
-
-
-PARAMS = pltpu.CompilerParams(vmem_limit_bytes=56 << 20)
-
-
-def build_bias(buckets, tables):
+    return pl.BlockSpec(memory_space=pltpu.VMEM)
+
+
+PARAMS = pltpu.CompilerParams(vmem_limit_bytes=28 << 20)
+
+
+def build_bias(buckets, tables, token):
     heads = tables.shape[0]
     seq_len = buckets.shape[0]
     padded = jnp.pad(tables, ((0, 0), (0, 128 - tables.shape[1])))
 
-    def body(bucket_ref, table_ref, out_ref):
+    def body(bucket_ref, table_ref, _, out_ref):
         head = pl.program_id(0)
         row = jnp.broadcast_to(table_ref[pl.ds(head, 1), :], (seq_len, 128))
         for part in range(seq_len // 128):
@@ -189,10 +286,11 @@
         body,
         out_shape=jax.ShapeDtypeStruct((heads, seq_len, seq_len), F32),
         grid=(heads,),
-        in_specs=[whole((seq_len, seq_len)), whole((heads, 128))],
+        in_specs=[whole((seq_len, seq_len)), whole((heads, 128)), whole(token.shape)],
         out_specs=pl.BlockSpec((1, seq_len, seq_len), lambda h: (h, 0, 0)),
         compiler_params=PARAMS,
-    )(buckets, padded)
+        cost_estimate=COST,
+    )(buckets, padded, token)
 
 
 def lane_masks(head_width):
@@ -204,10 +302,14 @@
     return jnp.where(mask, value, jnp.zeros_like(value))
 
 
+def both(own, got):
+    return own[...].astype(F32) + got[...].astype(F32)
+
+
 def stream_sum(base, partials):
     total = base[...].astype(F32)
     if partials:
-        total = total + (partials[0][...].astype(F32) + partials[1][...].astype(F32))
+        total = total + both(*partials)
     return total
 
 
@@ -249,7 +351,8 @@
                 head = 2 * pair + side
                 scores = dot_nt(query, masked(key, masks[side])) + bias_ref[head]
                 exp_part = jnp.exp(scores - jnp.max(scores, axis=-1, keepdims=True))
-                prob = (exp_part / jnp.sum(exp_part, axis=-1, keepdims=True)).astype(BF16)
+                share = 1.0 / jnp.sum(exp_part, axis=-1, keepdims=True)
+                prob = (exp_part * share).astype(BF16)
                 prob_ref[head] = prob
                 out = dot_nn(prob, masked(value, masks[side]))
                 mixed = out if mixed is None else mixed + out
@@ -269,11 +372,13 @@
         body,
         out_shape=[jax.ShapeDtypeStruct(shape, dtype) for shape, dtype, _ in shapes],
         grid=(seq_len // chunk,),
-        in_specs=[whole(full)] * (1 + count)
+        in_specs=[whole(full)]
+        + [whole(full)] * count
         + [whole((1, model)), whole(weights[0].shape), whole(weights[1].shape)]
         + [pl.BlockSpec((heads, chunk, seq_len), lambda i: (0, i, 0))],
         out_specs=[spec for _, _, spec in shapes],
         compiler_params=PARAMS,
+        cost_estimate=COST,
     )(base, *partials, gain[None], *weights, bias)
 
 
@@ -353,6 +458,7 @@
         out_specs=[whole((seq_len, 3 * width)), rows_of, whole(full)],
         scratch_shapes=[pltpu.VMEM((seq_len, width), F32)] * 2,
         compiler_params=PARAMS,
+        cost_estimate=COST,
     )(grad, *weights, joint, prob)
 
 
@@ -384,10 +490,10 @@
 
 def weight_grads(blocks, lefts, rights):
     model = lefts[0][0].shape[1]
-    cols = sum(y.shape[1] for _, y in lefts)
+    cols = sum(stop - start for _, _, start, stop in lefts)
     rows = model // blocks // 4
     half = ((blocks, 2, rows, cols), BF16)
-    flat = [t for pair in lefts + rights for t in pair]
+    flat = [t for pair in lefts + rights for t in pair[:2]]
 
     def body(where, *refs):
         inputs, outs = refs[: len(flat)], refs[len(flat) :]
@@ -395,8 +501,10 @@
         def side(number, pairs):
             return jnp.concatenate(
                 [
-                    dot_tn(inputs[number + 2 * i][...], inputs[number + 2 * i + 1][...]).astype(BF16)
-                    for i in range(len(pairs))
+                    dot_tn(
+                        inputs[number + 2 * i][...], inputs[number + 2 * i + 1][:, start:stop]
+                    ).astype(BF16)
+                    for i, (_, _, start, stop) in enumerate(pairs)
                 ],
                 axis=1,
             )
@@ -419,13 +527,13 @@
             hot = jnp.concatenate(
                 [jnp.where(index == level, 1.0, 0.0) for level in range(bucket_count)], axis=0
             ).astype(BF16)
-            left = jnp.concatenate(
+            right = jnp.concatenate(
                 [ds_ref[head, rows, :].astype(F32) for head in range(heads)], axis=0
             ).astype(BF16)
-            acc[...] += dot_nt(left, hot)
+            acc[...] += dot_nt(hot, right)
             return carry
 
-        lax.fori_loop(0, seq_len // group, one, 0, unroll=2)
+        lax.fori_loop(0, seq_len // group, one, 0, unroll=4)
         shape = acc.shape
         same = (
             lax.broadcasted_iota(jnp.int32, shape, 0) % group
@@ -433,15 +541,16 @@
         )
         kept = jnp.where(same, acc[...], 0.0)
         spread = (
-            lax.broadcasted_iota(jnp.int32, (shape[1], bucket_count), 0) // group
-            == lax.broadcasted_iota(jnp.int32, (shape[1], bucket_count), 1)
+            lax.broadcasted_iota(jnp.int32, (bucket_count, shape[0]), 1) // group
+            == lax.broadcasted_iota(jnp.int32, (bucket_count, shape[0]), 0)
         ).astype(F32)
         gather = (
-            lax.broadcasted_iota(jnp.int32, (heads, shape[0]), 1) // group
-            == lax.broadcasted_iota(jnp.int32, (heads, shape[0]), 0)
+            lax.broadcasted_iota(jnp.int32, (heads, shape[1]), 1) // group
+            == lax.broadcasted_iota(jnp.int32, (heads, shape[1]), 0)
         ).astype(F32)
         exact = dict(preferred_element_type=F32, precision=lax.Precision.HIGHEST)
-        out_ref[...] = jnp.dot(gather, jnp.dot(kept, spread, **exact), **exact)
+        by_level = jnp.dot(spread, kept, **exact)
+        out_ref[...] = lax.dot_general(gather, by_level, (((1,), (1,)), ((), ())), **exact)
 
     vmem = pl.BlockSpec(memory_space=pltpu.VMEM)
     return pl.pallas_call(
@@ -449,8 +558,9 @@
         out_shape=jax.ShapeDtypeStruct((heads, bucket_count), F32),
         in_specs=[vmem, vmem],
         out_specs=vmem,
-        scratch_shapes=[pltpu.VMEM((heads * group, bucket_count * group), F32)],
+        scratch_shapes=[pltpu.VMEM((bucket_count * group, heads * group), F32)],
         compiler_params=PARAMS,
+        cost_estimate=COST,
     )(ds, buckets)
 
 
@@ -471,9 +581,10 @@
             acc[...] = jnp.zeros_like(acc)
 
         pre = dot_nn(normed_ref[...], in_ref[...])
-        hidden = smooth_act(pre).astype(BF16)
+        act, slope = smooth_both(pre)
+        hidden = act.astype(BF16)
         hidden_ref[...] = hidden
-        slope_ref[...] = smooth_slope(pre).astype(BF16)
+        slope_ref[...] = slope.astype(BF16)
         acc[...] += dot_nt(hidden, out_ref[...])
 
         @pl.when(step == steps - 1)
@@ -497,11 +608,12 @@
         out_specs=[whole(full), whole(full), act, act, whole(full)],
         scratch_shapes=[pltpu.VMEM(full, F32)],
         compiler_params=PARAMS,
+        cost_estimate=COST,
     )(base, *partials, gain[None], w_in, w_out)
 
 
 def norm_step(grad_ref, rows_ref, gain_ref, own_ref, got_ref):
-    upstream = own_ref[...].astype(F32) + got_ref[...].astype(F32)
+    upstream = both(own_ref, got_ref)
     rows = rows_ref[...].astype(F32)
     scale = row_scale(rows)
     scaled = upstream * gain_ref[...]
@@ -523,7 +635,7 @@
         body,
         [(full, F32), (full, BF16), ((1, full[1]), F32)],
         place_scalars(),
-        (grad, rows, gain[None]) + tuple(partials),
+        (grad, rows, gain[None], *partials),
     )
 
 
@@ -568,6 +680,7 @@
         out_specs=[whole(full), whole(full), act, whole(full), whole((1, model))],
         scratch_shapes=[pltpu.VMEM(full, F32)],
         compiler_params=PARAMS,
+        cost_estimate=COST,
     )(grad, rows, gain[None], *partials, w_in, w_out, slope)
 
 
@@ -613,7 +726,7 @@
 def expert_step(rows, grads, router, w_in, w_out):
     half, model = rows[0].shape
     hidden_width = w_in.shape[1]
-    chunk = 256
+    chunk = 512
     steps = hidden_width // chunk
     total = 2 * half
 
@@ -634,9 +747,10 @@
             back_acc[...] = jnp.zeros_like(back_acc)
 
         pre = dot_nn(rows_ref[...], in_ref[...])
-        hidden = smooth_act(pre).astype(BF16)
+        act, slope = smooth_both(pre)
+        hidden = act.astype(BF16)
         hidden_ref[...] = hidden
-        dpre = (dot_nt(grad_ref[...], out_ref[...]) * smooth_slope(pre)).astype(BF16)
+        dpre = (dot_nt(grad_ref[...], out_ref[...]) * slope).astype(BF16)
         dpre_ref[...] = dpre
         res_acc[...] += dot_nn(hidden, out_ref[...])
         back_acc[...] += dot_nt(dpre, in_ref[...])
@@ -672,6 +786,7 @@
         out_specs=[act, act, whole((total, model))] + [whole(part)] * 4,
         scratch_shapes=[pltpu.VMEM((total, model), F32)] * 2 + [pltpu.VMEM((total, model), BF16)],
         compiler_params=PARAMS,
+        cost_estimate=COST,
     )(place_scalars(), *rows, *grads, router, w_in, w_out)
 
 
@@ -704,33 +819,65 @@
 def expert_grads(rows, hidden, dpre, grads):
     half, model = rows[0].shape
     hidden_width = hidden.shape[1]
-    chunk = 256
-
-    def body(own_ref, other_ref, hidden_ref, dpre_ref, grad_ref, in_ref, out_ref, rows_ref):
+    quarter = hidden_width // 4
+
+    def body(where, own_ref, other_ref, hidden_ref, dpre_ref, grad_ref, send_a, send_b, keep_a, keep_b, rows_ref):
         @pl.when(pl.program_id(0) == 0)
         def _():
             rows_ref[:half, :] = own_ref[...]
             rows_ref[half:, :] = other_ref[...]
 
-        in_ref[...] = dot_tn(rows_ref[...], dpre_ref[...]).astype(BF16)
-        out_ref[...] = dot_tn(hidden_ref[...], grad_ref[...]).astype(BF16)
-
-    act = pl.BlockSpec((2 * half, chunk), lambda i: (0, i))
+        step = pl.program_id(0)
+        x, y = where[1] & 1, where[1] >> 1
+        for first, value, keep, send in (
+            ((step & 1) == x, dot_tn(rows_ref[...], dpre_ref[...]), keep_a, send_a),
+            ((step >> 1) == y, dot_tn(hidden_ref[...], grad_ref[...]), keep_b, send_b),
+        ):
+            low = value.astype(BF16)
+
+            @pl.when(first)
+            def _():
+                keep[0] = low
+
+            @pl.when(jnp.logical_not(first))
+            def _():
+                send[0] = low
+
+    def early(step):
+        return jnp.minimum(step, 1)
+
+    def late(step):
+        return jnp.maximum(step - 2, 0)
+
+    def spot_keep(step, where):
+        y = where[1] >> 1
+        return (1 - y) * early(step) + y * late(step), 0, 0
+
+    def spot_send(step, where):
+        y = where[1] >> 1
+        return y * early(step) + (1 - y) * late(step), 0, 0
+
+    act = pl.BlockSpec((2 * half, quarter), lambda i, w: (0, i))
+    shape_a, shape_b = (model, quarter), (quarter, model)
+    col = pl.BlockSpec((1,) + shape_a, lambda i, w: (i >> 1, 0, 0))
     return pl.pallas_call(
         body,
-        out_shape=[
-            jax.ShapeDtypeStruct((model, hidden_width), BF16),
-            jax.ShapeDtypeStruct((hidden_width, model), BF16),
-        ],
-        grid=(hidden_width // chunk,),
-        in_specs=[whole((half, model))] * 2 + [act, act, whole((2 * half, model))],
-        out_specs=[
-            pl.BlockSpec((model, chunk), lambda i: (0, i)),
-            pl.BlockSpec((chunk, model), lambda i: (i, 0)),
-        ],
-        scratch_shapes=[pltpu.VMEM((2 * half, model), BF16)],
+        out_shape=[jax.ShapeDtypeStruct((2,) + shape, BF16) for shape in (shape_a, shape_b)] * 2,
+        grid_spec=pltpu.PrefetchScalarGridSpec(
+            num_scalar_prefetch=1,
+            grid=(4,),
+            in_specs=[whole(None), whole(None), act, act, whole(None)],
+            out_specs=[
+                col,
+                pl.BlockSpec((1,) + shape_b, spot_send),
+                col,
+                pl.BlockSpec((1,) + shape_b, spot_keep),
+            ],
+            scratch_shapes=[pltpu.VMEM((2 * half, model), BF16)],
+        ),
         compiler_params=PARAMS,
-    )(*rows, hidden, dpre, grads)
+        cost_estimate=COST,
+    )(place_scalars(), *rows, hidden, dpre, grads)
 
 
 def receive_slots(grad, rows, gain, spots, halves):
@@ -798,6 +945,7 @@
     head_local = table_first.shape[1] // lax.axis_size("mp")
 
     width = query_first.shape[1]
+    ff_width = dense_in.shape[1]
     shards = (
         (
             jnp.concatenate([query_first, key_first], axis=1),
@@ -809,14 +957,14 @@
             jnp.concatenate([value_second, output_second.T], axis=1),
         ),
     )
-    gathered = [gather_pair(*pair) for pair in shards]
+    far_one = z_spread(quarter_of(*shards[0]))
 
     stream_zero = lax.all_gather(tokens, "mp", axis=0, tiled=True)
     grad_four = lax.all_gather(cotangent, "mp", axis=0, tiled=True)
 
-    def local_bias(table):
+    def local_bias(table, token):
         return build_bias(
-            buckets, lax.dynamic_slice_in_dim(table, mp_index * head_local, head_local, 1).T
+            buckets, lax.dynamic_slice_in_dim(table, mp_index * head_local, head_local, 1).T, token
         )
 
     chosen = routes[:, 0]
@@ -834,97 +982,188 @@
     send_spots = jnp.where(in_own_half, spot, -1)[None, :]
     back_spots = jnp.where(in_own_half, spot, spot + half)[:, None]
 
-    def dispatch(blocks):
-        own = stacked(
-            [blocks[0]] + [shift(blocks[step], "expert", step) for step in range(1, z_count)]
-        )
+    def sent_on(blocks):
+        return [blocks[0]] + [shift(blocks[step], "expert", step) for step in range(1, z_count)]
+
+    def with_other(own):
         return own, flip(own, "mp", 0)
 
-    def give_back(blocks):
-        own = stacked(
-            [blocks[0]]
-            + [shift(blocks[step], "expert", z_count - step) for step in range(1, z_count)]
-        )
-        return own, flip(own, "mp", 0)
+    def sent_back(blocks):
+        return [blocks[0]] + [
+            shift(blocks[step], "expert", z_count - step) for step in range(1, z_count)
+        ]
 
     def swapped(partial):
         return partial, flip(partial, "mp", 0)
 
-    weights_one = assemble(*shards[0], gathered[0])
+    near_one = plane_first(far_one)
+    token = flip(far_one[0, 0, :8, :128], "mp", 0)
+    piece_ff, token = meet(quarter_of(*shards[1]), token)
+    got_ff = z_parts(piece_ff)
+    bias_one = local_bias(table_first, token)
+    near_one, bias_one = meet(near_one, bias_one)
+    diag_one = plane_second(*near_one)
+    bias_two = local_bias(table_second, near_one[0][0, 0, :8, :128])
+    diag_one, got_ff, bias_two = meet(diag_one, got_ff, bias_two)
+    far_ff = jnp.stack(got_ff)
+    near_ff = plane_first(far_ff)
+    weights_one = assemble(*shards[0], (far_one, *near_one, *diag_one))
     _, normed_one, joint_one, prob_one, mixed_one, partial = attention_forward(
-        stream_zero, (), norm_first, weights_one, local_bias(table_first)
-    )
-    w_in_full, w_out_full = assemble(*shards[1], gathered[1])
+        tie(stream_zero, far_ff), (), norm_first, weights_one, bias_one
+    )
+    piece_two, partial = meet(quarter_of(*shards[2]), partial)
+    got_two = z_parts(piece_two)
+    pair, near_ff = meet(swapped(partial), near_ff)
+    diag_ff = plane_second(*near_ff)
+    diag_ff, pair, got_two = meet(diag_ff, pair, got_two)
+    far_two = jnp.stack(got_two)
+    near_two = plane_first(far_two)
+    to_slots = (jnp.arange(half, dtype=jnp.int32)[:, None] == send_spots).astype(BF16)
+    grad_sent = dot_nn(to_slots, tie(grad_four, pair)).astype(BF16)
+    grad_got = sent_on([grad_sent[i * slots : (i + 1) * slots] for i in range(z_count)])
+    w_in_full, w_out_full = assemble(*shards[1], (far_ff, *near_ff, *diag_ff))
     stream_one, normed_ff, hidden, slope, partial = dense_forward(
-        stream_zero, swapped(partial), dense_gain, w_in_full, w_out_full
-    )
-
-    grad_four, partial = lax.optimization_barrier((grad_four, partial))
-    to_slots = (jnp.arange(half, dtype=jnp.int32)[:, None] == send_spots).astype(BF16)
-    grad_sent = dot_nn(to_slots, grad_four).astype(BF16)
-    grad_slots = dispatch([grad_sent[i * slots : (i + 1) * slots] for i in range(z_count)])
-
-    weights_two = assemble(*shards[2], gathered[2])
+        stream_zero, pair, dense_gain, w_in_full, tie(w_out_full, grad_sent)
+    )
+    near_two, partial = meet(near_two, partial)
+    diag_two = plane_second(*near_two)
+    pair, diag_two = meet(swapped(partial), diag_two)
+    weights_two = assemble(*shards[2], (far_two, *near_two, *diag_two))
     stream_two, normed_two, joint_two, prob_two, mixed_two, partial = attention_forward(
-        stream_one, swapped(partial), norm_second, weights_two, local_bias(table_second)
-    )
+        stream_one, pair, norm_second, weights_two, bias_two
+    )
+
+    partial, grad_got = meet(partial, grad_got)
 
     stream_three, moe_rows, *sent = send_slots(
         stream_two, swapped(partial), expert_gain, (send_spots, half), z_count
     )
-    moe_slots = dispatch(sent)
+    moe_got = sent_on(sent)
+    grad_slots = with_other(stacked(tie(grad_got, sent)))
+    moe_slots = with_other(stacked(tie(moe_got, grad_slots)))
     router_rows = router.T
     expert_hidden, expert_dpre, expert_rows, res_own, res_other, back_own, back_other = expert_step(
         moe_slots, grad_slots, router_rows, expert_in[0], expert_out[0]
     )
+    halves_e = expert_grads(moe_slots, expert_hidden, expert_dpre, expert_rows)
+    res_got, back_got, halves_e = meet(
+        flip(res_other, "mp", 0), flip(back_other, "mp", 0), halves_e
+    )
+    got_e = first_trip(*halves_e[:2])
+    keep_e = [part[None] for part in halves_e[2:]]
     *returns, grad_router = expert_finish(
-        (res_own, flip(res_other, "mp", 0)),
-        (back_own, flip(back_other, "mp", 0)),
+        (res_own, res_got),
+        (back_own, back_got),
         moe_slots[0],
         grad_slots[0],
         router_rows,
         z_count,
     )
-    back_slots = give_back(returns[:z_count])
-    grad_expert_in, grad_expert_out = expert_grads(
-        moe_slots, expert_hidden, expert_dpre, expert_rows
-    )
-    expert_in_sum, expert_out_sum = lax.psum((grad_expert_in, grad_expert_out), "dp")
-
+    back_slots = with_other(stacked(sent_back(returns[:z_count])))
     grad_three, grad_low, grad_expert_gain = receive_slots(
         grad_four, stream_three, expert_gain, back_spots, back_slots
     )
+    grad_low, got_e = meet(grad_low, got_e)
+    send_ea, send_eb, *keep_e = reduce_second(*keep_e, got_e[0][None], got_e[1][None])
+    send_ea, send_eb, grad_low, *result_blocks = meet(send_ea, send_eb, grad_low, *returns[z_count:])
+    got_e = second_trip(send_ea, send_eb)
+    result_got = sent_back(result_blocks)
+
+    def attention_grads(normed, dj, low, mixed):
+        return weight_grads(
+            z_count,
+            [(normed, dj, 0, 2 * width)],
+            [(normed, dj, 2 * width, 3 * width), (low, mixed, 0, width)],
+        )
 
     dj_two, ds_two, partial = attention_backward(grad_low, weights_two, joint_two, prob_two)
-
-    def attention_grads(normed, dj, low, mixed):
-        return reduce_pair(
-            *weight_grads(
-                z_count,
-                [(normed, dj[:, : 2 * width])],
-                [(normed, dj[:, 2 * width :]), (low, mixed)],
-            )
-        )
-
-    two = attention_grads(normed_two, dj_two, grad_low, mixed_two)
+    result_got, partial, dj_two, got_e = meet(result_got, partial, dj_two, got_e)
+    pair = swapped(partial)
+    held_e = expert_held(*keep_e, *got_e)
+    held_e, dj_two = meet(held_e, dj_two)
+    from_e = (flip(held_e[0], "dp", 1), flip(held_e[1], "dp", 0))
+    halves_two = attention_grads(normed_two, dj_two, grad_low, mixed_two)
+    pair, halves_two = meet(pair, halves_two)
+    got_two = first_trip(*halves_two[:2])
     grad_two, grad_low, dpre, partial, grad_norm_second = dense_backward(
-        grad_three, stream_two, norm_second, swapped(partial), w_in_full, w_out_full, slope
-    )
-    ff_in, ff_out = reduce_pair(
-        *weight_grads(z_count, [(normed_ff, dpre)], [(grad_low, hidden)])
-    )
-    grad_one, grad_low, grad_dense_gain = norm_kernel(
-        grad_two, stream_one, dense_gain, swapped(partial)
-    )
+        grad_three, stream_two, norm_second, pair, w_in_full, w_out_full, slope
+    )
+    from_e, partial, dpre = meet(from_e, partial, dpre)
+    pair = swapped(partial)
+    halves_ff = weight_grads(
+        z_count, [(normed_ff, dpre, 0, ff_width)], [(grad_low, hidden, 0, ff_width)]
+    )
+    pair, halves_ff, got_two = meet(pair, halves_ff, got_two)
+    got_ff = first_trip(*halves_ff[:2])
+    *send_two, keep_a, keep_b = reduce_second(*halves_two[2:], *got_two)
+    keep_two = (keep_a, keep_b)
+    send_two, pair = meet(send_two, pair)
+    got_two = second_trip(*send_two)
+    grad_one, grad_low, grad_dense_gain = norm_kernel(grad_two, stream_one, dense_gain, pair)
     dj_one, ds_one, partial = attention_backward(grad_low, weights_one, joint_one, prob_one)
-    one = attention_grads(normed_one, dj_one, grad_low, mixed_one)
-    grad_zero, _, grad_norm_first = norm_kernel(
-        grad_one, stream_zero, norm_first, swapped(partial)
-    )
+    pair = swapped(partial)
+    halves_one = attention_grads(normed_one, dj_one, grad_low, mixed_one)
+    pair, halves_one, got_two = meet(pair, halves_one, got_two)
+    own_two, send_two = reduce_third(*keep_two, *got_two)
+    send_two, halves_one = meet(send_two, halves_one)
+    got_one = first_trip(*halves_one[:2])
+    grad_zero, _, grad_norm_first = norm_kernel(grad_one, stream_zero, norm_first, pair)
+    grad_norm_first, got_ff, send_two = meet(grad_norm_first, got_ff, send_two)
+    got_two = z_trip(send_two)
+    *send_ff, keep_a, keep_b = reduce_second(*halves_ff[2:], *got_ff)
+    keep_ff = (keep_a, keep_b)
+    send_ff, ds_two, got_one = meet(send_ff, ds_two, got_one)
+    got_ff = second_trip(*send_ff)
+    *send_one, keep_a, keep_b = reduce_second(*halves_one[2:], *got_one)
+    keep_one = (keep_a, keep_b)
+    table_two_grad = table_grad(ds_two, buckets, bucket_count)
+    table_two_grad, got_ff, got_two, send_one = meet(table_two_grad, got_ff, got_two, send_one)
+    got_one = second_trip(*send_one)
+    own_ff, send_ff = reduce_third(*keep_ff, *got_ff)
+    send_ff, ds_one = meet(send_ff, ds_one)
+    got_ff = z_trip(send_ff)
+    held_two = reduce_fourth(own_two, got_two)
+    table_one_grad = table_grad(ds_one, buckets, bucket_count)
+    small = pack_small(
+        (grad_norm_first, grad_dense_gain, grad_norm_second, grad_expert_gain),
+        grad_router,
+        (table_one_grad, table_two_grad),
+    )
+    small, got_one, held_two = meet(small, got_one, held_two)
+    own_one, send_one = reduce_third(*keep_one, *got_one)
+    near_e = plane_first_e(held_e, from_e)
+    got_small = flip(small, "mp", 0)
+    send_one, got_small, got_ff = meet(send_one, got_small, got_ff)
+    small = small + got_small
+    got_one = z_trip(send_one)
+    held_ff = reduce_fourth(own_ff, got_ff)
+    held_ff, near_e = meet(held_ff, near_e)
+    near_ff = plane_first(held_ff)
+    got_small = flip(small, "dp", 0)
+    expert_in_sum, expert_out_sum = expert_last(held_e, from_e, near_e)
+    near_ff, got_small, got_one, expert_in_sum = meet(near_ff, got_small, got_one, expert_in_sum)
+    small = small + got_small
+    held_one = reduce_fourth(own_one, got_one)
+    diag_ff = plane_second(*near_ff)
+    got_small = flip(small, "dp", 1)
+    diag_ff, got_small, held_one = meet(diag_ff, got_small, held_one)
+    small = small + got_small
+    for bit in range(2, lax.axis_size("dp").bit_length() - 1):
+        small = small + flip(small, "dp", bit)
+    near_two, near_one = plane_first(held_two), plane_first(held_one)
+    got_small = flip(small, "expert", 0)
+    ff_in, ff_out = reduce_last(held_ff, near_ff, diag_ff)
+    near_two, near_one, got_small, ff_in = meet(near_two, near_one, got_small, ff_in)
+    small = small + got_small
+    diag_two, diag_one = plane_second(*near_two), plane_second(*near_one)
+    small = small + flip(small, "expert", 1)
+    two = reduce_last(held_two, near_two, diag_two)
+    one = reduce_last(held_one, near_one, diag_one)
     first_row = mp_index * tok_local
     grad_zero = lax.dynamic_slice_in_dim(grad_zero, first_row, tok_local, 0)
-
-    result_own, result_got = give_back(returns[z_count:])
+    result_own = stacked(result_got)
+
+    result_got = flip(result_own, "mp", 0)
     spots_here = lax.dynamic_slice_in_dim(back_spots, first_row, tok_local, 0)
     lanes = jnp.arange(half, dtype=jnp.int32)[None, :]
     result_rows = dot_nn((lanes == spots_here).astype(BF16), result_own) + dot_nn(
@@ -939,32 +1178,18 @@
         lax.dynamic_slice_in_dim(stream_three, first_row, tok_local, 0) + own_gate * result_rows
     )
 
-    table_one_grad = table_grad(ds_one, buckets, bucket_count)
-    table_two_grad = table_grad(ds_two, buckets, bucket_count)
-
-    def full_table(local):
-        zero = jnp.zeros((table_first.shape[1], bucket_count), F32)
-        return lax.dynamic_update_slice_in_dim(zero, local, mp_index * head_local, 0)
-
-    share = 1.0 / lax.axis_size("mp")
-    parts = [
-        grad_norm_first[0] * share,
-        grad_dense_gain[0] * share,
-        grad_norm_second[0] * share,
-        grad_expert_gain[0] * share,
-        grad_router.reshape(-1),
-        full_table(table_one_grad).reshape(-1),
-        full_table(table_two_grad).reshape(-1),
-    ]
-    sizes = [p.shape[0] for p in parts]
-    packed = all_sum(jnp.concatenate(parts).reshape(-1, 128)).reshape(-1)
-    small, start = [], 0
-    for size in sizes:
-        small.append(packed[start : start + size])
-        start += size
-    router_sum = small[4].reshape(expert_count, model_width).T
-    table_one_sum = small[5].reshape(table_first.shape[1], bucket_count).T
-    table_two_sum = small[6].reshape(table_first.shape[1], bucket_count).T
+    router_sum = small[4 : 4 + expert_count].T
+    base = 4 + expert_count
+    table_one_sum, table_two_sum = (
+        jnp.concatenate(
+            [
+                small[base : base + head_local, at * 128 : at * 128 + bucket_count]
+                for at in (layer * 2, layer * 2 + 1)
+            ],
+            axis=0,
+        ).T
+        for layer in range(2)
+    )
 
     return (
         final_rows,
@@ -986,8 +1211,8 @@
         table_two_sum,
         small[3],
         router_sum,
-        expert_in_sum.astype(F32)[None],
-        expert_out_sum.astype(F32)[None],
+        expert_in_sum[None],
+        expert_out_sum[None],
     )
 
 

time: 568 us -> 471 us (0.83)
  Pallas kernels: 189 us -> 138 us
  starting transfers between devices: 112 us -> 98.9 us
  local copies, waits for them, and re-layouts: 49.4 us -> 36.6 us
  between operations: 15.8 us -> 3.01 us
  other arithmetic: 14.4 us -> 7.48 us
    ppermute x30, starting transfers between devices: 66.5 us -> 48 us  [shift(): lax.ppermute(x, axis, [(i, (i + step) % count) for i in range(count)])]
    ppermute x53 -> x64, waiting for transfers between devices: 89.1 us -> 100 us  [flip(): return lax.ppermute(x, axis, [(i, i ^ 1 << bit) for i in range(count)])]
    pallas_call x2, Pallas kernels: 24.3 us -> 14 us  [table_grad(): pl.pallas_call(body, out_shape=jax.ShapeDtypeStruct((heads, bucket_count)...]
    broadcast_in_dim x5 -> x0, other arithmetic: 8.16 us -> none  [the longest x1 4.65 us: on_device(): expert_in_sum.astype(F32)[None]]
    ppermute x30, waiting for transfers between devices: 77 us -> 69.6 us  [shift(): lax.ppermute(x, axis, [(i, (i + step) % count) for i in range(count)])]
    pallas_call x2, Pallas kernels: 27 us -> 19.8 us  [attention_backward(): pl.pallas_call(body, out_shape=[jax.ShapeDtypeStruct((seq_len, 3 * width)...]
    pallas_call x1, Pallas kernels: 21.7 us -> 14.5 us  [expert_step(): pl.pallas_call(body, out_shape=[jax.ShapeDtypeStruct((total, hidden_width...]
    ppermute x53 -> x64, starting transfers between devices: 45.1 us -> 50.9 us  [flip(): return lax.ppermute(x, axis, [(i, i ^ 1 << bit) for i in range(count)])]
  transfers between devices with their start and end apart: 84 -> 94, of which waited for: 32 -> 34; matrix products, arithmetic and copies ran while one was open for 8% -> 4% of each run, Pallas kernels for 24% -> 23%
where the time goes in v1:
time: 471 us; the launch traced here: 462 us
  waiting for transfers between devices  170 us (36%)
  Pallas kernels  138 us (29%)
  starting transfers between devices  98.9 us (21%)
  local copies, waits for them, and re-layouts  36.6 us (8%)
  other arithmetic  7.48 us (2%)
  blocking collectives  4.86 us (1%)
    ppermute x64, waiting for transfers between devices, flip(): return lax.ppermute(x, axis, [(i, i ^ 1 << bit) for i in range(count)])  100 us
    ppermute x30, waiting for transfers between devices, shift(): lax.ppermute(x, axis, [(i, (i + step) % count) for i in range(count)])  69.6 us
    ppermute x64, starting transfers between devices, flip(): return lax.ppermute(x, axis, [(i, i ^ 1 << bit) for i in range(count)])  50.9 us
    ppermute x30, starting transfers between devices, shift(): lax.ppermute(x, axis, [(i, (i + step) % count) for i in range(count)])  48 us
    pallas_call x28, Pallas kernels, kernel_call(): pl.pallas_call(body, out_shape=[jax.ShapeDtypeStruct(shape, dtype) for sh...  40.8 us
    pallas_call x2, Pallas kernels, attention_forward(): pl.pallas_call(body, out_shape=[jax.ShapeDtypeStruct(shape, dtype) for sh...  20.8 us
    unnamed x226, local copies, waits for them, and re-layouts  20.7 us
    pallas_call x2, Pallas kernels, attention_backward(): pl.pallas_call(body, out_shape=[jax.ShapeDtypeStruct((seq_len, 3 * width)...  19.8 us
  transfers between devices with their start and end apart: 94, of which 34 were waited for; matrix products, arithmetic and copies ran while one was open for 4% of the time, Pallas kernels for 23%

profile of v1, /device:TPU:0, one launch (start us, length us, event | category | flops | bytes accessed | tf_op | source)
XLA Modules:
  0.0 461.9 jit_solution(5503572741248544399)
XLA Ops:
  4.2 5.0 %collective-permute-start.2 = (bf16[2,48,768]{2,1,0:T(8,128)(2,1)}, bf16[2,48,768]{2,1,0:T(8,128)(2,1)S(1)}, u32[]{:S(2)}, u32[]{:S(2)}) collective-permute-start(bf16[2,48,768]{2,1,0:T(8,128)(2,1)} %pad_maximum_fusion.7), channel_id=1, source_target_pairs={{0,6},{2,0},{4,2},{6,4},{1,7},{3,1},{5,3},{7,5},{8,14},{10,8},{12,... | collective-permute-start | bytes 442376 | tf_op jit(solution)/shard_map/ppermute | solution.py:61
  15.4 6.7 %collective-permute-done.1 = bf16[2,48,768]{2,1,0:T(8,128)(2,1)} collective-permute-done((bf16[2,48,768]{2,1,0:T(8,128)(2,1)}, bf16[2,48,768]{2,1,0:T(8,128)(2,1)}, u32[]{:S(2)}, u32[]{:S(2)}) %collective-permute-start.1) | collective-permute-done | bytes 147488 | tf_op jit(solution)/shard_map/ppermute | solution.py:61
  32.9 4.7 %shard_map.382.refs_4_ = f32[6,512,512]{2,1,0:T(8,128)S(1)} custom-call(s32[512,512]{1,0:T(8,128)S(1)} %copy-done.2, f32[6,128]{1,0:T(8,128)S(1)} %pad.7.table_ref, bf16[8,128]{1,0:T(8,128)(2,1)S(1)} %collective-permute-done.5._), custom_call_target="tpu_custom_call" | custom-call | flops 1 | bytes 1 | tf_op jit(solution)/shard_map/pallas_call | solution.py:285
  41.3 4.7 %shard_map.383.refs_6_ = f32[6,512,512]{2,1,0:T(8,128)S(1)} custom-call(s32[512,512]{1,0:T(8,128)S(1)} %copy-done.2, f32[6,128]{1,0:T(8,128)S(1)} %pad.8.table_ref, bf16[8,128]{1,0:T(8,128)(2,1)S(1)} %slice_bitcast_fusion.16._), custom_call_target="tpu_custom_call" | custom-call | flops 1 | bytes 1 | tf_op jit(solution)/shard_map/pallas_call | solution.py:285
  46.0 11.3 %collective-permute-done.9 = bf16[2,48,1536]{2,1,0:T(8,128)(2,1)S(1)} collective-permute-done((bf16[2,48,1536]{2,1,0:T(8,128)(2,1)}, bf16[2,48,1536]{2,1,0:T(8,128)(2,1)S(1)}, u32[]{:S(2)}, u32[]{:S(2)}) %collective-permute-start.9) | collective-permute-done | bytes 294944 | tf_op jit(solution)/shard_map/ppermute | solution.py:61
  61.6 10.4 %shard_map.385 = (f32[512,768]{1,0:T(8,128)}, bf16[512,768]{1,0:T(8,128)(2,1)S(1)}, bf16[512,1152]{1,0:T(8,128)(2,1)S(1)}, bf16[6,512,512]{2,1,0:T(8,128)(2,1)S(...) custom-call(bf16[512,768]{1,0:T(8,128)(2,1)S(1)} %all_gather.6.refs_0_.base_ref.rows_ref, ...), custom_call_target="tpu_custom_call" | custom-call | flops 1 | bytes 1 | tf_op jit(solution)/shard_map/pallas_call | solution.py:371
  86.6 8.1 %collective-permute-done.17 = bf16[2,48,768]{2,1,0:T(8,128)(2,1)S(1)} collective-permute-done((bf16[2,48,768]{2,1,0:T(8,128)(2,1)S(1)}, bf16[2,48,768]{2,1,0:T(8,128)(2,1)S(1)}, u32[]{:S(2)}, u32[]{:S(2)}) %collective-permute-start.17) | collective-permute-done | bytes 147488 | tf_op jit(solution)/shard_map/ppermute | solution.py:61
  102.2 5.5 %shard_map.387 = (f32[512,768]{1,0:T(8,128)S(1)}, bf16[512,768]{1,0:T(8,128)(2,1)S(1)}, bf16[512,1536]{1,0:T(8,128)(2,1)S(1)}, bf16[512,1536]{1,0:T(8,128)(2,1)S(1)}, bf16[512,768]{1,0:T(8,128)(2,1)S(1)}) custom-call(bf16[512,768]{1,0:T(8,128)(2,1)S(1)} %all_gather.6.refs_0_.base_ref.rows_ref, bf16[512,768]{1,0:T(8,128)(2,1)S(1)} %get-tuple-element.325.own_ref, ...), custom_call_target="tpu_custom_call" | custom-call | flops 1 | bytes 1 | tf_op jit(solution)/shard_map/pallas_call | solution.py:597
  117.9 10.3 %shard_map.389 = (f32[512,768]{1,0:T(8,128)S(1)}, bf16[512,768]{1,0:T(8,128)(2,1)S(1)}, bf16[512,1152]{1,0:T(8,128)(2,1)S(1)}, bf16[6,512,512]{2,1,0:T(8,128)(2,...) custom-call(f32[512,768]{1,0:T(8,128)S(1)} %get-tuple-element.333.refs_0_.rows_ref, ...), custom_call_target="tpu_custom_call" | custom-call | flops 1 | bytes 1 | tf_op jit(solution)/shard_map/pallas_call | solution.py:371
  148.6 5.3 %collective-permute-done.28.refs_1_ = bf16[128,768]{1,0:T(8,128)(2,1)S(1)} collective-permute-done((bf16[128,768]{1,0:T(8,128)(2,1)S(1)}, bf16[128,768]{1,0:T(8,128)(2,1)S(1)}, u32[]{:S(2)}, u32[]{:S(2)}) %collective-permute-start.28) | collective-permute-done | bytes 196640 | tf_op jit(solution)/shard_map/ppermute | solution.py:61
  153.9 7.8 %collective-permute-done.29.refs_2_ = bf16[128,768]{1,0:T(8,128)(2,1)S(1)} collective-permute-done((bf16[128,768]{1,0:T(8,128)(2,1)S(1)}, bf16[128,768]{1,0:T(8,128)(2,1)S(1)}, u32[]{:S(2)}, u32[]{:S(2)}) %collective-permute-start.29) | collective-permute-done | bytes 196640 | tf_op jit(solution)/shard_map/ppermute | solution.py:61
  164.7 14.5 %shard_map.393 = (bf16[1024,1536]{1,0:T(8,128)(2,1)S(1)}, bf16[1024,1536]{1,0:T(8,128)(2,1)S(1)}, bf16[1024,768]{1,0:T(8,128)(2,1)S(1)}, f32[512,768]{1,0:T(8,12...) custom-call(s32[2]{0:T(128)S(1)} %pad_add_fusion.where._, ...), custom_call_target="tpu_custom_call" | custom-call | flops 1 | bytes 1 | tf_op jit(solution)/shard_map/pallas_call | solution.py:767
  179.8 8.5 %shard_map.394 = (bf16[2,768,384]{2,1,0:T(8,128)(2,1)S(1)}, bf16[2,384,768]{2,1,0:T(8,128)(2,1)S(1)}, bf16[2,768,384]{2,1,0:T(8,128)(2,1)S(1)}, bf16[2,384,768]{2,1,0:T(8,128)(2,1)S(1)}) custom-call(s32[2]{0:T(128)S(1)} %pad_add_fusion.where._, bf16[512,768]{1,0:T(8,128)(2,1)S(1)} %shard_map.392.own_ref.rows_ref, ...), custom_call_target="tpu_custom_call" | custom-call | flops 1 | bytes 1 | tf_op jit(solution)/shard_map/pallas_call | solution.py:863
  192.2 4.3 collective-permute-start.35
  202.0 13.4 %collective-permute-done.36.refs_2_ = bf16[128,768]{1,0:T(8,128)(2,1)S(1)} collective-permute-done((bf16[128,768]{1,0:T(8,128)(2,1)S(1)}, bf16[128,768]{1,0:T(8,128)(2,1)S(1)}, u32[]{:S(2)}, u32[]{:S(2)}) %collective-permute-start.36) | collective-permute-done | bytes 196640 | tf_op jit(solution)/shard_map/ppermute | solution.py:61
  227.1 9.9 %shard_map.399 = (bf16[512,1152]{1,0:T(8,128)(2,1)S(1)}, bf16[6,512,512]{2,1,0:T(8,128)(2,1)S(1)}, bf16[512,768]{1,0:T(8,128)(2,1)S(1)}) custom-call(bf16[512,768]{1,0:T(8,128)(2,1)S(1)} %get-tuple-element.404.grad_ref.refs_4_, bf16[768,768]{1,0:T(8,128)(2,1)S(1)} %copy-done.11, bf16[768,768]{1,0:T(8,128)(2,1)S(1)} %copy-done.13, ...), custom_call_target="tpu_custom_call" | custom-call | flops 1 | bytes 1 | tf_op jit(solution)/shard_map/pallas_call | solution.py:443
  237.1 5.7 %collective-permute-done.42.refs_2_ = bf16[128,768]{1,0:T(8,128)(2,1)S(1)} collective-permute-done((bf16[128,768]{1,0:T(8,128)(2,1)S(1)}, bf16[128,768]{1,0:T(8,128)(2,1)S(1)}, u32[]{:S(2)}, u32[]{:S(2)}) %collective-permute-start.42) | collective-permute-done | bytes 196640 | tf_op jit(solution)/shard_map/ppermute | solution.py:61
  247.7 5.1 %shard_map.403 = (f32[512,768]{1,0:T(8,128)S(1)}, bf16[512,768]{1,0:T(8,128)(2,1)S(1)}, bf16[512,1536]{1,0:T(8,128)(2,1)S(1)}, bf16[512,768]{1,0:T(8,128)(2,1)S(1)}, f32[1,768]{1,0:T(1,128)S(1)}) custom-call(f32[512,768]{1,0:T(8,128)S(1)} %get-tuple-element.415.grad_ref, f32[512,768]{1,0:T(8,128)S(1)} %copy-done.9, ...), custom_call_target="tpu_custom_call" | custom-call | flops 1 | bytes 1 | tf_op jit(solution)/shard_map/pallas_call | solution.py:669
  252.7 6.7 %collective-permute-done.48.refs_2_ = bf16[1,768,384]{2,1,0:T(8,128)(2,1)S(1)} collective-permute-done((bf16[1,768,384]{2,1,0:T(8,128)(2,1)S(1)}, bf16[1,768,384]{2,1,0:T(8,128)(2,1)S(1)}, u32[]{:S(2)}, u32[]{:S(2)}) %collective-permute-start.48) | collective-permute-done | bytes 589856 | tf_op jit(solution)/shard_map/ppermute | solution.py:47
  261.9 4.0 shard_map.404
  265.9 9.7 %collective-permute-done.51.got_a = bf16[4,2,48,768]{3,2,1,0:T(8,128)(2,1)S(1)} collective-permute-done((bf16[4,2,48,768]{3,2,1,0:T(8,128)(2,1)S(1)}, bf16[4,2,48,768]{3,2,1,0:T(8,128)(2,1)S(1)}, u32[]{:S(2)}, u32[]{:S(2)}) %collective-permute-start.51) | collective-permute-done | bytes 589856 | tf_op jit(solution)/shard_map/ppermute | solution.py:47
  279.0 9.9 %shard_map.407 = (bf16[512,1152]{1,0:T(8,128)(2,1)S(1)}, bf16[6,512,512]{2,1,0:T(8,128)(2,1)S(1)}, bf16[512,768]{1,0:T(8,128)(2,1)S(1)}) custom-call(bf16[512,768]{1,0:T(8,128)(2,1)S(1)} %get-tuple-element.461.grad_ref.refs_4_, bf16[768,768]{1,0:T(8,128)(2,1)S(1)} %copy-done.15, bf16[768,768]{1,0:T(8,128)(2,1)S(1)} %copy-done.17, ...), custom_call_target="tpu_custom_call" | custom-call | flops 1 | bytes 1 | tf_op jit(solution)/shard_map/pallas_call | solution.py:443
  295.7 29.1 %collective-permute-done.54.got_a = bf16[4,48,768]{2,1,0:T(8,128)(2,1)S(1)} collective-permute-done((bf16[4,48,768]{2,1,0:T(8,128)(2,1)S(1)}, bf16[4,48,768]{2,1,0:T(8,128)(2,1)S(1)}, u32[]{:S(2)}, u32[]{:S(2)}) %collective-permute-start.54) | collective-permute-done | bytes 294944 | tf_op jit(solution)/shard_map/ppermute | solution.py:47
  331.2 9.0 %collective-permute-done.58.got_a = bf16[4,2,48,768]{3,2,1,0:T(8,128)(2,1)S(1)} collective-permute-done((bf16[4,2,48,768]{3,2,1,0:T(8,128)(2,1)S(1)}, bf16[4,2,48,768]{3,2,1,0:T(8,128)(2,1)S(1)}, u32[]{:S(2)}, u32[]{:S(2)}) %collective-permute-start.58) | collective-permute-done | bytes 589856 | tf_op jit(solution)/shard_map/ppermute | solution.py:47
  347.5 7.0 %shard_map.412.refs_6_ = f32[6,32]{1,0:T(8,128)S(1)} custom-call(bf16[6,512,512]{2,1,0:T(8,128)(2,1)S(1)} %get-tuple-element.510.ds_ref, s32[512,512]{1,0:T(8,128)S(1)} %copy-done.2), custom_call_target="tpu_custom_call" | custom-call | flops 1 | bytes 1 | tf_op jit(solution)/shard_map/pallas_call | solution.py:556
  369.8 7.0 %shard_map.415.refs_5_ = f32[6,32]{1,0:T(8,128)S(1)} custom-call(bf16[6,512,512]{2,1,0:T(8,128)(2,1)S(1)} %copy-done.27, s32[512,512]{1,0:T(8,128)S(1)} %copy-done.2), custom_call_target="tpu_custom_call" | custom-call | flops 1 | bytes 1 | tf_op jit(solution)/shard_map/pallas_call | solution.py:556
  379.5 6.1 %collective-permute-done.69 = bf16[1,2,48,1536]{3,2,1,0:T(8,128)(2,1)S(1)} collective-permute-done((bf16[1,2,48,1536]{3,2,1,0:T(8,128)(2,1)S(1)}, bf16[1,2,48,1536]{3,2,1,0:T(8,128)(2,1)S(1)}, u32[]{:S(2)}, u32[]{:S(2)}) %collective-permute-start.69) | collective-permute-done | bytes 294944 | tf_op jit(solution)/shard_map/ppermute | solution.py:61
  394.3 7.5 %collective-permute-done.72.refs_5_ = bf16[1,384,768]{2,1,0:T(8,128)(2,1)S(1)} collective-permute-done((bf16[1,384,768]{2,1,0:T(8,128)(2,1)S(1)}, bf16[1,384,768]{2,1,0:T(8,128)(2,1)S(1)}, u32[]{:S(2)}, u32[]{:S(2)}) %collective-permute-start.72) | collective-permute-done | bytes 589856 | tf_op jit(solution)/shard_map/ppermute | solution.py:47
  401.8 4.3 collective-permute-done.73.refs_6_
  406.0 7.3 %collective-permute-done.74.refs_7_ = bf16[1,384,768]{2,1,0:T(8,128)(2,1)S(1)} collective-permute-done((bf16[1,384,768]{2,1,0:T(8,128)(2,1)S(1)}, bf16[1,384,768]{2,1,0:T(8,128)(2,1)S(1)}, u32[]{:S(2)}, u32[]{:S(2)}) %collective-permute-start.74) | collective-permute-done | bytes 589856 | tf_op jit(solution)/shard_map/ppermute | solution.py:47
  417.8 4.3 collective-permute-start.79
  427.1 4.8 %shard_map.418 = (f32[768,1536]{1,0:T(8,128)}, f32[1536,768]{1,0:T(8,128)}) custom-call(s32[2]{0:T(128)S(1)} %pad_add_fusion.where._, bf16[1,768,384]{2,1,0:T(8,128)(2,1)S(1)} %copy-done.50, bf16[1,384,768]{2,1,0:T(8,128)(2,1)S(1)} %copy-done.52, bf16[1,768,384]{2,1,0:T(8,128)(2,1)S(1)} %copy-done.54, bf16[1,384,768]{2,1,0:T(8,128)(2,1)S(1)} %copy-done.56, ...), custom_call_target="tpu_custom_call" | custom-call | flops 1 | bytes 1 | tf_op jit(solution)/shard_map/pallas_call | solution.py:69
  (507 shorter events, 200.9 us)
Async XLA Ops:
  28.1 18.0 %collective-permute-start.10 = (bf16[2,48,1536]{2,1,0:T(8,128)(2,1)}, bf16[2,48,1536]{2,1,0:T(8,128)(2,1)S(1)}, u32[]{:S(2)}, u32[]{:S(2)}) collective-permute-start(bf16[2,48,1536]{2,1,0:T(8,128)(2,1)} %pad_maximum_fusion.5), channel_id=1, source_target_pairs={{0,6},{2,0},{4,2},{6,4},{1,7},{3,1},{5,3},{7,5},{8,14},{10,8},{12,... | collective-permute-start | bytes 884744 | tf_op jit(solution)/shard_map/ppermute | solution.py:61
  29.5 27.9 %collective-permute-start.9 = (bf16[2,48,1536]{2,1,0:T(8,128)(2,1)}, bf16[2,48,1536]{2,1,0:T(8,128)(2,1)S(1)}, u32[]{:S(2)}, u32[]{:S(2)}) collective-permute-start(bf16[2,48,1536]{2,1,0:T(8,128)(2,1)} %pad_maximum_fusion.5), channel_id=1, source_target_pairs={{0,4},{2,6},{4,0},{6,2},{1,5},{3,7},{5,1},{7,3},{8,12},{10,14},{12... | collective-permute-start | bytes 884744 | tf_op jit(solution)/shard_map/ppermute | solution.py:61
  30.9 26.5 %collective-permute-start.8 = (bf16[2,48,1536]{2,1,0:T(8,128)(2,1)}, bf16[2,48,1536]{2,1,0:T(8,128)(2,1)S(1)}, u32[]{:S(2)}, u32[]{:S(2)}) collective-permute-start(bf16[2,48,1536]{2,1,0:T(8,128)(2,1)} %pad_maximum_fusion.5), channel_id=1, source_target_pairs={{0,2},{2,4},{4,6},{6,0},{1,3},{3,5},{5,7},{7,1},{8,10},{10,12},{12... | collective-permute-start | bytes 884744 | tf_op jit(solution)/shard_map/ppermute | solution.py:61
  39.5 17.9 %collective-permute-start.6 = (bf16[3,48,768]{2,1,0:T(8,128)(2,1)S(1)}, bf16[3,48,768]{2,1,0:T(8,128)(2,1)S(1)}, u32[]{:S(2)}, u32[]{:S(2)}) collective-permute-start(bf16[3,48,768]{2,1,0:T(8,128)(2,1)S(1)} %slice_bitcast_fusion.7), channel_id=1, source_target_pairs={{0,16},{8,24},{16,0},{24,8},{1,17},{9,25},{17,1},{25,9},{2,18},{10... | collective-permute-start | bytes 663560 | tf_op jit(solution)/shard_map/ppermute | solution.py:47
  40.1 17.3 %collective-permute-start.7 = (bf16[3,48,768]{2,1,0:T(8,128)(2,1)S(1)}, bf16[3,48,768]{2,1,0:T(8,128)(2,1)S(1)}, u32[]{:S(2)}, u32[]{:S(2)}) collective-permute-start(bf16[3,48,768]{2,1,0:T(8,128)(2,1)S(1)} %slice_bitcast_fusion.6), channel_id=1, source_target_pairs={{0,8},{8,0},{16,24},{24,16},{1,9},{9,1},{17,25},{25,17},{2,10},{10... | collective-permute-start | bytes 663560 | tf_op jit(solution)/shard_map/ppermute | solution.py:47
  57.5 21.3 %collective-permute-start.13 = (bf16[3,2,48,1536]{3,2,0,1:T(8,128)(2,1)S(1)}, bf16[3,2,48,1536]{3,2,0,1:T(8,128)(2,1)S(1)}, u32[]{:S(2)}, u32[]{:S(2)}) collective-permute-start(bf16[3,2,48,1536]{3,2,0,1:T(8,128)(2,1)S(1)} %pad_maximum_fusion), channel_id=1, source_target_pairs={{0,16},{8,24},{16,0},{24,8},{1,17},{9,25},{17,1},{25,9},{2,18},{10... | collective-permute-start | bytes 2654216 | tf_op jit(solution)/shard_map/ppermute | solution.py:47
  58.1 20.9 %collective-permute-start.12 = (bf16[3,2,48,1536]{3,2,0,1:T(8,128)(2,1)S(1)}, bf16[3,2,48,1536]{3,2,0,1:T(8,128)(2,1)S(1)}, u32[]{:S(2)}, u32[]{:S(2)}) collective-permute-start(bf16[3,2,48,1536]{3,2,0,1:T(8,128)(2,1)S(1)} %pad_maximum_fusion), channel_id=1, source_target_pairs={{0,8},{8,0},{16,24},{24,16},{1,9},{9,1},{17,25},{25,17},{2,10},{10... | collective-permute-start | bytes 2654216 | tf_op jit(solution)/shard_map/ppermute | solution.py:47
  110.9 22.8 %collective-permute-start.26 = (bf16[128,768]{1,0:T(8,128)(2,1)S(1)}, bf16[128,768]{1,0:T(8,128)(2,1)S(1)}, u32[]{:S(2)}, u32[]{:S(2)}) collective-permute-start(bf16[128,768]{1,0:T(8,128)(2,1)S(1)} %get-tuple-element.596), channel_id=1, source_target_pairs={{0,6},{2,0},{4,2},{6,4},{1,7},{3,1},{5,3},{7,5},{8,14},{10,8},{12,... | collective-permute-start | bytes 589832 | tf_op jit(solution)/shard_map/ppermute | solution.py:61
  110.9 23.5 %collective-permute-start.25 = (bf16[128,768]{1,0:T(8,128)(2,1)S(1)}, bf16[128,768]{1,0:T(8,128)(2,1)S(1)}, u32[]{:S(2)}, u32[]{:S(2)}) collective-permute-start(bf16[128,768]{1,0:T(8,128)(2,1)S(1)} %get-tuple-element.597), channel_id=1, source_target_pairs={{0,4},{2,6},{4,0},{6,2},{1,5},{3,7},{5,1},{7,3},{8,12},{10,14},{12... | collective-permute-start | bytes 589832 | tf_op jit(solution)/shard_map/ppermute | solution.py:61
  115.8 19.3 %collective-permute-start.24 = (bf16[128,768]{1,0:T(8,128)(2,1)S(1)}, bf16[128,768]{1,0:T(8,128)(2,1)S(1)}, u32[]{:S(2)}, u32[]{:S(2)}) collective-permute-start(bf16[128,768]{1,0:T(8,128)(2,1)S(1)} %get-tuple-element.598), channel_id=1, source_target_pairs={{0,2},{2,4},{4,6},{6,0},{1,3},{3,5},{5,7},{7,1},{8,10},{10,12},{12... | collective-permute-start | bytes 589832 | tf_op jit(solution)/shard_map/ppermute | solution.py:61
  143.7 18.1 %collective-permute-start.31 = (bf16[512,768]{1,0:T(8,128)(2,1)S(1)}, bf16[512,768]{1,0:T(8,128)(2,1)S(1)}, u32[]{:S(2)}, u32[]{:S(2)}) collective-permute-start(bf16[512,768]{1,0:T(8,128)(2,1)S(1)} %shard_map.391.own_grad.grad_ref), channel_id=1, source_target_pairs={{0,1},{1,0},{2,3},{3,2},{4,5},{5,4},{6,7},{7,6},{8,9},{9,8},{10,11... | collective-permute-start | bytes 2359304 | tf_op jit(solution)/shard_map/ppermute | solution.py:47
  188.3 32.1 %collective-permute-start.39 = (bf16[2,768,384]{2,1,0:T(8,128)(2,1)S(1)}, bf16[2,768,384]{2,1,0:T(8,128)(2,1)S(1)}, u32[]{:S(2)}, u32[]{:S(2)}) collective-permute-start(bf16[2,768,384]{2,1,0:T(8,128)(2,1)S(1)} %get-tuple-element.389), channel_id=1, source_target_pairs={{0,8},{8,0},{16,24},{24,16},{1,9},{9,1},{17,25},{25,17},{2,10},{10... | collective-permute-start | bytes 3538952 | tf_op jit(solution)/shard_map/ppermute | solution.py:47
  188.9 31.6 %collective-permute-start.40 = (bf16[2,384,768]{2,1,0:T(8,128)(2,1)S(1)}, bf16[2,384,768]{2,1,0:T(8,128)(2,1)S(1)}, u32[]{:S(2)}, u32[]{:S(2)}) collective-permute-start(bf16[2,384,768]{2,1,0:T(8,128)(2,1)S(1)} %get-tuple-element.390), channel_id=1, source_target_pairs={{0,16},{8,24},{16,0},{24,8},{1,17},{9,25},{17,1},{25,9},{2,18},{10... | collective-permute-start | bytes 3538952 | tf_op jit(solution)/shard_map/ppermute | solution.py:47
  196.6 18.8 %collective-permute-start.36 = (bf16[128,768]{1,0:T(8,128)(2,1)S(1)}, bf16[128,768]{1,0:T(8,128)(2,1)S(1)}, u32[]{:S(2)}, u32[]{:S(2)}) collective-permute-start(bf16[128,768]{1,0:T(8,128)(2,1)S(1)} %get-tuple-element.386), channel_id=1, source_target_pairs={{0,4},{2,6},{4,0},{6,2},{1,5},{3,7},{5,1},{7,3},{8,12},{10,14},{12... | collective-permute-start | bytes 589832 | tf_op jit(solution)/shard_map/ppermute | solution.py:61
  221.7 21.1 %collective-permute-start.44 = (bf16[1,768,384]{2,1,0:T(8,128)(2,1)S(1)}, bf16[1,768,384]{2,1,0:T(8,128)(2,1)S(1)}, u32[]{:S(2)}, u32[]{:S(2)}) collective-permute-start(bf16[1,768,384]{2,1,0:T(8,128)(2,1)S(1)} %get-tuple-element.409), channel_id=1, source_target_pairs={{0,16},{8,24},{16,0},{24,8},{1,17},{9,25},{17,1},{25,9},{2,18},{10... | collective-permute-start | bytes 1769480 | tf_op jit(solution)/shard_map/ppermute | solution.py:47
  222.3 20.4 %collective-permute-start.45 = (bf16[1,384,768]{2,1,0:T(8,128)(2,1)S(1)}, bf16[1,384,768]{2,1,0:T(8,128)(2,1)S(1)}, u32[]{:S(2)}, u32[]{:S(2)}) collective-permute-start(bf16[1,384,768]{2,1,0:T(8,128)(2,1)S(1)} %get-tuple-element.410), channel_id=1, source_target_pairs={{0,8},{8,0},{16,24},{24,16},{1,9},{9,1},{17,25},{25,17},{2,10},{10... | collective-permute-start | bytes 1769480 | tf_op jit(solution)/shard_map/ppermute | solution.py:47
  225.1 17.7 %collective-permute-start.42 = (bf16[128,768]{1,0:T(8,128)(2,1)S(1)}, bf16[128,768]{1,0:T(8,128)(2,1)S(1)}, u32[]{:S(2)}, u32[]{:S(2)}) collective-permute-start(bf16[128,768]{1,0:T(8,128)(2,1)S(1)} %get-tuple-element.402), channel_id=1, source_target_pairs={{0,4},{2,6},{4,0},{6,2},{1,5},{3,7},{5,1},{7,3},{8,12},{10,14},{12... | collective-permute-start | bytes 589832 | tf_op jit(solution)/shard_map/ppermute | solution.py:61
  288.9 35.9 %collective-permute-start.53 = (bf16[512,768]{1,0:T(8,128)(2,1)S(1)}, bf16[512,768]{1,0:T(8,128)(2,1)S(1)}, u32[]{:S(2)}, u32[]{:S(2)}) collective-permute-start(bf16[512,768]{1,0:T(8,128)(2,1)S(1)} %get-tuple-element.474.own_ref), channel_id=1, source_target_pairs={{0,1},{1,0},{2,3},{3,2},{4,5},{5,4},{6,7},{7,6},{8,9},{9,8},{10,11... | collective-permute-start | bytes 2359304 | tf_op jit(solution)/shard_map/ppermute | solution.py:47
  289.0 41.0 %collective-permute-start.56 = (bf16[4,2,48,1536]{3,2,1,0:T(8,128)(2,1)S(1)}, bf16[4,2,48,1536]{3,2,1,0:T(8,128)(2,1)S(1)}, u32[]{:S(2)}, u32[]{:S(2)}) collective-permute-start(bf16[4,2,48,1536]{3,2,1,0:T(8,128)(2,1)S(1)} %get-tuple-element.478), channel_id=1, source_target_pairs={{0,8},{8,0},{16,24},{24,16},{1,9},{9,1},{17,25},{25,17},{2,10},{10... | collective-permute-start | bytes 3538952 | tf_op jit(solution)/shard_map/ppermute | solution.py:47
  290.5 39.5 %collective-permute-start.57 = (bf16[4,2,48,1536]{3,2,1,0:T(8,128)(2,1)S(1)}, bf16[4,2,48,1536]{3,2,1,0:T(8,128)(2,1)S(1)}, u32[]{:S(2)}, u32[]{:S(2)}) collective-permute-start(bf16[4,2,48,1536]{3,2,1,0:T(8,128)(2,1)S(1)} %get-tuple-element.479), channel_id=1, source_target_pairs={{0,16},{8,24},{16,0},{24,8},{1,17},{9,25},{17,1},{25,9},{2,18},{10... | collective-permute-start | bytes 3538952 | tf_op jit(solution)/shard_map/ppermute | solution.py:47
  291.9 32.9 %collective-permute-start.54 = (bf16[4,48,768]{2,1,0:T(8,128)(2,1)S(1)}, bf16[4,48,768]{2,1,0:T(8,128)(2,1)S(1)}, u32[]{:S(2)}, u32[]{:S(2)}) collective-permute-start(bf16[4,48,768]{2,1,0:T(8,128)(2,1)S(1)} %get-tuple-element.472), channel_id=1, source_target_pairs={{0,16},{8,24},{16,0},{24,8},{1,17},{9,25},{17,1},{25,9},{2,18},{10... | collective-permute-start | bytes 884744 | tf_op jit(solution)/shard_map/ppermute | solution.py:47
  292.5 32.3 %collective-permute-start.55 = (bf16[4,48,768]{2,1,0:T(8,128)(2,1)S(1)}, bf16[4,48,768]{2,1,0:T(8,128)(2,1)S(1)}, u32[]{:S(2)}, u32[]{:S(2)}) collective-permute-start(bf16[4,48,768]{2,1,0:T(8,128)(2,1)S(1)} %get-tuple-element.473), channel_id=1, source_target_pairs={{0,8},{8,0},{16,24},{24,16},{1,9},{9,1},{17,25},{25,17},{2,10},{10... | collective-permute-start | bytes 884744 | tf_op jit(solution)/shard_map/ppermute | solution.py:47
  340.5 17.2 %collective-permute-start.60 = (bf16[4,48,1536]{2,1,0:T(8,128)(2,1)S(1)}, bf16[4,48,1536]{2,1,0:T(8,128)(2,1)S(1)}, u32[]{:S(2)}, u32[]{:S(2)}) collective-permute-start(bf16[4,48,1536]{2,1,0:T(8,128)(2,1)S(1)} %get-tuple-element.511), channel_id=1, source_target_pairs={{0,16},{8,24},{16,0},{24,8},{1,17},{9,25},{17,1},{25,9},{2,18},{10... | collective-permute-start | bytes 1769480 | tf_op jit(solution)/shard_map/ppermute | solution.py:47
  358.4 18.7 %collective-permute-start.65 = (bf16[4,48,768]{2,1,0:T(8,128)(2,1)}, bf16[4,48,768]{2,1,0:T(8,128)(2,1)}, u32[]{:S(2)}, u32[]{:S(2)}) collective-permute-start(bf16[4,48,768]{2,1,0:T(8,128)(2,1)} %get-tuple-element.530), channel_id=1, source_target_pairs={{0,16},{8,24},{16,0},{24,8},{1,17},{9,25},{17,1},{25,9},{2,18},{10... | collective-permute-start | bytes 884744 | tf_op jit(solution)/shard_map/ppermute | solution.py:47
  359.8 17.4 %collective-permute-start.66 = (bf16[4,48,768]{2,1,0:T(8,128)(2,1)}, bf16[4,48,768]{2,1,0:T(8,128)(2,1)}, u32[]{:S(2)}, u32[]{:S(2)}) collective-permute-start(bf16[4,48,768]{2,1,0:T(8,128)(2,1)} %get-tuple-element.531), channel_id=1, source_target_pairs={{0,8},{8,0},{16,24},{24,16},{1,9},{9,1},{17,25},{25,17},{2,10},{10... | collective-permute-start | bytes 884744 | tf_op jit(solution)/shard_map/ppermute | solution.py:47
  365.8 19.8 %collective-permute-start.69 = (bf16[1,2,48,1536]{3,2,1,0:T(8,128)(2,1)S(1)}, bf16[1,2,48,1536]{3,2,1,0:T(8,128)(2,1)S(1)}, u32[]{:S(2)}, u32[]{:S(2)}) collective-permute-start(bf16[1,2,48,1536]{3,2,1,0:T(8,128)(2,1)S(1)} %get-tuple-element.545), channel_id=1, source_target_pairs={{0,4},{2,6},{4,0},{6,2},{1,5},{3,7},{5,1},{7,3},{8,12},{10,14},{12... | collective-permute-start | bytes 884744 | tf_op jit(solution)/shard_map/ppermute | solution.py:61
  367.1 19.1 %collective-permute-start.70 = (bf16[1,2,48,1536]{3,2,1,0:T(8,128)(2,1)S(1)}, bf16[1,2,48,1536]{3,2,1,0:T(8,128)(2,1)S(1)}, u32[]{:S(2)}, u32[]{:S(2)}) collective-permute-start(bf16[1,2,48,1536]{3,2,1,0:T(8,128)(2,1)S(1)} %get-tuple-element.546), channel_id=1, source_target_pairs={{0,6},{2,0},{4,2},{6,4},{1,7},{3,1},{5,3},{7,5},{8,14},{10,8},{12,... | collective-permute-start | bytes 884744 | tf_op jit(solution)/shard_map/ppermute | solution.py:61
  377.2 40.6 %collective-permute-start.46 = (bf16[512,768]{1,0:T(8,128)(2,1)S(1)}, bf16[512,768]{1,0:T(8,128)(2,1)S(1)}, u32[]{:S(2)}, u32[]{:S(2)}) collective-permute-start(bf16[512,768]{1,0:T(8,128)(2,1)S(1)} %shard_map.400), channel_id=1, source_target_pairs={{0,1},{1,0},{2,3},{3,2},{4,5},{5,4},{6,7},{7,6},{8,9},{9,8},{10,11... | collective-permute-start | bytes 2359304 | tf_op jit(solution)/shard_map/ppermute | solution.py:47
  386.1 19.9 %collective-permute-start.73 = (bf16[1,768,384]{2,1,0:T(8,128)(2,1)S(1)}, bf16[1,768,384]{2,1,0:T(8,128)(2,1)S(1)}, u32[]{:S(2)}, u32[]{:S(2)}) collective-permute-start(bf16[1,768,384]{2,1,0:T(8,128)(2,1)S(1)} %copy-done.54), channel_id=1, source_target_pairs={{0,8},{8,0},{16,24},{24,16},{1,9},{9,1},{17,25},{25,17},{2,10},{10... | collective-permute-start | bytes 1769480 | tf_op jit(solution)/shard_map/ppermute | solution.py:47
  387.5 25.9 %collective-permute-start.74 = (bf16[1,384,768]{2,1,0:T(8,128)(2,1)S(1)}, bf16[1,384,768]{2,1,0:T(8,128)(2,1)S(1)}, u32[]{:S(2)}, u32[]{:S(2)}) collective-permute-start(bf16[1,384,768]{2,1,0:T(8,128)(2,1)S(1)} %copy-done.56), channel_id=1, source_target_pairs={{0,16},{8,24},{16,0},{24,8},{1,17},{9,25},{17,1},{25,9},{2,18},{10... | collective-permute-start | bytes 1769480 | tf_op jit(solution)/shard_map/ppermute | solution.py:47
  413.4 20.5 %collective-permute-start.76 = (bf16[1,2,48,1536]{3,2,1,0:T(8,128)(2,1)S(1)}, bf16[1,2,48,1536]{3,2,1,0:T(8,128)(2,1)S(1)}, u32[]{:S(2)}, u32[]{:S(2)}) collective-permute-start(bf16[1,2,48,1536]{3,2,1,0:T(8,128)(2,1)S(1)} %add_convert_fusion.own), channel_id=1, source_target_pairs={{0,16},{8,24},{16,0},{24,8},{1,17},{9,25},{17,1},{25,9},{2,18},{10... | collective-permute-start | bytes 884744 | tf_op jit(solution)/shard_map/ppermute | solution.py:47
  413.9 20.0 %collective-permute-start.75 = (bf16[1,2,48,1536]{3,2,1,0:T(8,128)(2,1)S(1)}, bf16[1,2,48,1536]{3,2,1,0:T(8,128)(2,1)S(1)}, u32[]{:S(2)}, u32[]{:S(2)}) collective-permute-start(bf16[1,2,48,1536]{3,2,1,0:T(8,128)(2,1)S(1)} %add_convert_fusion.own), channel_id=1, source_target_pairs={{0,8},{8,0},{16,24},{24,16},{1,9},{9,1},{17,25},{25,17},{2,10},{10... | collective-permute-start | bytes 884744 | tf_op jit(solution)/shard_map/ppermute | solution.py:47
  (174 other events, 1677.8 us)

commit v2 on v1

--- a/solution.py
+++ b/solution.py
@@ -85,7 +85,7 @@
 
 
 def plane_second(from_x, from_y):
-    return flip(from_x[:, 0], "dp", 1), flip(from_y[:, 1], "dp", 0)
+    return flip(from_x[0], "dp", 1), flip(from_y[1], "dp", 0)
 
 
 def quarter_of(left, right):
@@ -99,7 +99,7 @@
 
 
 def z_spread(piece):
-    return jnp.stack(z_parts(piece))
+    return jnp.stack(z_parts(piece), axis=1)
 
 
 def assemble(left, right, pieces):
@@ -116,7 +116,7 @@
                 for key, ref in ((0, own), (1, from_x), (2, from_y), (3, diag)):
                     row = pl.multiple_of(base + (place ^ key) * quarter, 16)
                     outs[side][pl.ds(row, quarter), :] = (
-                        ref[step - 1] if key == 3 else ref[step - 1, side]
+                        ref[step - 1] if key == 3 else ref[side, step - 1]
                     )
 
     full = ((count * rows, cols), left.dtype)
@@ -166,31 +166,34 @@
     return kernel_call(body, shapes, place_scalars(), far_sum(*parts))
 
 
-def plane_first_e(held, got):
-    return (
-        (flip(held[0], "dp", 0), flip(held[1], "dp", 1)),
-        (flip(got[0], "dp", 0), flip(got[1], "dp", 1)),
-    )
-
-
-def expert_last(held, got, diagonal):
+def last_trip_e(held, got):
+    both_a, both_b = (jnp.concatenate(pair, axis=0) for pair in zip(held, got))
+    return flip(both_a, "dp", 0), flip(both_b, "dp", 1)
+
+
+def expert_last(held, got, far):
     def body(where, *refs):
         place = where[1]
         for side in range(2):
-            own, near, far_near, far_diag = (refs[side + 2 * number] for number in range(4))
+            own, near, both = (refs[side + 2 * number] for number in range(3))
             rows, cols = own.shape[1:]
             first = 2 if side == 0 else 1
-            for key, ref in ((0, own), (first, near), (3 - first, far_near), (3, far_diag)):
+            for key, value in (
+                (0, own[0]),
+                (first, near[0]),
+                (3 - first, both[0]),
+                (3, both[1]),
+            ):
                 if side == 0:
                     at = pl.multiple_of((place ^ key) * cols, 128)
-                    refs[8][:, pl.ds(at, cols)] = ref[0].astype(F32)
+                    refs[6][:, pl.ds(at, cols)] = value.astype(F32)
                 else:
                     at = pl.multiple_of((place ^ key) * rows, 16)
-                    refs[9][pl.ds(at, rows), :] = ref[0].astype(F32)
+                    refs[7][pl.ds(at, rows), :] = value.astype(F32)
 
     (_, model, quarter), _ = (part.shape for part in held)
     shapes = [((model, 4 * quarter), F32), ((4 * quarter, model), F32)]
-    return kernel_call(body, shapes, place_scalars(), (*held, *got, *diagonal[0], *diagonal[1]))
+    return kernel_call(body, shapes, place_scalars(), (*held, *got, *far))
 
 
 def reduce_third(*parts):
@@ -199,13 +202,42 @@
     def body(where, keep_a, keep_b, got_a, got_b, *outs):
         for step, out in enumerate(outs):
             block = lax.rem(where[0] + step, blocks)
-            out[0, 0] = add_low(keep_a[block], got_a[block])
-            out[0, 1] = add_low(keep_b[block], got_b[block])
+            out[0] = add_low(keep_a[block], got_a[block])
+            out[1] = add_low(keep_b[block], got_b[block])
 
     own, *sends = kernel_call(
-        body, [((1, 2, rows, cols), BF16)] * blocks, place_scalars(), far_sum(*parts)
+        body, [((2, rows, cols), BF16)] * blocks, place_scalars(), far_sum(*parts)
     )
     return own, sends
+
+
+def reduce_halves(*parts):
+    blocks, rows, cols = parts[0].shape
+    half = blocks // 2
+
+    def body(where, keep_a, keep_b, got_a, got_b, send, keep):
+        upper = where[0] // half
+        for k in range(half):
+            for out, base in ((send, (1 - upper) * half), (keep, upper * half)):
+                out[k, 0] = add_low(keep_a[base + k], got_a[base + k])
+                out[k, 1] = add_low(keep_b[base + k], got_b[base + k])
+
+    return kernel_call(
+        body, [((half, 2, rows, cols), BF16)] * 2, place_scalars(), far_sum(*parts)
+    )
+
+
+def reduce_last_half(keep, got):
+    half = keep.shape[0]
+
+    def body(where, keep, got, send, own):
+        odd = lax.rem(where[0], half)
+        send[...] = add_low(keep[1 - odd], got[1 - odd])
+        own[...] = add_low(keep[odd], got[odd])
+
+    return kernel_call(
+        body, [(keep.shape[1:], BF16)] * 2, place_scalars(), (keep, got)
+    )
 
 
 def z_trip(sends):
@@ -219,20 +251,25 @@
     return total.astype(BF16)
 
 
-def reduce_last(held, near, diagonal):
-    _, _, rows, cols = held.shape
-
-    def body(where, own, from_x, from_y, diag_a, diag_b, out_a, out_b):
+def reduce_last(held, near, diagonal, widths):
+    _, rows, _ = held.shape
+
+    def body(where, own, from_x, from_y, diag_a, diag_b, *outs):
         place = where[1]
-        for side, (out, diag) in enumerate(((out_a, diag_a), (out_b, diag_b))):
-            for key, ref in ((0, own), (1, from_x), (2, from_y), (3, diag)):
-                row = pl.multiple_of((place ^ key) * rows, 8)
-                value = ref[0] if key == 3 else ref[0, side]
-                out[pl.ds(row, rows), :] = value.astype(F32)
-
-    return kernel_call(
-        body, [((4 * rows, cols), F32)] * 2, place_scalars(), (held, *near, *diagonal)
-    )
+        start = 0
+        for number, width in enumerate(widths):
+            cols = slice(start, start + width)
+            for side, diag in enumerate((diag_a, diag_b)):
+                out = outs[2 * number + side]
+                for key, ref in ((0, own), (1, from_x), (2, from_y), (3, diag)):
+                    row = pl.multiple_of((place ^ key) * rows, 8)
+                    value = ref[:, cols] if key == 3 else ref[side, :, cols]
+                    out[pl.ds(row, rows), :] = value.astype(F32)
+            start += width
+
+    shapes = [((4 * rows, width), F32) for width in widths for _ in range(2)]
+    outs = kernel_call(body, shapes, place_scalars(), (held, *near, *diagonal))
+    return [outs[2 * i : 2 * i + 2] for i in range(len(widths))]
 
 
 def pack_small(gains, router, tables):
@@ -267,7 +304,9 @@
     return pl.BlockSpec(memory_space=pltpu.VMEM)
 
 
-PARAMS = pltpu.CompilerParams(vmem_limit_bytes=28 << 20)
+PARAMS = pltpu.CompilerParams(vmem_limit_bytes=16 << 20)
+MIDDLE = pltpu.CompilerParams(vmem_limit_bytes=20 << 20)
+LARGE = pltpu.CompilerParams(vmem_limit_bytes=30 << 20)
 
 
 def build_bias(buckets, tables, token):
@@ -302,8 +341,12 @@
     return jnp.where(mask, value, jnp.zeros_like(value))
 
 
-def both(own, got):
-    return own[...].astype(F32) + got[...].astype(F32)
+def both(first, second):
+    if len(first.shape) == 2:
+        return first[...].astype(F32) + second[...].astype(F32)
+    return jnp.concatenate(
+        [part[0].astype(F32) + part[1].astype(F32) for part in (first, second)], axis=0
+    )
 
 
 def stream_sum(base, partials):
@@ -325,7 +368,8 @@
     def body(*refs):
         base_ref, part_refs = refs[0], refs[1 : 1 + count]
         gain_ref, wa_ref, wb_ref, bias_ref = refs[1 + count : 5 + count]
-        stream_ref, normed_ref, joint_ref, prob_ref, mixed_ref, partial_ref = refs[5 + count :]
+        stream_out, normed_out, joint_out, prob_ref, mixed_ref, partial_ref = refs[5 + count : -3]
+        stream_ref, normed_ref, joint_ref = refs[-3:]
         step = pl.program_id(0)
 
         @pl.when(step == 0)
@@ -341,6 +385,9 @@
 
         masks = lane_masks(head_width)
         rows = pl.ds(pl.multiple_of(step * chunk, chunk), chunk)
+        stream_out[...] = stream_ref[rows, :]
+        normed_out[...] = normed_ref[rows, :]
+        joint_out[...] = joint_ref[rows, :]
         for pair in range(heads // 2):
             cols = slice(pair * 2 * head_width, (pair + 1) * 2 * head_width)
             query = joint_ref[rows, cols]
@@ -360,23 +407,32 @@
         partial_ref[...] = dot_nt(mixed_ref[...], wb_ref[:, width:]).astype(BF16)
 
     full = (seq_len, model)
-    shapes = [
-        (full, F32, whole(full)),
-        (full, BF16, whole(full)),
-        ((seq_len, 3 * width), BF16, whole((seq_len, 3 * width))),
-        ((heads, seq_len, seq_len), BF16, pl.BlockSpec((heads, chunk, seq_len), lambda i: (0, i, 0))),
-        ((seq_len, width), BF16, pl.BlockSpec((chunk, width), lambda i: (i, 0))),
-        (full, BF16, pl.BlockSpec((chunk, model), lambda i: (i, 0))),
+    def by_rows(cols):
+        return pl.BlockSpec((chunk, cols), lambda i: (i, 0))
+
+    heads_of = pl.BlockSpec((heads, chunk, seq_len), lambda i: (0, i, 0))
+    kept = [
+        (full, F32, by_rows(model)),
+        (full, BF16, by_rows(model)),
+        ((seq_len, 3 * width), BF16, by_rows(3 * width)),
+        ((heads, seq_len, seq_len), BF16, heads_of),
+        ((seq_len, width), BF16, by_rows(width)),
     ]
     return pl.pallas_call(
         body,
-        out_shape=[jax.ShapeDtypeStruct(shape, dtype) for shape, dtype, _ in shapes],
+        out_shape=[pltpu.HBM(shape, dtype) for shape, dtype, _ in kept]
+        + [jax.ShapeDtypeStruct(full, BF16)],
         grid=(seq_len // chunk,),
         in_specs=[whole(full)]
         + [whole(full)] * count
         + [whole((1, model)), whole(weights[0].shape), whole(weights[1].shape)]
-        + [pl.BlockSpec((heads, chunk, seq_len), lambda i: (0, i, 0))],
-        out_specs=[spec for _, _, spec in shapes],
+        + [heads_of],
+        out_specs=[spec for _, _, spec in kept] + [by_rows(model)],
+        scratch_shapes=[
+            pltpu.VMEM(full, F32),
+            pltpu.VMEM(full, BF16),
+            pltpu.VMEM((seq_len, 3 * width), BF16),
+        ],
         compiler_params=PARAMS,
         cost_estimate=COST,
     )(base, *partials, gain[None], *weights, bias)
@@ -444,7 +500,7 @@
         body,
         out_shape=[
             jax.ShapeDtypeStruct((seq_len, 3 * width), BF16),
-            jax.ShapeDtypeStruct(prob.shape, BF16),
+            pltpu.HBM(prob.shape, BF16),
             jax.ShapeDtypeStruct(full, BF16),
         ],
         grid=(steps,),
@@ -599,8 +655,8 @@
         out_shape=[
             jax.ShapeDtypeStruct(full, F32),
             jax.ShapeDtypeStruct(full, BF16),
-            jax.ShapeDtypeStruct((seq_len, hidden_width), BF16),
-            jax.ShapeDtypeStruct((seq_len, hidden_width), BF16),
+            pltpu.HBM((seq_len, hidden_width), BF16),
+            pltpu.HBM((seq_len, hidden_width), BF16),
             jax.ShapeDtypeStruct(full, BF16),
         ],
         grid=(steps,),
@@ -767,8 +823,8 @@
     return pl.pallas_call(
         body,
         out_shape=[
-            jax.ShapeDtypeStruct((total, hidden_width), BF16),
-            jax.ShapeDtypeStruct((total, hidden_width), BF16),
+            pltpu.HBM((total, hidden_width), BF16),
+            pltpu.HBM((total, hidden_width), BF16),
             jax.ShapeDtypeStruct((total, model), BF16),
             jax.ShapeDtypeStruct(part, F32),
             jax.ShapeDtypeStruct(part, BF16),
@@ -785,7 +841,7 @@
         ],
         out_specs=[act, act, whole((total, model))] + [whole(part)] * 4,
         scratch_shapes=[pltpu.VMEM((total, model), F32)] * 2 + [pltpu.VMEM((total, model), BF16)],
-        compiler_params=PARAMS,
+        compiler_params=LARGE,
         cost_estimate=COST,
     )(place_scalars(), *rows, *grads, router, w_in, w_out)
 
@@ -875,9 +931,15 @@
             ],
             scratch_shapes=[pltpu.VMEM((2 * half, model), BF16)],
         ),
-        compiler_params=PARAMS,
+        compiler_params=MIDDLE,
         cost_estimate=COST,
-    )(place_scalars(), *rows, hidden, dpre, grads)
+    )(
+        place_scalars(),
+        *rows,
+        pltpu.with_memory_space_constraint(hidden, pltpu.HBM),
+        pltpu.with_memory_space_constraint(dpre, pltpu.HBM),
+        grads,
+    )
 
 
 def receive_slots(grad, rows, gain, spots, halves):
@@ -959,9 +1021,6 @@
     )
     far_one = z_spread(quarter_of(*shards[0]))
 
-    stream_zero = lax.all_gather(tokens, "mp", axis=0, tiled=True)
-    grad_four = lax.all_gather(cotangent, "mp", axis=0, tiled=True)
-
     def local_bias(table, token):
         return build_bias(
             buckets, lax.dynamic_slice_in_dim(table, mp_index * head_local, head_local, 1).T, token
@@ -996,27 +1055,35 @@
     def swapped(partial):
         return partial, flip(partial, "mp", 0)
 
+    def gathered(partial):
+        rows = partial.shape[0] // 2
+        return tuple(
+            lax.all_gather(part, "mp", axis=0) for part in (partial[:rows], partial[rows:])
+        )
+
+    piece_ff, far_one = meet(quarter_of(*shards[1]), far_one)
     near_one = plane_first(far_one)
-    token = flip(far_one[0, 0, :8, :128], "mp", 0)
-    piece_ff, token = meet(quarter_of(*shards[1]), token)
     got_ff = z_parts(piece_ff)
-    bias_one = local_bias(table_first, token)
-    near_one, bias_one = meet(near_one, bias_one)
+    bias_one = local_bias(table_first, far_one[0, 0, :8, :128])
+    tokens, cotangent, near_one, bias_one = meet(tokens, cotangent, near_one, bias_one)
     diag_one = plane_second(*near_one)
+    stream_zero = lax.all_gather(tokens, "mp", axis=0, tiled=True)
+    grad_four = lax.all_gather(cotangent, "mp", axis=0, tiled=True)
     bias_two = local_bias(table_second, near_one[0][0, 0, :8, :128])
-    diag_one, got_ff, bias_two = meet(diag_one, got_ff, bias_two)
-    far_ff = jnp.stack(got_ff)
+    diag_one, got_ff, bias_two, stream_zero, grad_four, send_spots, back_spots = meet(
+        diag_one, got_ff, bias_two, stream_zero, grad_four, send_spots, back_spots
+    )
+    piece_two, far_ff = meet(quarter_of(*shards[2]), jnp.stack(got_ff, axis=1))
     near_ff = plane_first(far_ff)
+    got_two = z_parts(piece_two)
     weights_one = assemble(*shards[0], (far_one, *near_one, *diag_one))
     _, normed_one, joint_one, prob_one, mixed_one, partial = attention_forward(
         tie(stream_zero, far_ff), (), norm_first, weights_one, bias_one
     )
-    piece_two, partial = meet(quarter_of(*shards[2]), partial)
-    got_two = z_parts(piece_two)
-    pair, near_ff = meet(swapped(partial), near_ff)
+    partial, near_ff, got_two = meet(partial, near_ff, got_two)
     diag_ff = plane_second(*near_ff)
-    diag_ff, pair, got_two = meet(diag_ff, pair, got_two)
-    far_two = jnp.stack(got_two)
+    far_two = jnp.stack(got_two, axis=1)
+    diag_ff, pair, far_two = meet(diag_ff, swapped(partial), far_two)
     near_two = plane_first(far_two)
     to_slots = (jnp.arange(half, dtype=jnp.int32)[:, None] == send_spots).astype(BF16)
     grad_sent = dot_nn(to_slots, tie(grad_four, pair)).astype(BF16)
@@ -1027,7 +1094,7 @@
     )
     near_two, partial = meet(near_two, partial)
     diag_two = plane_second(*near_two)
-    pair, diag_two = meet(swapped(partial), diag_two)
+    diag_two, pair = meet(diag_two, swapped(partial))
     weights_two = assemble(*shards[2], (far_two, *near_two, *diag_two))
     stream_two, normed_two, joint_two, prob_two, mixed_two, partial = attention_forward(
         stream_one, pair, norm_second, weights_two, bias_two
@@ -1035,12 +1102,11 @@
 
     partial, grad_got = meet(partial, grad_got)
 
+    grad_slots, pair = meet(with_other(stacked(grad_got)), swapped(partial))
     stream_three, moe_rows, *sent = send_slots(
-        stream_two, swapped(partial), expert_gain, (send_spots, half), z_count
-    )
-    moe_got = sent_on(sent)
-    grad_slots = with_other(stacked(tie(grad_got, sent)))
-    moe_slots = with_other(stacked(tie(moe_got, grad_slots)))
+        stream_two, pair, expert_gain, (send_spots, half), z_count
+    )
+    moe_slots = with_other(stacked(sent_on(sent)))
     router_rows = router.T
     expert_hidden, expert_dpre, expert_rows, res_own, res_other, back_own, back_other = expert_step(
         moe_slots, grad_slots, router_rows, expert_in[0], expert_out[0]
@@ -1065,103 +1131,109 @@
     )
     grad_low, got_e = meet(grad_low, got_e)
     send_ea, send_eb, *keep_e = reduce_second(*keep_e, got_e[0][None], got_e[1][None])
-    send_ea, send_eb, grad_low, *result_blocks = meet(send_ea, send_eb, grad_low, *returns[z_count:])
+    send_ea, send_eb, grad_low = meet(send_ea, send_eb, grad_low)
     got_e = second_trip(send_ea, send_eb)
-    result_got = sent_back(result_blocks)
-
-    def attention_grads(normed, dj, low, mixed):
-        return weight_grads(
+
+    def attention_grads(kernel, normed, dj, low, mixed):
+        return kernel(
             z_count,
             [(normed, dj, 0, 2 * width)],
             [(normed, dj, 2 * width, 3 * width), (low, mixed, 0, width)],
         )
 
     dj_two, ds_two, partial = attention_backward(grad_low, weights_two, joint_two, prob_two)
-    result_got, partial, dj_two, got_e = meet(result_got, partial, dj_two, got_e)
-    pair = swapped(partial)
+    partial, dj_two, got_e = meet(partial, dj_two, got_e)
     held_e = expert_held(*keep_e, *got_e)
-    held_e, dj_two = meet(held_e, dj_two)
+    held_e, dj_two, partial = meet(held_e, dj_two, partial)
     from_e = (flip(held_e[0], "dp", 1), flip(held_e[1], "dp", 0))
-    halves_two = attention_grads(normed_two, dj_two, grad_low, mixed_two)
-    pair, halves_two = meet(pair, halves_two)
+    halves_two = attention_grads(weight_grads, normed_two, dj_two, grad_low, mixed_two)
+    halves_two, partial = meet(halves_two, partial)
     got_two = first_trip(*halves_two[:2])
     grad_two, grad_low, dpre, partial, grad_norm_second = dense_backward(
-        grad_three, stream_two, norm_second, pair, w_in_full, w_out_full, slope
-    )
-    from_e, partial, dpre = meet(from_e, partial, dpre)
-    pair = swapped(partial)
+        grad_three, stream_two, norm_second, gathered(partial), w_in_full, w_out_full, slope
+    )
     halves_ff = weight_grads(
         z_count, [(normed_ff, dpre, 0, ff_width)], [(grad_low, hidden, 0, ff_width)]
     )
-    pair, halves_ff, got_two = meet(pair, halves_ff, got_two)
+    from_e, halves_ff, partial, got_two, *result_blocks = meet(
+        from_e, halves_ff, partial, got_two, *returns[z_count:]
+    )
     got_ff = first_trip(*halves_ff[:2])
+    result_got = sent_back(result_blocks)
     *send_two, keep_a, keep_b = reduce_second(*halves_two[2:], *got_two)
     keep_two = (keep_a, keep_b)
-    send_two, pair = meet(send_two, pair)
+    grad_one, grad_low, grad_dense_gain = norm_kernel(
+        grad_two, stream_one, dense_gain, gathered(tie(partial, send_two))
+    )
+    dj_one, ds_one, partial = attention_backward(grad_low, weights_one, joint_one, prob_one)
+    dj_one, partial, result_got, send_two = meet(dj_one, partial, result_got, send_two)
     got_two = second_trip(*send_two)
-    grad_one, grad_low, grad_dense_gain = norm_kernel(grad_two, stream_one, dense_gain, pair)
-    dj_one, ds_one, partial = attention_backward(grad_low, weights_one, joint_one, prob_one)
-    pair = swapped(partial)
-    halves_one = attention_grads(normed_one, dj_one, grad_low, mixed_one)
-    pair, halves_one, got_two = meet(pair, halves_one, got_two)
+    result_own = stacked(result_got)
+    halves_one = attention_grads(weight_grads, normed_one, dj_one, grad_low, mixed_one)
+    halves_one, partial = meet(halves_one, partial)
+    grad_zero, _, grad_norm_first = norm_kernel(
+        grad_one, stream_zero, norm_first, gathered(partial)
+    )
+    grad_norm_first, halves_one, got_two = meet(grad_norm_first, halves_one, got_two)
     own_two, send_two = reduce_third(*keep_two, *got_two)
-    send_two, halves_one = meet(send_two, halves_one)
-    got_one = first_trip(*halves_one[:2])
-    grad_zero, _, grad_norm_first = norm_kernel(grad_one, stream_zero, norm_first, pair)
-    grad_norm_first, got_ff, send_two = meet(grad_norm_first, got_ff, send_two)
+    send_two, got_ff, halves_one = meet(send_two, got_ff, halves_one)
     got_two = z_trip(send_two)
     *send_ff, keep_a, keep_b = reduce_second(*halves_ff[2:], *got_ff)
     keep_ff = (keep_a, keep_b)
-    send_ff, ds_two, got_one = meet(send_ff, ds_two, got_one)
+    send_ff, ds_two = meet(send_ff, ds_two)
     got_ff = second_trip(*send_ff)
+    table_two_grad = table_grad(ds_two, buckets, bucket_count)
+    table_two_grad, got_ff, got_two, halves_one = meet(table_two_grad, got_ff, got_two, halves_one)
+    send_ff, keep_ff = reduce_halves(*keep_ff, *got_ff)
+    send_ff, halves_one, ds_one, held_e, from_e = meet(send_ff, halves_one, ds_one, held_e, from_e)
+    got_ff = flip(send_ff, "expert", 1)
+    got_one = first_trip(*halves_one[:2])
+    far_e = last_trip_e(held_e, from_e)
+    table_one_grad = table_grad(ds_one, buckets, bucket_count)
+    table_one_grad, got_one, got_two = meet(table_one_grad, got_one, got_two)
     *send_one, keep_a, keep_b = reduce_second(*halves_one[2:], *got_one)
-    keep_one = (keep_a, keep_b)
-    table_two_grad = table_grad(ds_two, buckets, bucket_count)
-    table_two_grad, got_ff, got_two, send_one = meet(table_two_grad, got_ff, got_two, send_one)
     got_one = second_trip(*send_one)
-    own_ff, send_ff = reduce_third(*keep_ff, *got_ff)
-    send_ff, ds_one = meet(send_ff, ds_one)
-    got_ff = z_trip(send_ff)
     held_two = reduce_fourth(own_two, got_two)
-    table_one_grad = table_grad(ds_one, buckets, bucket_count)
     small = pack_small(
         (grad_norm_first, grad_dense_gain, grad_norm_second, grad_expert_gain),
         grad_router,
         (table_one_grad, table_two_grad),
     )
-    small, got_one, held_two = meet(small, got_one, held_two)
-    own_one, send_one = reduce_third(*keep_one, *got_one)
-    near_e = plane_first_e(held_e, from_e)
+    held_two, got_ff, small = meet(held_two, got_ff, small)
+    send_ff, keep_ff = reduce_last_half(keep_ff, got_ff)
+    got_ff = flip(send_ff, "expert", 0)
+    send_ff, got_one = meet(send_ff, got_one)
+    send_one, keep_one = reduce_halves(keep_a, keep_b, *got_one)
+    send_one, got_ff, held_two, small, far_e = meet(send_one, got_ff, held_two, small, far_e)
+    held = jnp.concatenate([add_low(keep_ff, got_ff), held_two], axis=-1)
+    near = plane_first(held)
+    got_one = flip(send_one, "expert", 1)
     got_small = flip(small, "mp", 0)
-    send_one, got_small, got_ff = meet(send_one, got_small, got_ff)
+    expert_in_sum, expert_out_sum = expert_last(held_e, from_e, far_e)
+    small, got_small, near, got_one, expert_in_sum = meet(
+        small, got_small, near, got_one, expert_in_sum
+    )
     small = small + got_small
-    got_one = z_trip(send_one)
-    held_ff = reduce_fourth(own_ff, got_ff)
-    held_ff, near_e = meet(held_ff, near_e)
-    near_ff = plane_first(held_ff)
-    got_small = flip(small, "dp", 0)
-    expert_in_sum, expert_out_sum = expert_last(held_e, from_e, near_e)
-    near_ff, got_small, got_one, expert_in_sum = meet(near_ff, got_small, got_one, expert_in_sum)
+    diagonal = plane_second(*near)
+    send_one, keep_one = reduce_last_half(keep_one, got_one)
+    got_one = flip(send_one, "expert", 0)
+    got_small = flip(small, "expert", 1)
+    diagonal, got_one, small, got_small = meet(diagonal, got_one, small, got_small)
     small = small + got_small
-    held_one = reduce_fourth(own_one, got_one)
-    diag_ff = plane_second(*near_ff)
-    got_small = flip(small, "dp", 1)
-    diag_ff, got_small, held_one = meet(diag_ff, got_small, held_one)
+    held_one = add_low(keep_one, got_one)
+    near_one = plane_first(held_one)
+    got_small = flip(small, "expert", 0)
+    (ff_in, ff_out), two = reduce_last(held, near, diagonal, (ff_width, 2 * width))
+    near_one, ff_in, small, got_small, result_own = meet(
+        near_one, ff_in, small, got_small, result_own
+    )
     small = small + got_small
-    for bit in range(2, lax.axis_size("dp").bit_length() - 1):
+    diag_one = plane_second(*near_one)
+    for bit in range(lax.axis_size("dp").bit_length() - 1):
         small = small + flip(small, "dp", bit)
-    near_two, near_one = plane_first(held_two), plane_first(held_one)
-    got_small = flip(small, "expert", 0)
-    ff_in, ff_out = reduce_last(held_ff, near_ff, diag_ff)
-    near_two, near_one, got_small, ff_in = meet(near_two, near_one, got_small, ff_in)
-    small = small + got_small
-    diag_two, diag_one = plane_second(*near_two), plane_second(*near_one)
-    small = small + flip(small, "expert", 1)
-    two = reduce_last(held_two, near_two, diag_two)
-    one = reduce_last(held_one, near_one, diag_one)
+    (one,) = reduce_last(held_one, near_one, diag_one, (2 * width,))
     first_row = mp_index * tok_local
     grad_zero = lax.dynamic_slice_in_dim(grad_zero, first_row, tok_local, 0)
-    result_own = stacked(result_got)
 
     result_got = flip(result_own, "mp", 0)
     spots_here = lax.dynamic_slice_in_dim(back_spots, first_row, tok_local, 0)

time: 471 us -> 420 us (0.89)
  waiting for transfers between devices: 170 us -> 130 us
  local copies, waits for them, and re-layouts: 36.6 us -> 16.8 us
  blocking collectives: 4.86 us -> 19.2 us
  starting transfers between devices: 98.9 us -> 90.4 us
  Pallas kernels: 138 us -> 144 us
    ppermute x30 -> x24, waiting for transfers between devices: 69.6 us -> 49.1 us  [shift(): lax.ppermute(x, axis, [(i, (i + step) % count) for i in range(count)])]
    ppermute x64 -> x58, waiting for transfers between devices: 100 us -> 80.5 us  [flip(): return lax.ppermute(x, axis, [(i, i ^ 1 << bit) for i in range(count)])]
    all_gather x0 -> x6, blocking collectives: none -> 14.5 us  [gathered(): lax.all_gather(part, 'mp', axis=0)]
    ppermute x30 -> x24, starting transfers between devices: 48 us -> 34 us  [shift(): lax.ppermute(x, axis, [(i, (i + step) % count) for i in range(count)])]
    unnamed x226 -> x116, local copies, waits for them, and re-layouts: 20.7 us -> 8.38 us
    ppermute x64 -> x58, starting transfers between devices: 50.9 us -> 56.3 us  [flip(): return lax.ppermute(x, axis, [(i, i ^ 1 << bit) for i in range(count)])]
    pallas_call x28 -> x29, Pallas kernels: 40.8 us -> 41.9 us  [kernel_call(): pl.pallas_call(body, out_shape=[jax.ShapeDtypeStruct(shape, dtype) for sh...]
  transfers between devices with their start and end apart: 94 -> 82, of which waited for: 34 -> 34; matrix products, arithmetic and copies ran while one was open for 4% -> 3% of each run, Pallas kernels for 23% -> 29%
where the time goes in v2:
time: 420 us; the launch traced here: 412 us
  Pallas kernels  144 us (34%)
  waiting for transfers between devices  130 us (31%)
  starting transfers between devices  90.4 us (22%)
  blocking collectives  19.2 us (5%)
  local copies, waits for them, and re-layouts  16.8 us (4%)
  other arithmetic  7.15 us (2%)
    ppermute x58, waiting for transfers between devices, flip(): return lax.ppermute(x, axis, [(i, i ^ 1 << bit) for i in range(count)])  80.5 us
    ppermute x58, starting transfers between devices, flip(): return lax.ppermute(x, axis, [(i, i ^ 1 << bit) for i in range(count)])  56.3 us
    ppermute x24, waiting for transfers between devices, shift(): lax.ppermute(x, axis, [(i, (i + step) % count) for i in range(count)])  49.1 us
    pallas_call x29, Pallas kernels, kernel_call(): pl.pallas_call(body, out_shape=[jax.ShapeDtypeStruct(shape, dtype) for sh...  41.9 us
    ppermute x24, starting transfers between devices, shift(): lax.ppermute(x, axis, [(i, (i + step) % count) for i in range(count)])  34 us
    pallas_call x2, Pallas kernels, attention_forward(): pl.pallas_call(body, out_shape=[pltpu.HBM(shape, dtype) for shape, dtype,...  21.4 us
    pallas_call x2, Pallas kernels, attention_backward(): pl.pallas_call(body, out_shape=[jax.ShapeDtypeStruct((seq_len, 3 * width)...  21.3 us
    pallas_call x1, Pallas kernels, expert_step(): pl.pallas_call(body, out_shape=[pltpu.HBM((total, hidden_width), BF16), p...  15.6 us
  transfers between devices with their start and end apart: 82, of which 34 were waited for; matrix products, arithmetic and copies ran while one was open for 3% of the time, Pallas kernels for 29%

profile of v2, /device:TPU:0, one launch (start us, length us, event | category | flops | bytes accessed | tf_op | source)
XLA Modules:
  0.0 412.4 jit_solution(3516136999652847030)
XLA Ops:
  4.2 5.0 %collective-permute-start.2 = (bf16[2,48,768]{2,1,0:T(8,128)(2,1)}, bf16[2,48,768]{2,1,0:T(8,128)(2,1)S(1)}, u32[]{:S(2)}, u32[]{:S(2)}) collective-permute-start(bf16[2,48,768]{2,1,0:T(8,128)(2,1)} %pad_maximum_fusion.9), channel_id=1, source_target_pairs={{0,6},{2,0},{4,2},{6,4},{1,7},{3,1},{5,3},{7,5},{8,14},{10,8},{12,... | collective-permute-start | bytes 442376 | tf_op jit(solution)/shard_map/ppermute | solution.py:61
  13.8 8.1 %collective-permute-done.1 = bf16[2,48,768]{2,1,0:T(8,128)(2,1)S(1)} collective-permute-done((bf16[2,48,768]{2,1,0:T(8,128)(2,1)}, bf16[2,48,768]{2,1,0:T(8,128)(2,1)S(1)}, u32[]{:S(2)}, u32[]{:S(2)}) %collective-permute-start.1) | collective-permute-done | bytes 147488 | tf_op jit(solution)/shard_map/ppermute | solution.py:61
  30.0 4.7 %shard_map.382.refs_4_ = f32[6,512,512]{2,1,0:T(8,128)S(1)} custom-call(s32[512,512]{1,0:T(8,128)S(1)} %copy-done, f32[6,128]{1,0:T(8,128)S(1)} %pad.7.table_ref, bf16[8,128]{1,0:T(8,128)(2,1)S(1)} %slice_bitcast_fusion.14._), custom_call_target="tpu_custom_call" | custom-call | flops 1 | bytes 1 | tf_op jit(solution)/shard_map/pallas_call | solution.py:324
  39.2 4.7 %shard_map.383.refs_6_ = f32[6,512,512]{2,1,0:T(8,128)S(1)} custom-call(s32[512,512]{1,0:T(8,128)S(1)} %copy-done, f32[6,128]{1,0:T(8,128)S(1)} %pad.8.table_ref, bf16[8,128]{1,0:T(8,128)(2,1)S(1)} %slice_bitcast_fusion.13._), custom_call_target="tpu_custom_call" | custom-call | flops 1 | bytes 1 | tf_op jit(solution)/shard_map/pallas_call | solution.py:324
  46.3 6.4 %collective-permute-done.8 = bf16[2,48,1536]{2,1,0:T(8,128)(2,1)S(1)} collective-permute-done((bf16[2,48,1536]{2,1,0:T(8,128)(2,1)S(1)}, bf16[2,48,1536]{2,1,0:T(8,128)(2,1)S(1)}, u32[]{:S(2)}, u32[]{:S(2)}) %collective-permute-start.8) | collective-permute-done | bytes 294944 | tf_op jit(solution)/shard_map/ppermute | solution.py:61
  57.2 10.6 %shard_map.385 = (f32[512,768]{1,0:T(8,128)}, bf16[512,768]{1,0:T(8,128)(2,1)}, bf16[512,1152]{1,0:T(8,128)(2,1)}, bf16[6,512,512]{2,1,0:T(8,128)(2,1)}, bf16[51...) custom-call(bf16[512,768]{1,0:T(8,128)(2,1)S(1)} %all_gather.42.refs_0_.base_ref.rows_ref, ...), custom_call_target="tpu_custom_call" | custom-call | flops 1 | bytes 1 | tf_op jit(solution)/shard_map/pallas_call | solution.py:421
  67.8 4.7 %collective-permute-done.11.from_y = bf16[2,3,48,1536]{3,2,1,0:T(8,128)(2,1)S(1)} collective-permute-done((bf16[2,3,48,1536]{3,2,1,0:T(8,128)(2,1)S(1)}, bf16[2,3,48,1536]{3,2,1,0:T(8,128)(2,1)S(1)}, u32[]{:S(2)}, u32[]{:S(2)}) %collective-permute-start.11) | collective-permute-done | bytes 884768 | tf_op jit(solution)/shard_map/ppermute | solution.py:47
  75.1 10.5 %collective-permute-done.16.diag_right = bf16[3,48,1536]{2,1,0:T(8,128)(2,1)S(1)} collective-permute-done((bf16[3,48,1536]{2,1,0:T(8,128)(2,1)S(1)}, bf16[3,48,1536]{2,1,0:T(8,128)(2,1)S(1)}, u32[]{:S(2)}, u32[]{:S(2)}) %collective-permute-start.16) | collective-permute-done | bytes 442400 | tf_op jit(solution)/shard_map/ppermute | solution.py:47
  90.3 6.4 %shard_map.387 = (f32[512,768]{1,0:T(8,128)S(1)}, bf16[512,768]{1,0:T(8,128)(2,1)S(1)}, bf16[512,1536]{1,0:T(8,128)(2,1)}, bf16[512,1536]{1,0:T(8,128)(2,1)}, bf16[512,768]{1,0:T(8,128)(2,1)S(1)}) custom-call(bf16[512,768]{1,0:T(8,128)(2,1)S(1)} %all_gather.42.refs_0_.base_ref.rows_ref, bf16[512,768]{1,0:T(8,128)(2,1)S(1)} %get-tuple-element.337.own_ref, ...), custom_call_target="tpu_custom_call" | custom-call | flops 1 | bytes 1 | tf_op jit(solution)/shard_map/pallas_call | solution.py:653
  103.2 3.3 collective-permute-done.21.diag_right
  108.4 10.8 %shard_map.389 = (f32[512,768]{1,0:T(8,128)}, bf16[512,768]{1,0:T(8,128)(2,1)}, bf16[512,1152]{1,0:T(8,128)(2,1)}, bf16[6,512,512]{2,1,0:T(8,128)(2,1)}, bf16[51...) custom-call(f32[512,768]{1,0:T(8,128)S(1)} %get-tuple-element.347.refs_0_.rows_ref, ...), custom_call_target="tpu_custom_call" | custom-call | flops 1 | bytes 1 | tf_op jit(solution)/shard_map/pallas_call | solution.py:421
  131.1 5.9 %collective-permute-done.28.refs_1_ = bf16[128,768]{1,0:T(8,128)(2,1)S(1)} collective-permute-done((bf16[128,768]{1,0:T(8,128)(2,1)S(1)}, bf16[128,768]{1,0:T(8,128)(2,1)S(1)}, u32[]{:S(2)}, u32[]{:S(2)}) %collective-permute-start.28) | collective-permute-done | bytes 196640 | tf_op jit(solution)/shard_map/ppermute | solution.py:61
  137.0 7.6 %collective-permute-done.29.refs_2_ = bf16[128,768]{1,0:T(8,128)(2,1)S(1)} collective-permute-done((bf16[128,768]{1,0:T(8,128)(2,1)S(1)}, bf16[128,768]{1,0:T(8,128)(2,1)S(1)}, u32[]{:S(2)}, u32[]{:S(2)}) %collective-permute-start.29) | collective-permute-done | bytes 196640 | tf_op jit(solution)/shard_map/ppermute | solution.py:61
  147.6 15.6 %shard_map.393 = (bf16[1024,1536]{1,0:T(8,128)(2,1)}, bf16[1024,1536]{1,0:T(8,128)(2,1)}, bf16[1024,768]{1,0:T(8,128)(2,1)S(1)}, f32[512,768]{1,0:T(8,128)S(1)},...) custom-call(s32[2]{0:T(128)S(1)} %pad_add_fusion.where._, ...), custom_call_target="tpu_custom_call" | custom-call | flops 1 | bytes 1 | tf_op jit(solution)/shard_map/pallas_call | solution.py:823
  163.7 9.2 %shard_map.394 = (bf16[2,768,384]{2,1,0:T(8,128)(2,1)S(1)}, bf16[2,384,768]{2,1,0:T(8,128)(2,1)S(1)}, bf16[2,768,384]{2,1,0:T(8,128)(2,1)S(1)}, bf16[2,384,768]{2,1,0:T(8,128)(2,1)S(1)}) custom-call(s32[2]{0:T(128)S(1)} %pad_add_fusion.where._, bf16[512,768]{1,0:T(8,128)(2,1)S(1)} %shard_map.392.own_ref.rows_ref, ...), custom_call_target="tpu_custom_call" | custom-call | flops 1 | bytes 1 | tf_op jit(solution)/shard_map/pallas_call | solution.py:919
  177.8 3.8 collective-permute-start.34
  183.3 3.6 collective-permute-done.34.refs_1_
  186.9 13.2 %collective-permute-done.35.refs_2_ = bf16[128,768]{1,0:T(8,128)(2,1)S(1)} collective-permute-done((bf16[128,768]{1,0:T(8,128)(2,1)S(1)}, bf16[128,768]{1,0:T(8,128)(2,1)S(1)}, u32[]{:S(2)}, u32[]{:S(2)}) %collective-permute-start.35) | collective-permute-done | bytes 196640 | tf_op jit(solution)/shard_map/ppermute | solution.py:61
  208.5 10.6 %shard_map.399 = (bf16[512,1152]{1,0:T(8,128)(2,1)S(1)}, bf16[6,512,512]{2,1,0:T(8,128)(2,1)}, bf16[512,768]{1,0:T(8,128)(2,1)S(1)}) custom-call(bf16[512,768]{1,0:T(8,128)(2,1)S(1)} %get-tuple-element.407.grad_ref.refs_4_, bf16[768,768]{1,0:T(8,128)(2,1)S(1)} %get-tuple-element.357.refs_4_.wa_ref, bf16[768,768]{1,0:T(8,128)(2,1)S(1)} %get-tuple-element.358.refs_5_.wb_ref, ...), custom_call_target="tpu_custom_call" | custom-call | flops 1 | bytes 1 | tf_op jit(solution)/shard_map/pallas_call | solution.py:499
  219.1 2.7 collective-permute-done.40.got_a
  235.8 5.0 %shard_map.402 = (f32[512,768]{1,0:T(8,128)S(1)}, bf16[512,768]{1,0:T(8,128)(2,1)S(1)}, bf16[512,1536]{1,0:T(8,128)(2,1)S(1)}, bf16[512,768]{1,0:T(8,128)(2,1)S(1)}, f32[1,768]{1,0:T(1,128)S(1)}) custom-call(f32[512,768]{1,0:T(8,128)S(1)} %get-tuple-element.423.grad_ref, f32[512,768]{1,0:T(8,128)S(1)} %copy-done.1, ...), custom_call_target="tpu_custom_call" | custom-call | flops 1 | bytes 1 | tf_op jit(solution)/shard_map/pallas_call | solution.py:725
  240.9 3.8 shard_map.403
  244.7 9.3 %collective-permute-done.42.refs_2_ = bf16[1,768,384]{2,1,0:T(8,128)(2,1)S(1)} collective-permute-done((bf16[1,768,384]{2,1,0:T(8,128)(2,1)S(1)}, bf16[1,768,384]{2,1,0:T(8,128)(2,1)S(1)}, u32[]{:S(2)}, u32[]{:S(2)}) %collective-permute-start.42) | collective-permute-done | bytes 589856 | tf_op jit(solution)/shard_map/ppermute | solution.py:47
  266.7 10.7 %shard_map.406 = (bf16[512,1152]{1,0:T(8,128)(2,1)S(1)}, bf16[6,512,512]{2,1,0:T(8,128)(2,1)}, bf16[512,768]{1,0:T(8,128)(2,1)S(1)}) custom-call(bf16[512,768]{1,0:T(8,128)(2,1)S(1)} %get-tuple-element.463.grad_ref.refs_4_, bf16[768,768]{1,0:T(8,128)(2,1)S(1)} %get-tuple-element.326.refs_2_.wa_ref, bf16[768,768]{1,0:T(8,128)(2,1)S(1)} %get-tuple-element.327.refs_3_.wb_ref, ...), custom_call_target="tpu_custom_call" | custom-call | flops 1 | bytes 1 | tf_op jit(solution)/shard_map/pallas_call | solution.py:499
  278.1 2.8 shard_map.407
  297.7 2.7 collective-permute-start.57
  300.4 7.0 %shard_map.411.refs_6_ = f32[6,32]{1,0:T(8,128)S(1)} custom-call(bf16[6,512,512]{2,1,0:T(8,128)(2,1)S(1)} %copy-done.4, s32[512,512]{1,0:T(8,128)S(1)} %copy-done), custom_call_target="tpu_custom_call" | custom-call | flops 1 | bytes 1 | tf_op jit(solution)/shard_map/pallas_call | solution.py:612
  318.9 7.0 %shard_map.413.refs_5_ = f32[6,32]{1,0:T(8,128)S(1)} custom-call(bf16[6,512,512]{2,1,0:T(8,128)(2,1)S(1)} %copy-done.5, s32[512,512]{1,0:T(8,128)S(1)} %copy-done), custom_call_target="tpu_custom_call" | custom-call | flops 1 | bytes 1 | tf_op jit(solution)/shard_map/pallas_call | solution.py:612
  325.9 27.0 %collective-permute-done.58.got_a = bf16[4,2,48,768]{3,2,1,0:T(8,128)(2,1)S(1)} collective-permute-done((bf16[4,2,48,768]{3,2,1,0:T(8,128)(2,1)S(1)}, bf16[4,2,48,768]{3,2,1,0:T(8,128)(2,1)S(1)}, u32[]{:S(2)}, u32[]{:S(2)}) %collective-permute-start.58) | collective-permute-done | bytes 589856 | tf_op jit(solution)/shard_map/ppermute | solution.py:47
  358.6 3.6 collective-permute-start.63
  372.1 5.9 %shard_map.418 = (f32[768,1536]{1,0:T(8,128)}, f32[1536,768]{1,0:T(8,128)}) custom-call(s32[2]{0:T(128)S(1)} %pad_add_fusion.where._, bf16[1,768,384]{2,1,0:T(8,128)(2,1)S(1)} %get-tuple-element.560.refs_0_, bf16[1,384,768]{2,1,0:T(8,128)(2,1)S(1)} %get-tuple-element.562.refs_1_, bf16[1,768,384]{2,1,0:T(8,128)(2,1)S(1)} %collective-permute-done.42.refs_2_, ...), custom_call_target="tpu_custom_call" | custom-call | flops 1 | bytes 1 | tf_op jit(solution)/shard_map/pallas_call | solution.py:69
  378.1 5.7 %collective-permute-done.69.got = bf16[2,2,48,768]{3,2,1,0:T(8,128)(2,1)S(1)} collective-permute-done((bf16[2,2,48,768]{3,2,1,0:T(8,128)(2,1)S(1)}, bf16[2,2,48,768]{3,2,1,0:T(8,128)(2,1)S(1)}, u32[]{:S(2)}, u32[]{:S(2)}) %collective-permute-start.69) | collective-permute-done | bytes 294944 | tf_op jit(solution)/shard_map/ppermute | solution.py:47
  (372 shorter events, 172.3 us)
Async XLA Ops:
  25.1 21.2 %collective-permute-start.9 = (bf16[2,48,1536]{2,1,0:T(8,128)(2,1)S(1)}, bf16[2,48,1536]{2,1,0:T(8,128)(2,1)S(1)}, u32[]{:S(2)}, u32[]{:S(2)}) collective-permute-start(bf16[2,48,1536]{2,1,0:T(8,128)(2,1)S(1)} %pad_maximum_fusion.8), channel_id=1, source_target_pairs={{0,6},{2,0},{4,2},{6,4},{1,7},{3,1},{5,3},{7,5},{8,14},{10,8},{12,... | collective-permute-start | bytes 884744 | tf_op jit(solution)/shard_map/ppermute | solution.py:61
  26.6 26.2 %collective-permute-start.8 = (bf16[2,48,1536]{2,1,0:T(8,128)(2,1)S(1)}, bf16[2,48,1536]{2,1,0:T(8,128)(2,1)S(1)}, u32[]{:S(2)}, u32[]{:S(2)}) collective-permute-start(bf16[2,48,1536]{2,1,0:T(8,128)(2,1)S(1)} %pad_maximum_fusion.8), channel_id=1, source_target_pairs={{0,4},{2,6},{4,0},{6,2},{1,5},{3,7},{5,1},{7,3},{8,12},{10,14},{12... | collective-permute-start | bytes 884744 | tf_op jit(solution)/shard_map/ppermute | solution.py:61
  28.0 24.7 %collective-permute-start.7 = (bf16[2,48,1536]{2,1,0:T(8,128)(2,1)S(1)}, bf16[2,48,1536]{2,1,0:T(8,128)(2,1)S(1)}, u32[]{:S(2)}, u32[]{:S(2)}) collective-permute-start(bf16[2,48,1536]{2,1,0:T(8,128)(2,1)S(1)} %pad_maximum_fusion.8), channel_id=1, source_target_pairs={{0,2},{2,4},{4,6},{6,0},{1,3},{3,5},{5,7},{7,1},{8,10},{10,12},{12... | collective-permute-start | bytes 884744 | tf_op jit(solution)/shard_map/ppermute | solution.py:61
  34.8 17.9 %collective-permute-start.5 = (bf16[3,48,768]{2,1,0:T(8,128)(2,1)S(1)}, bf16[3,48,768]{2,1,0:T(8,128)(2,1)S(1)}, u32[]{:S(2)}, u32[]{:S(2)}) collective-permute-start(bf16[3,48,768]{2,1,0:T(8,128)(2,1)S(1)} %slice_bitcast_fusion.9), channel_id=1, source_target_pairs={{0,16},{8,24},{16,0},{24,8},{1,17},{9,25},{17,1},{25,9},{2,18},{10... | collective-permute-start | bytes 663560 | tf_op jit(solution)/shard_map/ppermute | solution.py:47
  35.4 17.4 %collective-permute-start.6 = (bf16[3,48,768]{2,1,0:T(8,128)(2,1)S(1)}, bf16[3,48,768]{2,1,0:T(8,128)(2,1)S(1)}, u32[]{:S(2)}, u32[]{:S(2)}) collective-permute-start(bf16[3,48,768]{2,1,0:T(8,128)(2,1)S(1)} %slice_bitcast_fusion.8), channel_id=1, source_target_pairs={{0,8},{8,0},{16,24},{24,16},{1,9},{9,1},{17,25},{25,17},{2,10},{10... | collective-permute-start | bytes 663560 | tf_op jit(solution)/shard_map/ppermute | solution.py:47
  52.9 19.6 %collective-permute-start.11 = (bf16[2,3,48,1536]{3,2,1,0:T(8,128)(2,1)S(1)}, bf16[2,3,48,1536]{3,2,1,0:T(8,128)(2,1)S(1)}, u32[]{:S(2)}, u32[]{:S(2)}) collective-permute-start(bf16[2,3,48,1536]{3,2,1,0:T(8,128)(2,1)S(1)} %pad_maximum_fusion.2.own), channel_id=1, source_target_pairs={{0,16},{8,24},{16,0},{24,8},{1,17},{9,25},{17,1},{25,9},{2,18},{10... | collective-permute-start | bytes 2654216 | tf_op jit(solution)/shard_map/ppermute | solution.py:47
  53.4 19.3 %collective-permute-start.10 = (bf16[2,3,48,1536]{3,2,1,0:T(8,128)(2,1)S(1)}, bf16[2,3,48,1536]{3,2,1,0:T(8,128)(2,1)S(1)}, u32[]{:S(2)}, u32[]{:S(2)}) collective-permute-start(bf16[2,3,48,1536]{3,2,1,0:T(8,128)(2,1)S(1)} %pad_maximum_fusion.2.own), channel_id=1, source_target_pairs={{0,8},{8,0},{16,24},{24,16},{1,9},{9,1},{17,25},{25,17},{2,10},{10... | collective-permute-start | bytes 2654216 | tf_op jit(solution)/shard_map/ppermute | solution.py:47
  100.7 18.5 %collective-permute-start.25 = (bf16[128,768]{1,0:T(8,128)(2,1)S(1)}, bf16[128,768]{1,0:T(8,128)(2,1)S(1)}, u32[]{:S(2)}, u32[]{:S(2)}) collective-permute-start(bf16[128,768]{1,0:T(8,128)(2,1)S(1)} %get-tuple-element.613), channel_id=1, source_target_pairs={{0,6},{2,0},{4,2},{6,4},{1,7},{3,1},{5,3},{7,5},{8,14},{10,8},{12,... | collective-permute-start | bytes 589832 | tf_op jit(solution)/shard_map/ppermute | solution.py:61
  100.8 20.0 %collective-permute-start.24 = (bf16[128,768]{1,0:T(8,128)(2,1)S(1)}, bf16[128,768]{1,0:T(8,128)(2,1)S(1)}, u32[]{:S(2)}, u32[]{:S(2)}) collective-permute-start(bf16[128,768]{1,0:T(8,128)(2,1)S(1)} %get-tuple-element.614), channel_id=1, source_target_pairs={{0,4},{2,6},{4,0},{6,2},{1,5},{3,7},{5,1},{7,3},{8,12},{10,14},{12... | collective-permute-start | bytes 589832 | tf_op jit(solution)/shard_map/ppermute | solution.py:61
  127.9 16.7 %collective-permute-start.29 = (bf16[128,768]{1,0:T(8,128)(2,1)S(1)}, bf16[128,768]{1,0:T(8,128)(2,1)S(1)}, u32[]{:S(2)}, u32[]{:S(2)}) collective-permute-start(bf16[128,768]{1,0:T(8,128)(2,1)S(1)} %get-tuple-element.374), channel_id=1, source_target_pairs={{0,4},{2,6},{4,0},{6,2},{1,5},{3,7},{5,1},{7,3},{8,12},{10,14},{12... | collective-permute-start | bytes 589832 | tf_op jit(solution)/shard_map/ppermute | solution.py:61
  129.4 15.2 %collective-permute-start.30 = (bf16[128,768]{1,0:T(8,128)(2,1)S(1)}, bf16[128,768]{1,0:T(8,128)(2,1)S(1)}, u32[]{:S(2)}, u32[]{:S(2)}) collective-permute-start(bf16[128,768]{1,0:T(8,128)(2,1)S(1)} %get-tuple-element.375), channel_id=1, source_target_pairs={{0,6},{2,0},{4,2},{6,4},{1,7},{3,1},{5,3},{7,5},{8,14},{10,8},{12,... | collective-permute-start | bytes 589832 | tf_op jit(solution)/shard_map/ppermute | solution.py:61
  173.0 32.1 %collective-permute-start.38 = (bf16[2,768,384]{2,1,0:T(8,128)(2,1)S(1)}, bf16[2,768,384]{2,1,0:T(8,128)(2,1)S(1)}, u32[]{:S(2)}, u32[]{:S(2)}) collective-permute-start(bf16[2,768,384]{2,1,0:T(8,128)(2,1)S(1)} %get-tuple-element.398), channel_id=1, source_target_pairs={{0,8},{8,0},{16,24},{24,16},{1,9},{9,1},{17,25},{25,17},{2,10},{10... | collective-permute-start | bytes 3538952 | tf_op jit(solution)/shard_map/ppermute | solution.py:47
  173.7 31.5 %collective-permute-start.39 = (bf16[2,384,768]{2,1,0:T(8,128)(2,1)S(1)}, bf16[2,384,768]{2,1,0:T(8,128)(2,1)S(1)}, u32[]{:S(2)}, u32[]{:S(2)}) collective-permute-start(bf16[2,384,768]{2,1,0:T(8,128)(2,1)S(1)} %get-tuple-element.399), channel_id=1, source_target_pairs={{0,16},{8,24},{16,0},{24,8},{1,17},{9,25},{17,1},{25,9},{2,18},{10... | collective-permute-start | bytes 3538952 | tf_op jit(solution)/shard_map/ppermute | solution.py:47
  181.5 18.6 %collective-permute-start.35 = (bf16[128,768]{1,0:T(8,128)(2,1)S(1)}, bf16[128,768]{1,0:T(8,128)(2,1)S(1)}, u32[]{:S(2)}, u32[]{:S(2)}) collective-permute-start(bf16[128,768]{1,0:T(8,128)(2,1)S(1)} %get-tuple-element.395), channel_id=1, source_target_pairs={{0,4},{2,6},{4,0},{6,2},{1,5},{3,7},{5,1},{7,3},{8,12},{10,14},{12... | collective-permute-start | bytes 589832 | tf_op jit(solution)/shard_map/ppermute | solution.py:61
  183.1 17.0 %collective-permute-start.36 = (bf16[128,768]{1,0:T(8,128)(2,1)S(1)}, bf16[128,768]{1,0:T(8,128)(2,1)S(1)}, u32[]{:S(2)}, u32[]{:S(2)}) collective-permute-start(bf16[128,768]{1,0:T(8,128)(2,1)S(1)} %get-tuple-element.396), channel_id=1, source_target_pairs={{0,2},{2,4},{4,6},{6,0},{1,3},{3,5},{5,7},{7,1},{8,10},{10,12},{12... | collective-permute-start | bytes 589832 | tf_op jit(solution)/shard_map/ppermute | solution.py:61
  206.3 15.5 %collective-permute-start.40 = (bf16[1,768,384]{2,1,0:T(8,128)(2,1)S(1)}, bf16[1,768,384]{2,1,0:T(8,128)(2,1)S(1)}, u32[]{:S(2)}, u32[]{:S(2)}) collective-permute-start(bf16[1,768,384]{2,1,0:T(8,128)(2,1)S(1)} %get-tuple-element.412), channel_id=1, source_target_pairs={{0,16},{8,24},{16,0},{24,8},{1,17},{9,25},{17,1},{25,9},{2,18},{10... | collective-permute-start | bytes 1769480 | tf_op jit(solution)/shard_map/ppermute | solution.py:47
  226.5 18.2 %collective-permute-start.44 = (bf16[4,2,48,768]{3,2,1,0:T(8,128)(2,1)S(1)}, bf16[4,2,48,768]{3,2,1,0:T(8,128)(2,1)S(1)}, u32[]{:S(2)}, u32[]{:S(2)}) collective-permute-start(bf16[4,2,48,768]{3,2,1,0:T(8,128)(2,1)S(1)} %get-tuple-element.442), channel_id=1, source_target_pairs={{0,8},{8,0},{16,24},{24,16},{1,9},{9,1},{17,25},{25,17},{2,10},{10... | collective-permute-start | bytes 1769480 | tf_op jit(solution)/shard_map/ppermute | solution.py:47
  227.5 17.2 %collective-permute-start.45 = (bf16[4,2,48,768]{3,2,1,0:T(8,128)(2,1)S(1)}, bf16[4,2,48,768]{3,2,1,0:T(8,128)(2,1)S(1)}, u32[]{:S(2)}, u32[]{:S(2)}) collective-permute-start(bf16[4,2,48,768]{3,2,1,0:T(8,128)(2,1)S(1)} %get-tuple-element.443), channel_id=1, source_target_pairs={{0,16},{8,24},{16,0},{24,8},{1,17},{9,25},{17,1},{25,9},{2,18},{10... | collective-permute-start | bytes 1769480 | tf_op jit(solution)/shard_map/ppermute | solution.py:47
  228.6 25.4 %collective-permute-start.42 = (bf16[1,768,384]{2,1,0:T(8,128)(2,1)S(1)}, bf16[1,768,384]{2,1,0:T(8,128)(2,1)S(1)}, u32[]{:S(2)}, u32[]{:S(2)}) collective-permute-start(bf16[1,768,384]{2,1,0:T(8,128)(2,1)S(1)} %get-tuple-element.560.refs_0_), channel_id=1, source_target_pairs={{0,16},{8,24},{16,0},{24,8},{1,17},{9,25},{17,1},{25,9},{2,18},{10... | collective-permute-start | bytes 1769480 | tf_op jit(solution)/shard_map/ppermute | solution.py:47
  229.5 24.6 %collective-permute-start.43 = (bf16[1,384,768]{2,1,0:T(8,128)(2,1)S(1)}, bf16[1,384,768]{2,1,0:T(8,128)(2,1)S(1)}, u32[]{:S(2)}, u32[]{:S(2)}) collective-permute-start(bf16[1,384,768]{2,1,0:T(8,128)(2,1)S(1)} %get-tuple-element.562.refs_1_), channel_id=1, source_target_pairs={{0,8},{8,0},{16,24},{24,16},{1,9},{9,1},{17,25},{25,17},{2,10},{10... | collective-permute-start | bytes 1769480 | tf_op jit(solution)/shard_map/ppermute | solution.py:47
  254.9 22.5 %collective-permute-start.46 = (bf16[128,768]{1,0:T(8,128)(2,1)S(1)}, bf16[128,768]{1,0:T(8,128)(2,1)S(1)}, u32[]{:S(2)}, u32[]{:S(2)}) collective-permute-start(bf16[128,768]{1,0:T(8,128)(2,1)S(1)} %get-tuple-element.469), channel_id=1, source_target_pairs={{0,6},{2,0},{4,2},{6,4},{1,7},{3,1},{5,3},{7,5},{8,14},{10,8},{12,... | collective-permute-start | bytes 589832 | tf_op jit(solution)/shard_map/ppermute | solution.py:61
  255.0 23.1 %collective-permute-start.47 = (bf16[128,768]{1,0:T(8,128)(2,1)S(1)}, bf16[128,768]{1,0:T(8,128)(2,1)S(1)}, u32[]{:S(2)}, u32[]{:S(2)}) collective-permute-start(bf16[128,768]{1,0:T(8,128)(2,1)S(1)} %get-tuple-element.470), channel_id=1, source_target_pairs={{0,4},{2,6},{4,0},{6,2},{1,5},{3,7},{5,1},{7,3},{8,12},{10,14},{12... | collective-permute-start | bytes 589832 | tf_op jit(solution)/shard_map/ppermute | solution.py:61
  255.8 22.3 %collective-permute-start.48 = (bf16[128,768]{1,0:T(8,128)(2,1)S(1)}, bf16[128,768]{1,0:T(8,128)(2,1)S(1)}, u32[]{:S(2)}, u32[]{:S(2)}) collective-permute-start(bf16[128,768]{1,0:T(8,128)(2,1)S(1)} %get-tuple-element.471), channel_id=1, source_target_pairs={{0,2},{2,4},{4,6},{6,0},{1,3},{3,5},{5,7},{7,1},{8,10},{10,12},{12... | collective-permute-start | bytes 589832 | tf_op jit(solution)/shard_map/ppermute | solution.py:61
  257.7 34.4 %collective-permute-start.51 = (bf16[4,2,48,1536]{3,2,1,0:T(8,128)(2,1)S(1)}, bf16[4,2,48,1536]{3,2,1,0:T(8,128)(2,1)S(1)}, u32[]{:S(2)}, u32[]{:S(2)}) collective-permute-start(bf16[4,2,48,1536]{3,2,1,0:T(8,128)(2,1)S(1)} %get-tuple-element.492), channel_id=1, source_target_pairs={{0,8},{8,0},{16,24},{24,16},{1,9},{9,1},{17,25},{25,17},{2,10},{10... | collective-permute-start | bytes 3538952 | tf_op jit(solution)/shard_map/ppermute | solution.py:47
  258.9 33.2 %collective-permute-start.52 = (bf16[4,2,48,1536]{3,2,1,0:T(8,128)(2,1)S(1)}, bf16[4,2,48,1536]{3,2,1,0:T(8,128)(2,1)S(1)}, u32[]{:S(2)}, u32[]{:S(2)}) collective-permute-start(bf16[4,2,48,1536]{3,2,1,0:T(8,128)(2,1)S(1)} %get-tuple-element.493), channel_id=1, source_target_pairs={{0,16},{8,24},{16,0},{24,8},{1,17},{9,25},{17,1},{25,9},{2,18},{10... | collective-permute-start | bytes 3538952 | tf_op jit(solution)/shard_map/ppermute | solution.py:47
  293.2 15.6 %collective-permute-start.53 = (bf16[4,48,1536]{2,1,0:T(8,128)(2,1)S(1)}, bf16[4,48,1536]{2,1,0:T(8,128)(2,1)S(1)}, u32[]{:S(2)}, u32[]{:S(2)}) collective-permute-start(bf16[4,48,1536]{2,1,0:T(8,128)(2,1)S(1)} %get-tuple-element.506), channel_id=1, source_target_pairs={{0,16},{8,24},{16,0},{24,8},{1,17},{9,25},{17,1},{25,9},{2,18},{10... | collective-permute-start | bytes 1769480 | tf_op jit(solution)/shard_map/ppermute | solution.py:47
  311.5 56.0 %collective-permute-start.65 = (bf16[2,384,768]{2,1,0:T(8,128)(2,1)}, bf16[2,384,768]{2,1,0:T(8,128)(2,1)}, u32[]{:S(2)}, u32[]{:S(2)}) collective-permute-start(bf16[2,384,768]{2,1,0:T(8,128)(2,1)} %pad_maximum_fusion.1), channel_id=1, source_target_pairs={{0,16},{8,24},{16,0},{24,8},{1,17},{9,25},{17,1},{25,9},{2,18},{10... | collective-permute-start | bytes 3538952 | tf_op jit(solution)/shard_map/ppermute | solution.py:47
  313.5 54.0 %collective-permute-start.64 = (bf16[2,768,384]{2,1,0:T(8,128)(2,1)}, bf16[2,768,384]{2,1,0:T(8,128)(2,1)}, u32[]{:S(2)}, u32[]{:S(2)}) collective-permute-start(bf16[2,768,384]{2,1,0:T(8,128)(2,1)} %pad_maximum_fusion), channel_id=1, source_target_pairs={{0,8},{8,0},{16,24},{24,16},{1,9},{9,1},{17,25},{25,17},{2,10},{10... | collective-permute-start | bytes 3538952 | tf_op jit(solution)/shard_map/ppermute | solution.py:47
  314.6 38.3 %collective-permute-start.58 = (bf16[4,2,48,768]{3,2,1,0:T(8,128)(2,1)S(1)}, bf16[4,2,48,768]{3,2,1,0:T(8,128)(2,1)S(1)}, u32[]{:S(2)}, u32[]{:S(2)}) collective-permute-start(bf16[4,2,48,768]{3,2,1,0:T(8,128)(2,1)S(1)} %get-tuple-element.528), channel_id=1, source_target_pairs={{0,8},{8,0},{16,24},{24,16},{1,9},{9,1},{17,25},{25,17},{2,10},{10... | collective-permute-start | bytes 1769480 | tf_op jit(solution)/shard_map/ppermute | solution.py:47
  315.5 37.4 %collective-permute-start.59 = (bf16[4,2,48,768]{3,2,1,0:T(8,128)(2,1)S(1)}, bf16[4,2,48,768]{3,2,1,0:T(8,128)(2,1)S(1)}, u32[]{:S(2)}, u32[]{:S(2)}) collective-permute-start(bf16[4,2,48,768]{3,2,1,0:T(8,128)(2,1)S(1)} %get-tuple-element.529), channel_id=1, source_target_pairs={{0,16},{8,24},{16,0},{24,8},{1,17},{9,25},{17,1},{25,9},{2,18},{10... | collective-permute-start | bytes 1769480 | tf_op jit(solution)/shard_map/ppermute | solution.py:47
  316.7 39.8 %collective-permute-start.60 = (bf16[2,2,48,1536]{3,2,1,0:T(8,128)(2,1)S(1)}, bf16[2,2,48,1536]{3,2,1,0:T(8,128)(2,1)S(1)}, u32[]{:S(2)}, u32[]{:S(2)}) collective-permute-start(bf16[2,2,48,1536]{3,2,1,0:T(8,128)(2,1)S(1)} %get-tuple-element.542), channel_id=1, source_target_pairs={{0,4},{2,6},{4,0},{6,2},{1,5},{3,7},{5,1},{7,3},{8,12},{10,14},{12... | collective-permute-start | bytes 1769480 | tf_op jit(solution)/shard_map/ppermute | solution.py:47
  368.6 15.2 %collective-permute-start.68 = (bf16[2,48,2304]{2,1,0:T(8,128)(2,1)S(1)}, bf16[2,48,2304]{2,1,0:T(8,128)(2,1)S(1)}, u32[]{:S(2)}, u32[]{:S(2)}) collective-permute-start(bf16[2,48,2304]{2,1,0:T(8,128)(2,1)S(1)} %pad_maximum_fusion.5.own), channel_id=1, source_target_pairs={{0,16},{8,24},{16,0},{24,8},{1,17},{9,25},{17,1},{25,9},{2,18},{10... | collective-permute-start | bytes 1327112 | tf_op jit(solution)/shard_map/ppermute | solution.py:47
  (107 other events, 1055.9 us)
